TPU v7x, 32 devices: a whole 2x2x4 slice. The times are simulated.
32 devices in a mesh: dp: 16 (over z, y, core), tensor: 2 (over x).
Axes of the slice: x: 2, y: 2, z: 4, core: 2. Of those that a mesh axis runs over, the one named last changes fastest.
Arguments:
- layer_input: bfloat16 [65536, 512], P(('dp', 'tensor')), may hold values from -6 to 6
- output_grad: bfloat16 [65536, 512], P(('dp', 'tensor')), may hold values from -6 to 6
- qkv_weight: bfloat16 [1536, 512], P('tensor'), may hold values from -0.375 to 0.375
- query_bias: bfloat16 [512], P('tensor'), may hold values from -3 to 3
- value_bias: bfloat16 [512], P('tensor'), may hold values from -3 to 3
- proj_weight: bfloat16 [512, 512], P('tensor'), may hold values from -0.875 to 0.875
- proj_bias: bfloat16 [512], replicated, may hold values from -2 to 2
- first_gain: bfloat16 [512], replicated, may hold values from 0.5 to 1.5
- first_shift: bfloat16 [512], replicated, may hold values from -2 to 2
- up_weight: bfloat16 [512, 2048], P(None, 'tensor'), may hold values from -0.25 to 0.25
- up_bias: bfloat16 [2048], P('tensor'), may hold values from -3 to 3
- down_weight: bfloat16 [2048, 512], P('tensor'), may hold values from -0.125 to 0.125
- down_bias: bfloat16 [512], replicated, may hold values from -2 to 2
- second_gain: bfloat16 [512], replicated, may hold values from 0.5 to 1.5
- second_shift: bfloat16 [512], replicated, may hold values from -2 to 2
Outputs:
- layer_output: bfloat16 [65536, 512], P(('dp', 'tensor'))
- input_grad: bfloat16 [65536, 512], P(('dp', 'tensor'))
- qkv_weight_grad: float32 [1536, 512], P('tensor')
- query_bias_grad: float32 [512], P('tensor')
- value_bias_grad: float32 [512], P('tensor')
- proj_weight_grad: float32 [512, 512], P('tensor')
- proj_bias_grad: float32 [512], replicated
- first_gain_grad: float32 [512], replicated
- first_shift_grad: float32 [512], replicated
- up_weight_grad: float32 [512, 2048], P(None, 'tensor')
- up_bias_grad: float32 [2048], P('tensor')
- down_weight_grad: float32 [2048, 512], P('tensor')
- down_bias_grad: float32 [512], replicated
- second_gain_grad: float32 [512], replicated
- second_shift_grad: float32 [512], replicated
All inputs are finite; a program needn't handle non-finite values.
Results may differ from a plain program's by a relative error of at most 0.022.
The roundings to bfloat16 on the way count: a program that leaves them out, or rounds other values in their place, can miss the bound.
Values may be sent and summed in bfloat16 or wider, within the bound.
No kernel may reach another device: no remote copies, remote signals or barrier semaphores. Data moves between devices by JAX's collectives and lax.ppermute only.
A program may use at most 256 MiB of HBM per device.

v0:
```python
from functools import partial

import jax
import jax.numpy as jnp
from jax import lax
from jax.experimental import pallas as pl
from jax.experimental.pallas import tpu as pltpu
from jax.sharding import PartitionSpec as P

HEAD_DIM = 64
SEQ_LEN = 1024
PART_ROWS = 3 * HEAD_DIM

norm_eps = 1e-05
f32 = jnp.float32
bf16 = jnp.bfloat16


def matmul_rows(left, right):
    return lax.dot_general(
        left, right, (((0,), (0,)), ((), ())), preferred_element_type=jnp.float32
    )


def matmul_back(left, right):
    return lax.dot_general(
        left, right, (((1,), (1,)), ((), ())), preferred_element_type=jnp.float32
    )


def attend_forward(queries, key_rows, value_rows):
    seq_heads = key_rows.shape[0] * key_rows.shape[1]
    head_dim = queries.shape[-1]
    score_scale = head_dim ** (-0.5)
    block_rows = min(512, SEQ_LEN)
    block_count = SEQ_LEN // block_rows
    item_count = seq_heads * block_count
    query_items = queries.reshape(item_count, block_rows, head_dim)
    key_all = key_rows.reshape(seq_heads, SEQ_LEN, head_dim)
    value_all = value_rows.reshape(seq_heads, SEQ_LEN, head_dim)

    def one_block(block_item):
        query_blk, position = block_item
        owner_index = position // block_count
        keys_here = key_all[owner_index]
        values_here = value_all[owner_index]
        scores = matmul_back(query_blk, keys_here) * score_scale
        row_top = jnp.max(scores, axis=-1, keepdims=True)
        exponent = jnp.exp(scores - row_top)
        row_total = jnp.sum(exponent, axis=-1, keepdims=True)
        weights_now = exponent / row_total
        mixed_rows = jnp.dot(
            weights_now.astype(jnp.bfloat16), values_here, preferred_element_type=jnp.float32
        )
        return (mixed_rows, row_top[:, 0] + jnp.log(row_total[:, 0]))

    mixed_rows, log_total = lax.map(
        one_block, (query_items, jnp.arange(item_count, dtype=jnp.int32))
    )
    return (mixed_rows.reshape(queries.shape), log_total.reshape(queries.shape[:-1]))


def attend_backward(queries, key_rows, value_rows, log_total, context_low):
    seq_heads = key_rows.shape[0] * key_rows.shape[1]
    head_dim = queries.shape[-1]
    score_scale = head_dim ** (-0.5)
    block_rows = min(512, SEQ_LEN)
    block_count = SEQ_LEN // block_rows
    item_count = seq_heads * block_count
    query_items = queries.reshape(item_count, block_rows, head_dim)
    total_items = log_total.reshape(item_count, block_rows)
    grad_items = context_low.reshape(item_count, block_rows, head_dim)
    key_all = key_rows.reshape(seq_heads, SEQ_LEN, head_dim)
    value_all = value_rows.reshape(seq_heads, SEQ_LEN, head_dim)

    def one_block(block_item):
        query_blk, total_blk, grad_blk, position = block_item
        owner_index = position // block_count
        keys_here = key_all[owner_index]
        values_here = value_all[owner_index]
        scores = matmul_back(query_blk, keys_here) * score_scale
        weights_now = jnp.exp(scores - total_blk[:, None])
        grad_weights = matmul_back(grad_blk, values_here)
        grad_scores = weights_now * (
            grad_weights - jnp.sum(weights_now * grad_weights, axis=-1, keepdims=True)
        )
        score_low = grad_scores.astype(jnp.bfloat16)
        grad_query = jnp.dot(score_low, keys_here, preferred_element_type=jnp.float32) * score_scale
        grad_key = matmul_rows(score_low, query_blk) * score_scale
        grad_value = matmul_rows(weights_now.astype(jnp.bfloat16), grad_blk)
        return (grad_query, grad_key, grad_value)

    grad_query, grad_key, grad_value = lax.map(
        one_block, (query_items, total_items, grad_items, jnp.arange(item_count, dtype=jnp.int32))
    )
    grad_key = jnp.sum(grad_key.reshape(seq_heads, block_count, SEQ_LEN, head_dim), axis=1)
    grad_value = jnp.sum(grad_value.reshape(seq_heads, block_count, SEQ_LEN, head_dim), axis=1)
    return (
        grad_query.reshape(queries.shape),
        grad_key.reshape(key_rows.shape),
        grad_value.reshape(value_rows.shape),
    )


def norm_forward(hidden, gain_vec, shift_vec):
    center = jnp.mean(hidden, axis=-1)
    second = jnp.mean(hidden * hidden, axis=-1) - center * center
    inv_std = lax.rsqrt(second + norm_eps)
    normal = (hidden - center[:, None]) * inv_std[:, None]
    return (normal * gain_vec + shift_vec, normal, inv_std)


def norm_backward(upstream, normal, inv_std, gain_vec):
    scaled = upstream * gain_vec
    first_mean = jnp.mean(scaled, axis=-1)
    second_mean = jnp.mean(scaled * normal, axis=-1)
    grad_in = inv_std[:, None] * (scaled - first_mean[:, None] - normal * second_mean[:, None])
    return (grad_in, jnp.sum(upstream * normal, axis=0), jnp.sum(upstream, axis=0))


def rows_in(value):
    return lax.all_gather(value, "tensor", axis=0, tiled=True)


def part_out(value):
    return lax.psum_scatter(value, "tensor", scatter_dimension=0, tiled=True)


def gather_grad(value):
    return lax.all_gather(value, "tensor", axis=0, tiled=True)


def part_back(value):
    return lax.psum_scatter(value, "tensor", scatter_dimension=0, tiled=True)


def token_body(
    layer_input,
    output_grad,
    qkv_weight,
    query_bias,
    value_bias,
    proj_weight,
    proj_bias,
    first_gain,
    first_shift,
    up_weight,
    up_bias,
    down_weight,
    down_bias,
    second_gain,
    second_shift,
):
    heads_here = query_bias.shape[0] // HEAD_DIM
    query_bf = query_bias.astype(jnp.float32).reshape(heads_here, HEAD_DIM)
    value_bf = value_bias.astype(jnp.float32).reshape(heads_here, HEAD_DIM)
    bias_rows = jnp.stack([query_bf, jnp.zeros_like(query_bf), value_bf], axis=1)
    gain_one = first_gain.astype(jnp.float32)
    shift_one = first_shift.astype(jnp.float32)
    gain_two = second_gain.astype(jnp.float32)
    shift_two = second_shift.astype(jnp.float32)
    input_full = rows_in(layer_input)
    row_count = input_full.shape[0]
    seq_count = row_count // SEQ_LEN
    projected = matmul_back(input_full, qkv_weight).reshape(row_count, heads_here, 3, HEAD_DIM)
    packed = (projected + bias_rows).astype(jnp.bfloat16)
    parts = packed.reshape(seq_count, SEQ_LEN, heads_here, 3, HEAD_DIM).transpose(3, 0, 2, 1, 4)
    queries, key_rows, value_rows = (parts[0], parts[1], parts[2])
    mixed_rows, log_total = attend_forward(queries, key_rows, value_rows)
    context = (
        mixed_rows.transpose(0, 2, 1, 3)
        .reshape(row_count, heads_here * HEAD_DIM)
        .astype(jnp.bfloat16)
    )
    partial_branch = jnp.dot(context, proj_weight, preferred_element_type=jnp.float32)
    branch = part_out(partial_branch) + proj_bias.astype(jnp.float32)
    normed_one, normal_one, inv_one = norm_forward(
        layer_input.astype(jnp.float32) + branch, gain_one, shift_one
    )
    normed_full = rows_in(normed_one.astype(jnp.bfloat16))
    inner_pre = jnp.dot(
        normed_full, up_weight, preferred_element_type=jnp.float32
    ) + up_bias.astype(jnp.float32)
    active, gelu_back = jax.vjp(partial(jax.nn.gelu, approximate=False), inner_pre)
    active_low = active.astype(jnp.bfloat16)
    second = part_out(
        jnp.dot(active_low, down_weight, preferred_element_type=jnp.float32)
    ) + down_bias.astype(jnp.float32)
    result_rows, normal_two, inv_two = norm_forward(normed_one + second, gain_two, shift_two)
    upstream = output_grad.astype(jnp.float32)
    grad_two, gain_two_grad, shift_two_grad = norm_backward(upstream, normal_two, inv_two, gain_two)
    second_low = grad_two.astype(jnp.bfloat16)
    down_b_grad = jnp.sum(second_low.astype(jnp.float32), axis=0)
    second_full = gather_grad(second_low)
    down_w_grad = matmul_rows(active_low, second_full)
    grad_active = matmul_back(second_full, down_weight)
    inner_low = gelu_back(grad_active)[0].astype(jnp.bfloat16)
    up_b_grad = jnp.sum(inner_low.astype(jnp.float32), axis=0)
    up_w_grad = matmul_rows(normed_full, inner_low)
    grad_mid = grad_two + part_back(matmul_back(inner_low, up_weight))
    grad_one, gain_one_grad, shift_one_grad = norm_backward(grad_mid, normal_one, inv_one, gain_one)
    branch_low = grad_one.astype(jnp.bfloat16)
    proj_b_grad = jnp.sum(branch_low.astype(jnp.float32), axis=0)
    branch_full = gather_grad(branch_low)
    proj_w_grad = matmul_rows(context, branch_full)
    context_low = matmul_back(branch_full, proj_weight).astype(jnp.bfloat16)
    context_low = context_low.reshape(seq_count, SEQ_LEN, heads_here, HEAD_DIM).transpose(
        0, 2, 1, 3
    )
    grad_query, grad_key, grad_value = attend_backward(
        queries, key_rows, value_rows, log_total, context_low
    )
    packed_low = jnp.stack([grad_query, grad_key, grad_value], axis=0).transpose(1, 3, 2, 0, 4)
    packed_low = packed_low.reshape(row_count, heads_here * 3 * HEAD_DIM).astype(jnp.bfloat16)
    packed_sums = jnp.sum(packed_low.astype(jnp.float32), axis=0).reshape(heads_here, 3, HEAD_DIM)
    query_b_grad = packed_sums[:, 0].reshape(heads_here * HEAD_DIM)
    value_b_grad = packed_sums[:, 2].reshape(heads_here * HEAD_DIM)
    qkv_w_grad = matmul_rows(packed_low, input_full)
    input_grad = (
        grad_one + part_back(jnp.dot(packed_low, qkv_weight, preferred_element_type=jnp.float32))
    ).astype(jnp.bfloat16)
    totals = (
        lax.psum(qkv_w_grad.astype(jnp.bfloat16), "dp").astype(jnp.float32),
        lax.psum(query_b_grad.astype(jnp.bfloat16), "dp").astype(jnp.float32),
        lax.psum(value_b_grad.astype(jnp.bfloat16), "dp").astype(jnp.float32),
        lax.psum(proj_w_grad.astype(jnp.bfloat16), "dp").astype(jnp.float32),
        lax.psum(up_w_grad.astype(jnp.bfloat16), "dp").astype(jnp.float32),
        lax.psum(up_b_grad.astype(jnp.bfloat16), "dp").astype(jnp.float32),
        lax.psum(down_w_grad.astype(jnp.bfloat16), "dp").astype(jnp.float32),
    )
    vectors = lax.psum(
        (proj_b_grad, gain_one_grad, shift_one_grad, down_b_grad, gain_two_grad, shift_two_grad),
        ("dp", "tensor"),
    )
    return (
        result_rows.astype(jnp.bfloat16),
        input_grad,
        totals[0],
        totals[1],
        totals[2],
        totals[3],
        vectors[0],
        vectors[1],
        vectors[2],
        totals[4],
        totals[5],
        totals[6],
        vectors[3],
        vectors[4],
        vectors[5],
    )


VMEM_LIMIT = 66_000_000
EXTRA = 16


def mm(left, right):
    return lax.dot_general(left, right, (((1,), (0,)), ((), ())), preferred_element_type=f32)


def mm_nt(left, right):
    return lax.dot_general(left, right, (((1,), (1,)), ((), ())), preferred_element_type=f32)


def mm_tn(left, right):
    return lax.dot_general(left, right, (((0,), (0,)), ((), ())), preferred_element_type=f32)


def kernel_params(limit=VMEM_LIMIT):
    return pltpu.CompilerParams(vmem_limit_bytes=limit)


def cost(flops, size):
    return pl.CostEstimate(flops=int(flops), bytes_accessed=int(size), transcendentals=0)


def in_vmem():
    return pl.BlockSpec(memory_space=pltpu.VMEM)


def aligned(start, size, by):
    return pl.ds(pl.multiple_of(start * size, by), size)


def pack_qkv_kernel(pos_ref, weight_ref, query_b_ref, value_b_ref, packed_ref, own_b_ref):
    half = weight_ref.shape[0]
    wide = query_b_ref.shape[0] // 2
    query_b, value_b = (ref[...].reshape(1, 2 * wide) for ref in (query_b_ref, value_b_ref))
    packed_ref[:half] = weight_ref[...]
    packed_ref[half:] = jnp.zeros_like(packed_ref[half:])
    own_b_ref[...] = jnp.zeros_like(own_b_ref)
    parity = lax.rem(pos_ref[0], 2)
    for k in range(2):
        cols = slice(k * wide, (k + 1) * wide)
        own_b_ref[k * EXTRA : k * EXTRA + 1, :wide] = query_b[:, cols]
        own_b_ref[k * EXTRA : k * EXTRA + 1, wide : 2 * wide] = value_b[:, cols]

        @pl.when(parity == k)
        def _():
            packed_ref[half : half + 1, :wide] = query_b[:, cols]
            packed_ref[half : half + 1, wide : 2 * wide] = value_b[:, cols]


def pack_qkv(pos, weight, query_b, value_b):
    rows, width = weight.shape
    half = rows // 2
    small = pl.BlockSpec(query_b.shape, lambda i, pos: (0,))
    return pl.pallas_call(
        pack_qkv_kernel,
        grid_spec=pltpu.PrefetchScalarGridSpec(
            num_scalar_prefetch=1,
            grid=(1,),
            in_specs=[pl.BlockSpec((half, width), lambda i, pos: (lax.rem(pos[0], 2), 0)), small, small],
            out_specs=[
                pl.BlockSpec((half + EXTRA, width), lambda i, pos: (0, 0)),
                pl.BlockSpec((2 * EXTRA, width), lambda i, pos: (0, 0)),
            ],
        ),
        out_shape=[
            jax.ShapeDtypeStruct((half + EXTRA, width), bf16),
            jax.ShapeDtypeStruct((2 * EXTRA, width), bf16),
        ],
        compiler_params=kernel_params(),
        cost_estimate=cost(0, 1 << 20),
        name="pack_qkv",
    )(pos, weight, query_b, value_b)


def pack_mlp_kernel(pos_ref, proj_ref, down_ref, up_ref, up_b_ref, *refs):
    vec_refs, packed_ref, vecs_ref = refs[:-2], refs[-2], refs[-1]
    width = proj_ref.shape[1]
    at = 0
    for value in (proj_ref[...], down_ref[...]):
        packed_ref[at : at + value.shape[0]] = value
        at += value.shape[0]
    blocks = up_ref.shape[1] // width
    for j in range(blocks):
        packed_ref[at : at + up_ref.shape[0]] = up_ref[:, j * width : (j + 1) * width]
        at += up_ref.shape[0]
    packed_ref[at:] = jnp.zeros_like(packed_ref[at:])
    vecs_ref[...] = jnp.zeros_like(vecs_ref)
    for j in range(blocks):
        row = up_b_ref[j * width : (j + 1) * width].reshape(1, width)
        packed_ref[at + j : at + j + 1] = row
        vecs_ref[8 + j : 9 + j] = row.astype(f32)
    for k, ref in enumerate(vec_refs):
        vecs_ref[k : k + 1] = ref[...].reshape(1, width).astype(f32)


def pack_mlp(pos, proj, down, up, up_b, vectors):
    width, hidden = up.shape
    rows = (proj.shape[0] + 2 * hidden) // 2 + EXTRA

    def half(array):
        return pl.BlockSpec((array.shape[0] // 2, array.shape[1]), lambda i, pos: (lax.rem(pos[0], 2), 0))

    def whole(array):
        return pl.BlockSpec(array.shape, lambda i, pos: (0,))

    return pl.pallas_call(
        pack_mlp_kernel,
        grid_spec=pltpu.PrefetchScalarGridSpec(
            num_scalar_prefetch=1,
            grid=(1,),
            in_specs=[half(proj), half(down), half(up), whole(up_b)] + [whole(v) for v in vectors],
            out_specs=[
                pl.BlockSpec((rows, width), lambda i, pos: (0, 0)),
                pl.BlockSpec((EXTRA, width), lambda i, pos: (0, 0)),
            ],
        ),
        out_shape=[jax.ShapeDtypeStruct((rows, width), bf16), jax.ShapeDtypeStruct((EXTRA, width), f32)],
        compiler_params=kernel_params(),
        cost_estimate=cost(0, 3 << 20),
        name="pack_mlp",
    )(pos, proj, down, up, up_b, *vectors)


def attn_fwd_kernel(pos_ref, x_ref, *refs, heads, q_block, fetched):
    packed_ref, probs_ref, ctx_ref, key_ref, score_a, score_b = refs[-6:]
    seq = x_ref.shape[0]
    scale = HEAD_DIM**-0.5
    wide = heads * HEAD_DIM
    part = heads * PART_ROWS
    if fetched:
        near = pl.program_id(1) == 0
        weight = jnp.where(near, refs[0][:part], refs[1][:part])
        bias = jnp.where(near, refs[0][part:].astype(f32), refs[1][part:].astype(f32))
    else:
        weight, bias = refs[0][...], refs[1][...].astype(f32)
    column = bias[:8, : 2 * wide].T
    raw = mm_nt(weight, x_ref[...])
    for h in range(heads):
        base = h * PART_ROWS
        ends = (base + HEAD_DIM, base + 2 * HEAD_DIM, base + PART_ROWS)
        query = raw[base : ends[0]] + column[h * HEAD_DIM : (h + 1) * HEAD_DIM, :1]
        value = raw[ends[1] : ends[2]] + column[wide + h * HEAD_DIM : wide + (h + 1) * HEAD_DIM, :1]
        packed_ref[0, 0, base : ends[0]] = query.astype(bf16)
        packed_ref[0, 0, ends[0] : ends[1]] = raw[ends[0] : ends[1]].astype(bf16)
        packed_ref[0, 0, ends[1] : ends[2]] = value.astype(bf16)
        keys = packed_ref[0, 0, ends[0] : ends[1], :].astype(f32)
        key_ref[h] = (keys.T * scale).astype(bf16)
    tiles = [(h, c) for h in range(heads) for c in range(0, seq, q_block)]
    scores = (score_a, score_b)

    def score(tile, ref):
        h, c = tile
        base = h * PART_ROWS
        ref[...] = mm(key_ref[h], packed_ref[0, 0, base : base + HEAD_DIM, c : c + q_block])

    def finish(tile, ref):
        h, c = tile
        base = h * PART_ROWS
        top = jnp.max(ref[...], axis=0, keepdims=True)
        exponent = jnp.exp(ref[...] - top)
        total = jnp.sum(exponent, axis=0, keepdims=True)
        probs = (exponent * (1.0 / total)).astype(bf16)
        probs_ref[0, 0, h, :, c : c + q_block] = probs
        mixed = mm(packed_ref[0, 0, base + 2 * HEAD_DIM : base + 3 * HEAD_DIM, :], probs)
        ctx_ref[0, 0, h * HEAD_DIM : (h + 1) * HEAD_DIM, c : c + q_block] = mixed.astype(bf16)

    score(tiles[0], scores[0])
    for j, tile in enumerate(tiles):
        if j + 1 < len(tiles):
            score(tiles[j + 1], scores[(j + 1) % 2])
        finish(tile, scores[j % 2])


def attn_fwd(pos, x, sources, shard, fetched, shapes, earlier):
    rows, width = x.shape
    n_seq = rows // SEQ_LEN
    heads = shapes[1].shape[2] // 2
    part = heads * PART_ROWS

    def at(k, pos):
        return lax.bitwise_xor(k, lax.rem(pos[0], 2)) if fetched else k

    if fetched:
        sizes = [pl.BlockSpec(v.shape, lambda s, k, pos: (0, 0), pipeline_mode=pl.Buffered(1)) for v in sources]
    else:
        sizes = [pl.BlockSpec((size, width), lambda s, k, pos: (k, 0)) for size in (part, EXTRA)]
    out_specs = [
        pl.BlockSpec((1, 1, part, SEQ_LEN), lambda s, k, pos: (shard, s, at(k, pos), 0)),
        pl.BlockSpec((1, 1, heads, SEQ_LEN, SEQ_LEN), lambda s, k, pos: (shard, s, at(k, pos), 0, 0)),
        pl.BlockSpec((1, 1, heads * HEAD_DIM, SEQ_LEN), lambda s, k, pos: (shard, s, at(k, pos), 0)),
    ]
    q_block = 512
    share = 2 * n_seq * heads
    flops = share * (2 * SEQ_LEN * width * PART_ROWS + 4 * SEQ_LEN * SEQ_LEN * HEAD_DIM * 6)
    return pl.pallas_call(
        partial(attn_fwd_kernel, heads=heads, q_block=q_block, fetched=fetched),
        grid_spec=pltpu.PrefetchScalarGridSpec(
            num_scalar_prefetch=1,
            grid=(n_seq, 2),
            in_specs=[pl.BlockSpec((SEQ_LEN, width), lambda s, k, pos: (s, 0))]
            + sizes
            + [pl.BlockSpec(memory_space=pl.ANY)] * len(earlier),
            out_specs=out_specs,
            scratch_shapes=[
                pltpu.VMEM((heads, SEQ_LEN, HEAD_DIM), bf16),
                pltpu.VMEM((SEQ_LEN, q_block), f32),
                pltpu.VMEM((SEQ_LEN, q_block), f32),
            ],
        ),
        out_shape=shapes,
        input_output_aliases={4: 0, 5: 1, 6: 2} if earlier else {},
        compiler_params=kernel_params(),
        cost_estimate=cost(flops // 8 if fetched else flops, share * 3 << 20),
        name="attn_fwd",
    )(pos, x, *sources, *earlier)


def piece_bits(*order):
    bits = [0]
    for bit in reversed(order):
        bits = bits + [b | bit for b in bits]
    return bits


MLP_SLOTS = 8
DOWN_ORDER = ("tensor", 2, 4)
UP_ORDER = (4, "tensor", 2)
DOWN_BITS = piece_bits(1, 2, 4)
UP_BITS = piece_bits(1, 4, 2)


def middle_kernel(
    pos_ref,
    x_ref,
    og_ref,
    ctx_ref,
    vecs_ref,
    proj_own,
    up_own,
    down_own,
    *refs,
    n_others,
    chunk,
):
    fetched, refs = refs[: 2 * n_others], refs[2 * n_others :]
    out_ref, grad_one_ref, ctx_low_ref, dn_keep_ref, dn_send_ref, up_keep_ref, up_send_ref, *refs = refs
    proj_got, up_got, down_got, up_b_ref, act_ref, slope_ref, proj_acc, up_acc, dn_acc, vec_acc, up_b_acc = refs
    step = pl.program_id(0)
    n_shards = n_others + 1
    ctx_rows, width = proj_own.shape
    hidden = up_own.shape[1]
    blocks = hidden // width
    inv_width = 1.0 / width

    def mean(v):
        return jnp.sum(v, axis=1, keepdims=True) * inv_width

    @pl.when(step == 0)
    def _():
        for ref in (proj_acc, up_acc, dn_acc):
            size = min(64, ref.shape[1])

            def clear(i, carry, ref=ref, size=size):
                for t in range(n_shards):
                    ref[t, aligned(i, size, size), :] = jnp.zeros((size, ref.shape[2]), f32)
                return carry

            lax.fori_loop(0, ref.shape[1] // size, clear, 0)
        for ref in (vec_acc, up_b_acc):
            ref[...] = jnp.zeros_like(ref)
        parity = lax.rem(pos_ref[0], 2)
        for j in range(blocks):
            up_b_ref[:, j * width : (j + 1) * width] = vecs_ref[8 + j : 9 + j, :]
        for t in range(n_others):
            for k in range(2):
                ref = fetched[2 * t + k]
                side = parity if k == 0 else 1 - parity
                rows = ctx_rows // 2
                proj_got[t, aligned(side, rows, rows), :] = ref[:rows]
                at = rows
                rows = hidden // 2
                down_got[t, aligned(side, rows, rows), :] = ref[at : at + rows]
                at += rows
                rows = width // 2
                for j in range(blocks):
                    up_got[t, aligned(side, rows, rows), j * width : (j + 1) * width] = ref[at : at + rows]
                    at += rows
                if k == 0:
                    for j in range(blocks):
                        to = (t + 1) * hidden + j * width
                        up_b_ref[:, to : to + width] = ref[at : at + EXTRA].astype(f32)[j : j + 1]

    def proj(t):
        return proj_own[...] if t == 0 else proj_got[t - 1]

    def up(t, c):
        return up_own[:, c : c + chunk] if t == 0 else up_got[t - 1, :, c : c + chunk]

    def down(t, c):
        return down_own[c : c + chunk, :] if t == 0 else down_got[t - 1, c : c + chunk, :]

    proj_b, gain_one, shift_one, down_b, gain_two, shift_two = (vecs_ref[k : k + 1, :] for k in range(6))
    branch = proj_b
    for t in range(n_shards):
        branch = branch + mm_tn(ctx_ref[t, 0], proj(t))
    mid_sum = x_ref[...].astype(f32) + branch
    center = mean(mid_sum)
    inv_one = lax.rsqrt(mean(mid_sum * mid_sum) - center * center + norm_eps)
    normal_one = (mid_sum - center) * inv_one
    normed_one = normal_one * gain_one + shift_one
    normed_low = normed_one.astype(bf16)
    second = down_b
    chunks = [(t, c) for t in range(n_shards) for c in range(0, hidden, chunk)]
    for t, c in chunks:
        at = t * hidden + c
        inner = mm(normed_low, up(t, c)) + up_b_ref[:, at : at + chunk]
        phi = 0.5 * lax.erf(inner * 0.7071067811865476) + 0.5
        active = (inner * phi).astype(bf16)
        act_ref[:, at : at + chunk] = active
        slope_ref[:, at : at + chunk] = phi + inner * (0.3989422804014327 * jnp.exp(-0.5 * inner * inner))
        second = second + mm(active, down(t, c))
    last_sum = normed_one + second
    center_two = mean(last_sum)
    inv_two = lax.rsqrt(mean(last_sum * last_sum) - center_two * center_two + norm_eps)
    normal_two = (last_sum - center_two) * inv_two
    out_ref[...] = (normal_two * gain_two + shift_two).astype(bf16)
    upstream = og_ref[...].astype(f32)
    scaled = upstream * gain_two
    grad_two = inv_two * (scaled - mean(scaled) - normal_two * mean(scaled * normal_two))
    second_low = grad_two.astype(bf16)
    normed_t = normed_low.T
    back = None
    for t, c in chunks:
        at = t * hidden + c
        grad_active = mm_nt(second_low, down(t, c))
        inner_low = (grad_active * slope_ref[:, at : at + chunk]).astype(bf16)
        up_b_acc[:, at : at + chunk] += jnp.sum(inner_low.astype(f32), axis=0, keepdims=True)
        part = mm_nt(inner_low, up(t, c))
        back = part if back is None else back + part
        up_acc[t, :, c : c + chunk] += mm(normed_t, inner_low)
        dn_acc[t, c : c + chunk, :] += mm_tn(act_ref[:, at : at + chunk], second_low)
    grad_mid = grad_two + back
    scaled_one = grad_mid * gain_one
    grad_one = inv_one * (scaled_one - mean(scaled_one) - normal_one * mean(scaled_one * normal_one))
    grad_one_ref[...] = grad_one
    branch_low = grad_one.astype(bf16)
    sums = (
        branch_low.astype(f32),
        grad_mid * normal_one,
        grad_mid,
        second_low.astype(f32),
        upstream * normal_two,
        upstream,
    )
    for k, value in enumerate(sums):
        vec_acc[k : k + 1, :] += jnp.sum(value, axis=0, keepdims=True)
    for t in range(n_shards):
        ctx_low_ref[t, 0] = mm_nt(proj(t), branch_low).astype(bf16)
        proj_acc[t] += mm(ctx_ref[t, 0], branch_low)

    @pl.when(step == pl.num_programs(0) - 1)
    def _():
        low = lax.rem(pos_ref[0], MLP_SLOTS)
        dn_rows, up_rows, proj_rows = hidden // MLP_SLOTS, width // MLP_SLOTS, ctx_rows // MLP_SLOTS
        half = MLP_SLOTS // 2
        for slot in range(MLP_SLOTS):
            dn_ref = dn_keep_ref if slot < half else dn_send_ref
            upk_ref = up_keep_ref if slot < half else up_send_ref
            k = slot % half
            dn_at = lax.bitwise_xor(low, DOWN_BITS[slot])
            rows = aligned(lax.bitwise_xor(low, UP_BITS[slot]), up_rows, up_rows)
            for t in range(n_shards):
                dn_ref[t, k, :dn_rows] = dn_acc[t, aligned(dn_at, dn_rows, dn_rows), :].astype(bf16)
                dn_ref[t, k, dn_rows:] = proj_acc[t, aligned(dn_at, proj_rows, proj_rows), :].astype(bf16)
                for j in range(blocks):
                    to = j * up_rows
                    upk_ref[t, k, to : to + up_rows] = up_acc[t, rows, j * width : (j + 1) * width].astype(bf16)
                to = blocks * up_rows
                upk_ref[t, k, to : to + 8] = vec_acc[...].astype(bf16)
                tail = [
                    up_b_acc[:, t * hidden + j * width : t * hidden + (j + 1) * width] for j in range(blocks)
                ]
                tail.append(jnp.zeros((8 - blocks, width), f32))
                upk_ref[t, k, to + 8 : to + EXTRA] = jnp.concatenate(tail, axis=0).astype(bf16)


def middle(pos, x, out_grad, ctx, vecs, proj, up, down, fetched):
    rows, width = x.shape
    n_shards, n_seq, ctx_rows, _ = ctx.shape
    hidden = up.shape[1]
    n_others = n_shards - 1
    block = 512
    per_seq = SEQ_LEN // block
    half = MLP_SLOTS // 2
    dn_rows, up_rows = (hidden + ctx_rows) // MLP_SLOTS, hidden // MLP_SLOTS + EXTRA

    def whole(array):
        return pl.BlockSpec(array.shape, lambda i, pos: (0,) * array.ndim, pipeline_mode=pl.Buffered(1))

    def kept(*shape):
        return pl.BlockSpec(shape, lambda i, pos: (0,) * len(shape))

    row = pl.BlockSpec((block, width), lambda i, pos: (i, 0))
    cols = pl.BlockSpec((n_shards, 1, ctx_rows, block), lambda i, pos: (0, i // per_seq, 0, i % per_seq))
    dn_shape, up_shape = (n_shards, half, dn_rows, width), (n_shards, half, up_rows, width)
    consts = [vecs, proj, up, down] + fetched
    return pl.pallas_call(
        partial(middle_kernel, n_others=n_others, chunk=min(1024, hidden)),
        grid_spec=pltpu.PrefetchScalarGridSpec(
            num_scalar_prefetch=1,
            grid=(rows // block,),
            in_specs=[row, row, cols] + [whole(array) for array in consts],
            out_specs=[row, row, cols, kept(*dn_shape), kept(*dn_shape), kept(*up_shape), kept(*up_shape)],
            scratch_shapes=[
                pltpu.VMEM((n_others, ctx_rows, width), bf16),
                pltpu.VMEM((n_others, width, hidden), bf16),
                pltpu.VMEM((n_others, hidden, width), bf16),
                pltpu.VMEM((1, n_shards * hidden), f32),
                pltpu.VMEM((block, n_shards * hidden), bf16),
                pltpu.VMEM((block, n_shards * hidden), f32),
                pltpu.VMEM((n_shards, ctx_rows, width), f32),
                pltpu.VMEM((n_shards, width, hidden), f32),
                pltpu.VMEM((n_shards, hidden, width), f32),
                pltpu.VMEM((8, width), f32),
                pltpu.VMEM((1, n_shards * hidden), f32),
            ],
        ),
        out_shape=[
            jax.ShapeDtypeStruct((rows, width), bf16),
            jax.ShapeDtypeStruct((rows, width), f32),
            jax.ShapeDtypeStruct(ctx.shape, bf16),
            jax.ShapeDtypeStruct(dn_shape, bf16),
            jax.ShapeDtypeStruct(dn_shape, bf16),
            jax.ShapeDtypeStruct(up_shape, bf16),
            jax.ShapeDtypeStruct(up_shape, bf16),
        ],
        compiler_params=kernel_params(),
        cost_estimate=cost(30 << 30, 30 << 20),
        name="middle",
    )(pos, x, out_grad, ctx, *consts)


def piece_number(pos, slot, cut):
    number = 0
    for k, bit in enumerate(cut):
        own = lax.bitwise_and(lax.shift_right_logical(pos, bit.bit_length() - 1), 1)
        flip = (slot >> (len(cut) - 1 - k)) & 1
        number = number + (lax.bitwise_xor(own, flip) << k)
    return number


def attn_bwd_kernel(
    pos_ref,
    x_ref,
    packed_ref,
    probs_ref,
    ctx_low_ref,
    sums_ref,
    *refs,
    head,
    cut,
    extra,
    q_block,
    unroll,
):
    grad_ref, keep_ref, send_ref, bias_ref, *refs = refs[-10:]
    value_ref, key_acc, value_acc, weight_acc, grad_a, grad_b = refs
    step = pl.program_id(0)
    seq = x_ref.shape[0]
    n_shards = packed_ref.shape[0]
    scale = HEAD_DIM**-0.5
    for t in range(n_shards):
        value_ref[t] = packed_ref[t, 0, 2 * HEAD_DIM : 3 * HEAD_DIM, :].T
    tiles = list(range(0, seq, q_block))
    buffers = (grad_a, grad_b)

    def start(t, c, ref):
        ref[...] = mm(value_ref[t], ctx_low_ref[t, 0, :, c : c + q_block])

    def finish(t, c, ref):
        cols = slice(c, c + q_block)
        probs_low = probs_ref[t, 0, 0, :, cols]
        probs = probs_low.astype(f32)
        weighted = probs * ref[...]
        total = jnp.sum(weighted, axis=0, keepdims=True)
        score_low = (weighted - probs * total).astype(bf16)
        grad_query = mm(packed_ref[t, 0, HEAD_DIM : 2 * HEAD_DIM, :], score_low) * scale
        grad_ref[t, 0, :HEAD_DIM, cols] = grad_query.astype(bf16)
        grad_key = mm_nt(packed_ref[t, 0, :HEAD_DIM, cols], score_low)
        grad_value = mm_nt(ctx_low_ref[t, 0, :, cols], probs_low)
        if c > 0:
            grad_key = key_acc[...] + grad_key
            grad_value = value_acc[...] + grad_value
        if c + q_block < seq:
            key_acc[...] = grad_key
            value_acc[...] = grad_value
        else:
            grad_ref[t, 0, HEAD_DIM : 2 * HEAD_DIM, :] = (grad_key * scale).astype(bf16)
            grad_ref[t, 0, 2 * HEAD_DIM :, :] = grad_value.astype(bf16)

    start(0, 0, buffers[0])

    def one_shard(t, carry):
        for j, c in enumerate(tiles):
            if j + 1 < len(tiles):
                start(t, tiles[j + 1], buffers[(j + 1) % 2])
            elif not unroll:
                start(jnp.minimum(t + 1, n_shards - 1), 0, buffers[(j + 1) % 2])
            elif t + 1 < n_shards:
                start(t + 1, 0, buffers[(j + 1) % 2])
            finish(t, c, buffers[j % 2])
        return carry

    if unroll:
        for t in range(n_shards):
            one_shard(t, 0)
    else:
        lax.fori_loop(0, n_shards, one_shard, 0)

    @pl.when(step == 0)
    def _():
        weight_acc[...] = jnp.zeros_like(weight_acc)
        bias_ref[...] = sums_ref[...]

    ones = jnp.ones((8, seq), bf16)
    for t in range(n_shards):
        weight_acc[t] += mm(grad_ref[t, 0], x_ref[...])
        bias_ref[t, head : head + 1] += mm_nt(ones, grad_ref[t, 0])[:1]

    @pl.when(step == pl.num_programs(0) - 1)
    def _():
        slots = 1 << len(cut)
        half = slots // 2
        rows = PART_ROWS // slots
        for slot in range(slots):
            at = piece_number(pos_ref[0], slot, cut)
            ref = keep_ref if slot < half else send_ref
            for t in range(n_shards):
                ref[t, slot % half, :rows] = weight_acc[t, aligned(at, rows, 8), :].astype(bf16)
                if extra:
                    padded = jnp.concatenate(
                        [bias_ref[t], jnp.zeros((EXTRA, ref.shape[3] - PART_ROWS), f32)], axis=1
                    )
                    ref[t, slot % half, rows:] = padded.astype(bf16)


def attn_bwd(pos, x, packed, probs, ctx_low, sums, head, first, group, cut, extra, unroll, earlier):
    rows, width = x.shape
    n_shards, n_seq = packed.shape[:2]
    q_block = 256
    slots = 1 << len(cut)
    each = PART_ROWS // slots + (EXTRA if extra else 0)
    pieces = (n_shards, slots // 2, group * each, width)
    piece = pl.BlockSpec((n_shards, slots // 2, each, width), lambda s, pos: (0, 0, head - first, 0))
    sum_spec = pl.BlockSpec(sums.shape, lambda s, pos: (0, 0, 0))
    return pl.pallas_call(
        partial(attn_bwd_kernel, head=head, cut=cut, extra=extra, q_block=q_block, unroll=unroll),
        grid_spec=pltpu.PrefetchScalarGridSpec(
            num_scalar_prefetch=1,
            grid=(n_seq,),
            in_specs=[
                pl.BlockSpec((SEQ_LEN, width), lambda s, pos: (s, 0)),
                pl.BlockSpec((n_shards, 1, PART_ROWS, SEQ_LEN), lambda s, pos: (0, s, head, 0)),
                pl.BlockSpec((n_shards, 1, 1, SEQ_LEN, SEQ_LEN), lambda s, pos: (0, s, head, 0, 0)),
                pl.BlockSpec((n_shards, 1, HEAD_DIM, SEQ_LEN), lambda s, pos: (0, s, head, 0)),
                sum_spec,
            ]
            + [pl.BlockSpec(memory_space=pl.ANY)] * len(earlier),
            out_specs=[
                pl.BlockSpec((n_shards, 1, PART_ROWS, SEQ_LEN), lambda s, pos: (0, s, 0, 0)),
                piece,
                piece,
                sum_spec,
            ],
            scratch_shapes=[
                pltpu.VMEM((n_shards, SEQ_LEN, HEAD_DIM), bf16),
                pltpu.VMEM((HEAD_DIM, SEQ_LEN), f32),
                pltpu.VMEM((HEAD_DIM, SEQ_LEN), f32),
                pltpu.VMEM((n_shards, PART_ROWS, width), f32),
                pltpu.VMEM((SEQ_LEN, q_block), f32),
                pltpu.VMEM((SEQ_LEN, q_block), f32),
            ],
        ),
        out_shape=[
            jax.ShapeDtypeStruct((n_shards, n_seq, PART_ROWS, SEQ_LEN), bf16),
            jax.ShapeDtypeStruct(pieces, bf16),
            jax.ShapeDtypeStruct(pieces, bf16),
            jax.ShapeDtypeStruct(sums.shape, f32),
        ],
        input_output_aliases={6: 1, 7: 2} if earlier else {},
        compiler_params=kernel_params(48_000_000),
        cost_estimate=cost(8 << 30, 10 << 20),
        name="attn_bwd",
    )(pos, x, packed, probs, ctx_low, sums, *earlier)


def input_grad_kernel(pos_ref, grad_one_ref, own_ref, *refs, n_others):
    fetched, grads, out_ref, got_ref = refs[: 2 * n_others], refs[2 * n_others : -2], refs[-2], refs[-1]
    half = own_ref.shape[0] // 2

    @pl.when(pl.program_id(0) == 0)
    def _():
        parity = lax.rem(pos_ref[0], 2)
        for t in range(n_others):
            for k in range(2):
                side = parity if k == 0 else 1 - parity
                got_ref[t, aligned(side, half, half), :] = fetched[2 * t + k][:half]

    total = grad_one_ref[...]
    for t in range(n_others + 1):
        weight = own_ref if t == 0 else got_ref.at[t - 1]
        for head, ref in enumerate(grads):
            total = total + mm_tn(ref[t, 0], weight[head * PART_ROWS : (head + 1) * PART_ROWS, :])
    out_ref[...] = total.astype(bf16)


def input_gradient(pos, grad_one, own, fetched, packed_grads):
    rows, width = grad_one.shape
    n_shards = packed_grads[0].shape[0]
    block = 512
    per_seq = SEQ_LEN // block
    row = pl.BlockSpec((block, width), lambda i, pos: (i, 0))
    cols = pl.BlockSpec((n_shards, 1, PART_ROWS, block), lambda i, pos: (0, i // per_seq, 0, i % per_seq))

    def whole(array):
        return pl.BlockSpec(array.shape, lambda i, pos: (0, 0), pipeline_mode=pl.Buffered(1))

    return pl.pallas_call(
        partial(input_grad_kernel, n_others=n_shards - 1),
        grid_spec=pltpu.PrefetchScalarGridSpec(
            num_scalar_prefetch=1,
            grid=(rows // block,),
            in_specs=[row, whole(own)] + [whole(v) for v in fetched] + [cols] * len(packed_grads),
            out_specs=row,
            scratch_shapes=[pltpu.VMEM((n_shards - 1,) + own.shape, bf16)],
        ),
        out_shape=jax.ShapeDtypeStruct((rows, width), bf16),
        compiler_params=kernel_params(48_000_000),
        cost_estimate=cost(4 << 30, 12 << 20),
        name="input_gradient",
    )(pos, grad_one, own, *fetched, *packed_grads)


def mlp_place_kernel(pos_ref, dn_near, dn_far, up_near, up_far, proj_out, up_out, dn_out):
    low = lax.rem(pos_ref[0], MLP_SLOTS)
    half = MLP_SLOTS // 2
    width = proj_out.shape[1]
    hidden = dn_out.shape[0]
    dn_rows, up_rows, proj_rows = hidden // MLP_SLOTS, width // MLP_SLOTS, proj_out.shape[0] // MLP_SLOTS
    for slot in range(MLP_SLOTS):
        dn_ref = dn_near if slot < half else dn_far
        up_ref = up_near if slot < half else up_far
        k = slot % half
        at = lax.bitwise_xor(low, DOWN_BITS[slot])
        dn_out[aligned(at, dn_rows, dn_rows), :] = dn_ref[k, :dn_rows].astype(f32)
        proj_out[aligned(at, proj_rows, proj_rows), :] = dn_ref[k, dn_rows:].astype(f32)
        rows = aligned(lax.bitwise_xor(low, UP_BITS[slot]), up_rows, up_rows)
        for j in range(hidden // width):
            up_out[rows, j * width : (j + 1) * width] = up_ref[k, j * up_rows : (j + 1) * up_rows].astype(f32)


def mlp_place(pos, dn_parts, up_parts, ctx_rows, width, hidden):
    return pl.pallas_call(
        mlp_place_kernel,
        in_specs=[pl.BlockSpec(memory_space=pltpu.SMEM)] + [in_vmem()] * 4,
        out_specs=[in_vmem()] * 3,
        out_shape=[
            jax.ShapeDtypeStruct((ctx_rows, width), f32),
            jax.ShapeDtypeStruct((width, hidden), f32),
            jax.ShapeDtypeStruct((hidden, width), f32),
        ],
        compiler_params=kernel_params(48_000_000),
        cost_estimate=cost(0, 14 << 20),
        name="mlp_place",
    )(pos, *dn_parts, *up_parts)


def qkv_place_kernel(pos_ref, *refs, groups):
    bias_ref, out_ref, query_ref, value_ref = refs[-4:]
    for g, (first, group, cut, each) in enumerate(groups):
        slots = 1 << len(cut)
        half = slots // 2
        rows = PART_ROWS // slots
        for slot in range(slots):
            at = aligned(piece_number(pos_ref[0], slot, cut), rows, 8)
            for k in range(group):
                value = refs[2 * g + slot // half][slot % half, k * each : k * each + rows]
                out_ref[first + k, at, :] = value.astype(f32)
    heads = out_ref.shape[0]
    for k, ref in ((0, query_ref), (2, value_ref)):
        parts = [bias_ref[h : h + 1, k * HEAD_DIM : (k + 1) * HEAD_DIM] for h in range(heads)]
        ref[...] = jnp.concatenate(parts, axis=1).reshape(heads * HEAD_DIM)


def qkv_place(pos, parts, bias, groups, heads):
    flat = [half for pair in parts for half in pair]
    vector = jax.ShapeDtypeStruct((heads * HEAD_DIM,), f32)
    return pl.pallas_call(
        partial(qkv_place_kernel, groups=groups),
        in_specs=[pl.BlockSpec(memory_space=pltpu.SMEM)] + [in_vmem()] * (len(flat) + 1),
        out_specs=[in_vmem()] * 3,
        out_shape=[jax.ShapeDtypeStruct((heads, PART_ROWS, flat[0].shape[2]), f32), vector, vector],
        compiler_params=kernel_params(48_000_000),
        cost_estimate=cost(0, 3 << 20),
        name="qkv_place",
    )(pos, *flat, bias)


def swap_dp(value, bits, n_dp):
    return lax.ppermute(value, "dp", [(i, i ^ bits) for i in range(n_dp)])


def shift_tensor(value, by, n_tensor):
    return lax.ppermute(value, "tensor", [((i + by) % n_tensor, i) for i in range(n_tensor)])


def reduce_pieces(keep, send, order, n_dp, n_tensor):
    halved = [axis for axis in order if axis != "tensor"]
    got = swap_dp(send, 1, n_dp)
    got = after(got, (yield send))
    parts = [keep[t].astype(f32) + got[t].astype(f32) for t in range(n_tensor)]
    for axis in order:
        if axis == "tensor":
            outs = [parts[by].astype(bf16) for by in range(1, n_tensor)]
            gots = [shift_tensor(out, -by, n_tensor) for by, out in enumerate(outs, 1)]
            gots = after(gots, (yield outs))
            parts = [sum((got.astype(f32) for got in gots), parts[0])]
        else:
            cut = parts[0].shape[0] // 2
            out = jnp.stack([part[cut:].astype(bf16) for part in parts])
            got = swap_dp(out, axis, n_dp)
            got = after(got, (yield out))
            parts = [part[:cut] + got[t].astype(f32) for t, part in enumerate(parts)]
    own = parts[0]
    bits = 2
    while bits < n_dp:
        if bits not in halved:
            out = own.astype(bf16)
            got = swap_dp(out, bits, n_dp)
            got = after(got, (yield out))
            own = own + got.astype(f32)
        bits *= 2
    near = own.astype(bf16)
    for axis in reversed(halved):
        got = swap_dp(near, axis, n_dp)
        got = after(got, (yield near))
        near = jnp.concatenate([near, got], axis=0)
    got = swap_dp(near, 1, n_dp)
    got = after(got, (yield near))
    return near, got, own


class Sums:
    def __init__(self):
        self.live, self.done, self.fresh = {}, {}, set()

    def add(self, name, generator):
        self.live[name] = generator
        self.fresh.add(name)

    def step(self, ready, *names):
        sent = []
        for name in names:
            if name in self.live:
                try:
                    sent.append(self.live[name].send(None if name in self.fresh else ready))
                    self.fresh.discard(name)
                except StopIteration as stop:
                    self.done[name] = stop.value
                    del self.live[name]
        return sent

    def finish(self):
        while self.live:
            self.step((), *list(self.live))


def after(value, *others):
    return lax.optimization_barrier((value, others))[0]


def sequence_body(n_dp, n_tensor, *arrays):
    (
        layer_input,
        output_grad,
        qkv_weight,
        query_bias,
        value_bias,
        proj_weight,
        proj_bias,
        first_gain,
        first_shift,
        up_weight,
        up_bias,
        down_weight,
        down_bias,
        second_gain,
        second_shift,
    ) = arrays
    rows, width = layer_input.shape
    n_seq = rows // SEQ_LEN
    ctx_rows, hidden = proj_weight.shape[0], up_weight.shape[1]
    n_heads = ctx_rows // HEAD_DIM
    pos = lax.axis_index("dp").astype(jnp.int32).reshape(1)
    shifts = range(1, n_tensor)

    qkv_half, own_bias = pack_qkv(pos, qkv_weight, query_bias, value_bias)
    qkv_near = [shift_tensor(qkv_half, by, n_tensor) for by in shifts]
    vectors = [proj_bias, first_gain, first_shift, down_bias, second_gain, second_shift]
    mlp_half, vecs = pack_mlp(after(pos, qkv_half), proj_weight, down_weight, up_weight, up_bias, vectors)
    shapes = [
        jax.ShapeDtypeStruct((n_tensor, n_seq, n_heads * PART_ROWS, SEQ_LEN), bf16),
        jax.ShapeDtypeStruct((n_tensor, n_seq, n_heads, SEQ_LEN, SEQ_LEN), bf16),
        jax.ShapeDtypeStruct((n_tensor, n_seq, n_heads * HEAD_DIM, SEQ_LEN), bf16),
    ]
    mlp_near = [shift_tensor(mlp_half, by, n_tensor) for by in shifts]
    x = after(layer_input, mlp_half)
    stacks = attn_fwd(pos, x, (qkv_weight, own_bias), 0, False, shapes, ())
    qkv_near = after(qkv_near, stacks[2])
    qkv_far = [swap_dp(near, 1, n_dp) for near in qkv_near]
    for t in shifts:
        stacks = attn_fwd(pos, layer_input, (qkv_near[t - 1], qkv_far[t - 1]), t, True, shapes, stacks)
    packed, probs, ctx = stacks
    mlp_near = after(mlp_near, ctx)
    mlp_far = [swap_dp(near, 1, n_dp) for near in mlp_near]
    fetched = [half for pair in zip(mlp_near, mlp_far) for half in pair]
    result, grad_one, ctx_low, dn_keep, dn_send, up_keep, up_send = middle(
        pos, layer_input, output_grad, ctx, vecs, proj_weight, up_weight, down_weight, fetched
    )
    sums = Sums()
    sums.add("dn", reduce_pieces(dn_keep, dn_send, DOWN_ORDER, n_dp, n_tensor))
    sums.add("up", reduce_pieces(up_keep, up_send, UP_ORDER, n_dp, n_tensor))
    bias_sums = jnp.zeros((n_tensor, EXTRA, PART_ROWS), f32)
    packed_grads = []
    ready = ()
    early = n_heads - 1
    stacked = ()
    early_cut, early_order = (1, 2), ("tensor", 2)
    for head in range(n_heads):
        last = head == early
        if last and early:
            sums.add("qa", reduce_pieces(*stacked, early_order, n_dp, n_tensor))
        sent = sums.step(ready, *SCHEDULE[min(head, len(SCHEDULE) - 3)])
        x = after(layer_input, sent)
        grads, keep, send, bias_sums = attn_bwd(
            pos,
            x,
            packed,
            probs,
            ctx_low,
            bias_sums,
            head,
            early if last else 0,
            1 if last else early,
            (1,) if last else early_cut,
            last,
            head in UNROLLED,
            () if last else stacked,
        )
        ready = bias_sums
        packed_grads.append(grads)
        if not last:
            stacked = (keep, send)
    sums.add("qb", reduce_pieces(keep, send, ("tensor",), n_dp, n_tensor))
    sent = sums.step(ready, *SCHEDULE[-2])
    qkv_fetched = [half for pair in zip(qkv_near, qkv_far) for half in pair]
    input_grad = input_gradient(pos, after(grad_one, sent), qkv_weight, qkv_fetched, packed_grads)
    ready = input_grad
    for name in SCHEDULE[-1]:
        sent = sums.step(ready, name)
        ready = sent or ready
    sums.finish()
    dn_near, dn_far, _ = sums.done["dn"]
    up_near, up_far, up_own = sums.done["up"]
    proj_wg, up_wg, dn_wg = mlp_place(pos, (dn_near, dn_far), (up_near, up_far), ctx_rows, width, hidden)
    groups = [(0, early, early_cut, PART_ROWS // 4)] if early else []
    groups.append((early, 1, (1,), PART_ROWS // 2 + EXTRA))
    parts = [sums.done[name][:2] for name in ("qa", "qb") if name in sums.done]
    bias = sums.done["qb"][2][0, -EXTRA:]
    qkv_wg, query_bg, value_bg = qkv_place(pos, parts, bias, groups, n_heads)
    small = up_own[0, -EXTRA:]
    return (
        result,
        input_grad,
        qkv_wg.reshape(n_heads * PART_ROWS, width),
        query_bg,
        value_bg,
        proj_wg,
        small[0],
        small[1],
        small[2],
        up_wg,
        small[8 : 8 + hidden // width].reshape(hidden),
        dn_wg,
        small[3],
        small[4],
        small[5],
    )


SCHEDULE = (
    ("dn", "up"),
    ("dn", "up"),
    ("dn", "up"),
    ("qa", "dn", "up", "qa"),
    ("qb", "qa", "dn", "up", "qb"),
    ("qb", "qa", "dn", "up", "qb", "qa", "up", "dn", "qb", "qa", "up", "dn", "qb", "qa"),
)
UNROLLED = ()


def solution(mesh):
    n_dp, n_tensor = mesh.shape["dp"], mesh.shape["tensor"]

    def body(*arrays):
        rows = arrays[0].shape[0]
        if rows % SEQ_LEN == 0 and n_dp % 8 == 0 and n_dp & (n_dp - 1) == 0:
            return sequence_body(n_dp, n_tensor, *arrays)
        return token_body(*arrays)

    return jax.shard_map(
        body,
        mesh=mesh,
        in_specs=(
            P(("dp", "tensor"), None),
            P(("dp", "tensor"), None),
            P("tensor", None),
            P("tensor"),
            P("tensor"),
            P("tensor", None),
            P(),
            P(),
            P(),
            P(None, "tensor"),
            P("tensor"),
            P("tensor", None),
            P(),
            P(),
            P(),
        ),
        out_specs=(
            P(("dp", "tensor"), None),
            P(("dp", "tensor"), None),
            P("tensor", None),
            P("tensor"),
            P("tensor"),
            P("tensor", None),
            P(),
            P(),
            P(),
            P(None, "tensor"),
            P("tensor"),
            P("tensor", None),
            P(),
            P(),
            P(),
        ),
        check_vma=False,
    )
```

profile of v0, /device:TPU:0, one launch (start us, length us, event | category | flops | bytes accessed | tf_op | source)
XLA Modules:
  0.0 216.8 jit_solution(10784949918512652152)
XLA Ops:
  0.7 1.8 pack_qkv.1
  2.5 2.9 %collective-permute-start = (bf16[400,512]{1,0:T(8,128)(2,1)}, bf16[400,512]{1,0:T(8,128)(2,1)S(1)}, u32[]{:S(2)}, u32[]{:S(2)}) collective-permute-start(bf16[400,512]{1,0:T(8,128)(2,1)} %get-tuple-element.88), channel_id=1, source_target_pairs={{1,0},{0,1},{3,2},{2,3},{5,4},{4,5},{7,6},{6,7},{9,8},{8,9},{11,10... | collective-permute-start | bytes 1228808 | tf_op jit(solution)/shard_map/ppermute | solution.py:969
  5.4 2.4 %pack_mlp.1 = (bf16[1168,512]{1,0:T(8,128)(2,1)}, f32[16,512]{1,0:T(8,128)}) custom-call(s32[1]{0:T(128)} %bitcast.pos_ref, bf16[256,512]{1,0:T(8,128)(2,1)} %proj_own.1, bf16[1024,512]{1,0:T(8,128)(2,1)} %down_own.1, bf16[512,1024]{1,0:T(8,128)(2,1)} %up_own.1, bf16[1024]{0:T(1024)(128)(2,1)} %up_b_ref.1, bf16[512]{0:T(512)(128)(2,1)} %refs_0_.2, ...), custom_call_target="tpu_custom_call" | custom-call | bytes 3145728 | tf_op jit(solution)/shard_map/pack_mlp/pallas_call | solution.py:361
  7.8 19.7 %attn_fwd.2 = (bf16[2,2,768,1024]{3,2,1,0:T(8,128)(2,1)}, bf16[2,2,4,1024,1024]{4,3,2,1,0:T(8,128)(2,1)}, bf16[2,2,256,1024]{3,2,1,0:T(8,128)(2,1)}) custom-call(s32[1]{0:T(128)} %bitcast.pos_ref, bf16[2048,512]{1,0:T(8,128)(2,1)} %x_ref.8, bf16[768,512]{1,0:T(8,128)(2,1)} %own_ref.1, bf16[32,512]{1,0:T(8,128)(2,1)} %get-tuple-element.92.refs_1_), custom_call_target="tpu_custom_call" | custom-call | flops 14495514624 | bytes 25165824 | tf_op jit(solution)/shard_map/attn_fwd/pallas_call | solution.py:450
  27.6 1.7 collective-permute-done.1.refs_1_
  29.4 0.8 copy-done.5
  30.2 19.8 %attn_fwd.3 = (bf16[2,2,768,1024]{3,2,1,0:T(8,128)(2,1)}, bf16[2,2,4,1024,1024]{4,3,2,1,0:T(8,128)(2,1)}, bf16[2,2,256,1024]{3,2,1,0:T(8,128)(2,1)}) custom-call(s32[1]{0:T(128)} %bitcast.pos_ref, bf16[2048,512]{1,0:T(8,128)(2,1)} %x_ref.8, bf16[400,512]{1,0:T(8,128)(2,1)} %copy-done.3, ...), custom_call_target="tpu_custom_call", output_to_operand_aliasing={{0}: (4, {}), {1}: (5, {}), {2}: (6, {})} | custom-call | flops 1811939328 | bytes 25165824 | tf_op jit(solution)/shard_map/attn_fwd/pallas_call | solution.py:450
  49.9 0.2 collective-permute-start.3
  50.2 3.0 %collective-permute-done.3.refs_1_ = bf16[1168,512]{1,0:T(8,128)(2,1)} collective-permute-done((bf16[1168,512]{1,0:T(8,128)(2,1)}, bf16[1168,512]{1,0:T(8,128)(2,1)}, u32[]{:S(2)}, u32[]{:S(2)}) %collective-permute-start.3) | collective-permute-done | bytes 1196064 | tf_op jit(solution)/shard_map/ppermute | solution.py:965
  53.2 43.8 %middle.1 = (bf16[2048,512]{1,0:T(8,128)(2,1)}, f32[2048,512]{1,0:T(8,128)}, bf16[2,2,256,1024]{3,2,1,0:T(8,128)(2,1)}, bf16[2,4,160,512]{3,2,1,0:T(8,128)(2,1)}...) custom-call(s32[1]{0:T(128)} %bitcast.pos_ref, ...), custom_call_target="tpu_custom_call" | custom-call | flops 32212254720 | bytes 31457280 | tf_op jit(solution)/shard_map/middle/pallas_call | solution.py:662
  97.0 0.3 collective-permute-start.6
  97.3 0.2 collective-permute-start.4
  97.5 1.6 copy-done
  99.1 1.6 copy-done.1
  100.7 14.7 %attn_bwd.4 = (bf16[2,2,192,1024]{3,2,1,0:T(8,128)(2,1)S(1)}, bf16[2,2,144,512]{3,2,1,0:T(8,128)(2,1)S(1)}, bf16[2,2,144,512]{3,2,1,0:T(8,128)(2,1)S(1)}, f32[2,16,192]{2,1,0:T(8,128)S(1)}) custom-call(s32[1]{0:T(128)} %bitcast.pos_ref, bf16[2048,512]{1,0:T(8,128)(2,1)S(1)} %copy-done, bf16[2,2,768,1024]{3,2,1,0:T(8,128)(2,1)} %get-tuple-element.106.packed_ref, ...), custom_call_target="tpu_custom_call" | custom-call | flops 8589934592 | bytes 10485760 | tf_op jit(solution)/shard_map/attn_bwd/pallas_call | solution.py:811
  115.5 0.4 convert_add_fusion.1
  116.0 2.1 collective-permute-start.7
  118.2 0.2 fusion
  118.4 1.6 collective-permute-start.5
  119.9 14.7 %attn_bwd.5 = (bf16[2,2,192,1024]{3,2,1,0:T(8,128)(2,1)S(1)}, bf16[2,2,144,512]{3,2,1,0:T(8,128)(2,1)S(1)}, bf16[2,2,144,512]{3,2,1,0:T(8,128)(2,1)S(1)}, f32[2,16,192]{2,1,0:T(8,128)S(1)}) custom-call(s32[1]{0:T(128)} %bitcast.pos_ref, bf16[2048,512]{1,0:T(8,128)(2,1)S(1)} %copy-done, ...), custom_call_target="tpu_custom_call", output_to_operand_aliasing={{1}: (6, {}), {2}: (7, {})} | custom-call | flops 8589934592 | bytes 10485760 | tf_op jit(solution)/shard_map/attn_bwd/pallas_call | solution.py:811
  134.6 0.1 fusion.6
  134.7 0.6 collective-permute-start.9
  135.3 0.3 bitcast_add_fusion
  135.6 1.6 collective-permute-start.8
  137.2 14.6 %attn_bwd.6 = (bf16[2,2,192,1024]{3,2,1,0:T(8,128)(2,1)S(1)}, bf16[2,2,144,512]{3,2,1,0:T(8,128)(2,1)S(1)}, bf16[2,2,144,512]{3,2,1,0:T(8,128)(2,1)S(1)}, f32[2,16,192]{2,1,0:T(8,128)S(1)}) custom-call(s32[1]{0:T(128)} %bitcast.pos_ref, bf16[2048,512]{1,0:T(8,128)(2,1)S(1)} %copy-done, ...), custom_call_target="tpu_custom_call", output_to_operand_aliasing={{1}: (6, {}), {2}: (7, {})} | custom-call | flops 8589934592 | bytes 10485760 | tf_op jit(solution)/shard_map/attn_bwd/pallas_call | solution.py:811
  151.9 0.1 fusion.2
  152.1 0.6 collective-permute-start.13
  152.7 0.1 slice_add_fusion
  152.8 1.1 collective-permute-start.12
  154.0 0.1 fusion.5
  154.0 1.6 collective-permute-start.11
  155.6 15.2 %attn_bwd.7 = (bf16[2,2,192,1024]{3,2,1,0:T(8,128)(2,1)S(1)}, bf16[2,1,112,512]{3,2,1,0:T(8,128)(2,1)S(1)}, bf16[2,1,112,512]{3,2,1,0:T(8,128)(2,1)S(1)}, f32[2,16,192]{2,1,0:T(8,128)}) custom-call(s32[1]{0:T(128)} %bitcast.pos_ref, bf16[2048,512]{1,0:T(8,128)(2,1)S(1)} %copy-done, bf16[2,2,768,1024]{3,2,1,0:T(8,128)(2,1)} %get-tuple-element.106.packed_ref, ...), custom_call_target="tpu_custom_call" | custom-call | flops 8589934592 | bytes 10485760 | tf_op jit(solution)/shard_map/attn_bwd/pallas_call | solution.py:811
  170.9 2.6 %collective-permute-start.20 = (bf16[1,160,512]{2,1,0:T(8,128)(2,1)S(1)}, bf16[1,160,512]{2,1,0:T(8,128)(2,1)S(1)}, u32[]{:S(2)}, u32[]{:S(2)}) collective-permute-start(bf16[1,160,512]{2,1,0:T(8,128)(2,1)S(1)} %fusion.7), channel_id=1, source_target_pairs={{0,16},{2,18},{4,20},{6,22},{8,24},{10,26},{12,28},{14,30},{16,0},... | collective-permute-start | bytes 491528 | tf_op jit(solution)/shard_map/ppermute | solution.py:965
  173.6 0.4 collective-permute-start.19
  174.0 0.6 collective-permute-start.16
  174.5 0.1 bitcast_add_fusion.1
  174.7 1.6 collective-permute-start.15
  176.3 7.7 %input_gradient.1 = bf16[2048,512]{1,0:T(8,128)(2,1)} custom-call(s32[1]{0:T(128)} %bitcast.pos_ref, f32[2048,512]{1,0:T(8,128)} %get-tuple-element.136.grad_one_ref, bf16[768,512]{1,0:T(8,128)(2,1)S(1)} %copy-done.2, bf16[400,512]{1,0:T(8,128)(2,1)S(1)} %copy-done.4, bf16[400,512]{1,0:T(8,128)(2,1)S(1)} %copy-done.6, ...), custom_call_target="tpu_custom_call" | custom-call | flops 4294967296 | bytes 12582912 | tf_op jit(solution)/shard_map/input_gradient/pallas_call | solution.py:883
  184.1 0.6 collective-permute-start.18
  184.7 1.1 collective-permute-start.17
  185.8 1.0 collective-permute-start.23
  186.9 1.5 collective-permute-done.19
  188.5 1.6 collective-permute-start.24
  190.1 0.6 fusion.20
  190.7 0.1 collective-permute-start.22
  190.9 0.7 collective-permute-done.17
  191.6 2.8 %collective-permute-start.21 = (bf16[1,144,512]{2,1,0:T(8,128)(2,1)S(1)}, bf16[1,144,512]{2,1,0:T(8,128)(2,1)S(1)}, u32[]{:S(2)}, u32[]{:S(2)}) collective-permute-start(bf16[1,144,512]{2,1,0:T(8,128)(2,1)S(1)} %fusion.8), channel_id=1, source_target_pairs={{0,16},{2,18},{4,20},{6,22},{8,24},{10,26},{12,28},{14,30},{16,0},... | collective-permute-start | bytes 442376 | tf_op jit(solution)/shard_map/ppermute | solution.py:965
  194.5 0.9 collective-permute-start.28
  195.5 1.5 collective-permute-start.27
  196.9 3.4 %collective-permute-done.22 = bf16[1,112,512]{2,1,0:T(8,128)(2,1)S(1)} collective-permute-done((bf16[1,112,512]{2,1,0:T(8,128)(2,1)S(1)}, bf16[1,112,512]{2,1,0:T(8,128)(2,1)S(1)}, u32[]{:S(2)}, u32[]{:S(2)}) %collective-permute-start.22) | collective-permute-done | bytes 114720 | tf_op jit(solution)/shard_map/ppermute | solution.py:965
  200.3 0.1 fusion.15
  200.5 0.6 collective-permute-done.21
  201.1 0.1 add_convert_fusion.3
  201.2 1.3 collective-permute-start.25
  202.5 6.9 %collective-permute-done.28 = bf16[2,144,512]{2,1,0:T(8,128)(2,1)S(1)} collective-permute-done((bf16[2,144,512]{2,1,0:T(8,128)(2,1)S(1)}, bf16[2,144,512]{2,1,0:T(8,128)(2,1)S(1)}, u32[]{:S(2)}, u32[]{:S(2)}) %collective-permute-start.28) | collective-permute-done | bytes 294944 | tf_op jit(solution)/shard_map/ppermute | solution.py:965
  209.5 0.1 collective-permute-start.32
  209.6 0.5 collective-permute-start.31
  210.2 0.1 fusion.18
  210.3 0.1 collective-permute-start.29
  210.4 0.6 copy.37
  211.0 0.5 collective-permute-start.30
  211.5 1.6 collective-permute-done.30.refs_3_
  213.0 1.3 qkv_place.1
  214.3 2.5 %mlp_place.1 = (f32[256,512]{1,0:T(8,128)}, f32[512,1024]{1,0:T(8,128)}, f32[1024,512]{1,0:T(8,128)}) custom-call(s32[1]{0:T(128)} %bitcast.pos_ref, bf16[4,160,512]{2,1,0:T(8,128)(2,1)S(1)} %pad_maximum_fusion.dn_near, bf16[4,160,512]{2,1,0:T(8,128)(2,1)S(1)} %collective-permute-done.31.dn_far, bf16[4,144,512]{2,1,0:T(8,128)(2,1)S(1)} %pad_maximum_fusion.2.up_near, ...), custom_call_target="tpu_custom_call" | custom-call | bytes 14680064 | tf_op jit(solution)/shard_map/mlp_place/pallas_call | solution.py:918
  (69 shorter events, 1.2 us)
Async XLA Ops:
  2.5 25.1 %collective-permute-start = (bf16[400,512]{1,0:T(8,128)(2,1)}, bf16[400,512]{1,0:T(8,128)(2,1)S(1)}, u32[]{:S(2)}, u32[]{:S(2)}) collective-permute-start(bf16[400,512]{1,0:T(8,128)(2,1)} %get-tuple-element.88), channel_id=1, source_target_pairs={{1,0},{0,1},{3,2},{2,3},{5,4},{4,5},{7,6},{6,7},{9,8},{8,9},{11,10... | collective-permute-start | bytes 1228808 | tf_op jit(solution)/shard_map/ppermute | solution.py:969
  7.8 42.1 %collective-permute-start.2 = (bf16[1168,512]{1,0:T(8,128)(2,1)}, bf16[1168,512]{1,0:T(8,128)(2,1)}, u32[]{:S(2)}, u32[]{:S(2)}) collective-permute-start(bf16[1168,512]{1,0:T(8,128)(2,1)} %get-tuple-element.90), channel_id=1, source_target_pairs={{1,0},{0,1},{3,2},{2,3},{5,4},{4,5},{7,6},{6,7},{9,8},{8,9},{11,10... | collective-permute-start | bytes 3588104 | tf_op jit(solution)/shard_map/ppermute | solution.py:969
  27.5 1.8 copy-start.3
  27.5 1.8 collective-permute-start.1
  29.3 0.8 copy-start.5
  49.9 3.2 %collective-permute-start.3 = (bf16[1168,512]{1,0:T(8,128)(2,1)}, bf16[1168,512]{1,0:T(8,128)(2,1)}, u32[]{:S(2)}, u32[]{:S(2)}) collective-permute-start(bf16[1168,512]{1,0:T(8,128)(2,1)} %collective-permute-done.2.refs_0_), channel_id=1, source_target_pairs={{0,2},{2,0},{4,6},{6,4},{8,10},{10,8},{12,14},{14,12},{16,18},{18,... | collective-permute-start | bytes 3588104 | tf_op jit(solution)/shard_map/ppermute | solution.py:965
  97.0 18.5 %collective-permute-start.6 = (bf16[2,4,144,512]{3,2,1,0:T(8,128)(2,1)}, bf16[2,4,144,512]{3,2,1,0:T(8,128)(2,1)S(1)}, u32[]{:S(2)}, u32[]{:S(2)}) collective-permute-start(bf16[2,4,144,512]{3,2,1,0:T(8,128)(2,1)} %get-tuple-element.104), channel_id=1, source_target_pairs={{0,2},{2,0},{4,6},{6,4},{8,10},{10,8},{12,14},{14,12},{16,18},{18,... | collective-permute-start | bytes 3538952 | tf_op jit(solution)/shard_map/ppermute | solution.py:965
  97.3 20.9 %collective-permute-start.4 = (bf16[2,4,160,512]{3,2,1,0:T(8,128)(2,1)}, bf16[2,4,160,512]{3,2,1,0:T(8,128)(2,1)S(1)}, u32[]{:S(2)}, u32[]{:S(2)}) collective-permute-start(bf16[2,4,160,512]{3,2,1,0:T(8,128)(2,1)} %get-tuple-element.103), channel_id=1, source_target_pairs={{0,2},{2,0},{4,6},{6,4},{8,10},{10,8},{12,14},{14,12},{16,18},{18,... | collective-permute-start | bytes 3932168 | tf_op jit(solution)/shard_map/ppermute | solution.py:965
  97.5 1.6 copy-start
  99.1 1.6 copy-start.1
  100.7 14.7 %copy-start.8 = (bf16[2,4,144,512]{3,2,1,0:T(8,128)(2,1)S(1)}, bf16[2,4,144,512]{3,2,1,0:T(8,128)(2,1)}, u32[]{:S(2)}) copy-start(bf16[2,4,144,512]{3,2,1,0:T(8,128)(2,1)} %get-tuple-element.111) | copy-start | bytes 3538948
  115.8 2.3 %copy-start.7 = (bf16[2,4,160,512]{3,2,1,0:T(8,128)(2,1)S(1)}, bf16[2,4,160,512]{3,2,1,0:T(8,128)(2,1)}, u32[]{:S(2)}) copy-start(bf16[2,4,160,512]{3,2,1,0:T(8,128)(2,1)} %get-tuple-element.102) | copy-start | bytes 3932164
  116.0 18.6 %collective-permute-start.7 = (bf16[2,2,144,512]{3,2,1,0:T(8,128)(2,1)S(1)}, bf16[2,2,144,512]{3,2,1,0:T(8,128)(2,1)S(1)}, u32[]{:S(2)}, u32[]{:S(2)}) collective-permute-start(bf16[2,2,144,512]{3,2,1,0:T(8,128)(2,1)S(1)} %pad_maximum_fusion.1), channel_id=1, source_target_pairs={{0,8},{2,10},{4,12},{6,14},{8,0},{10,2},{12,4},{14,6},{16,24},{18,... | collective-permute-start | bytes 1769480 | tf_op jit(solution)/shard_map/ppermute | solution.py:965
  118.4 17.0 %collective-permute-start.5 = (bf16[4,160,512]{2,1,0:T(8,128)(2,1)S(1)}, bf16[4,160,512]{2,1,0:T(8,128)(2,1)S(1)}, u32[]{:S(2)}, u32[]{:S(2)}) collective-permute-start(bf16[4,160,512]{2,1,0:T(8,128)(2,1)S(1)} %fusion), channel_id=1, source_target_pairs={{1,0},{0,1},{3,2},{2,3},{5,4},{4,5},{7,6},{6,7},{9,8},{8,9},{11,10... | collective-permute-start | bytes 1966088 | tf_op jit(solution)/shard_map/ppermute | solution.py:969
  134.7 17.2 %collective-permute-start.9 = (bf16[2,144,512]{2,1,0:T(8,128)(2,1)S(1)}, bf16[2,144,512]{2,1,0:T(8,128)(2,1)S(1)}, u32[]{:S(2)}, u32[]{:S(2)}) collective-permute-start(bf16[2,144,512]{2,1,0:T(8,128)(2,1)S(1)} %fusion.6), channel_id=1, source_target_pairs={{1,0},{0,1},{3,2},{2,3},{5,4},{4,5},{7,6},{6,7},{9,8},{8,9},{11,10... | collective-permute-start | bytes 884744 | tf_op jit(solution)/shard_map/ppermute | solution.py:969
  135.6 17.0 %collective-permute-start.8 = (bf16[1,2,160,512]{3,2,1,0:T(8,128)(2,1)S(1)}, bf16[1,2,160,512]{3,2,1,0:T(8,128)(2,1)S(1)}, u32[]{:S(2)}, u32[]{:S(2)}) collective-permute-start(bf16[1,2,160,512]{3,2,1,0:T(8,128)(2,1)S(1)} %fusion.4), channel_id=1, source_target_pairs={{0,4},{2,6},{4,0},{6,2},{8,12},{10,14},{12,8},{14,10},{16,20},{18,... | collective-permute-start | bytes 983048 | tf_op jit(solution)/shard_map/ppermute | solution.py:965
  151.9 2.1 collective-permute-start.10
  152.1 18.7 %collective-permute-start.13 = (bf16[1,1,144,512]{3,2,1,0:T(8,128)(2,1)S(1)}, bf16[1,1,144,512]{3,2,1,0:T(8,128)(2,1)S(1)}, u32[]{:S(2)}, u32[]{:S(2)}) collective-permute-start(bf16[1,1,144,512]{3,2,1,0:T(8,128)(2,1)S(1)} %fusion.12), channel_id=1, source_target_pairs={{0,4},{2,6},{4,0},{6,2},{8,12},{10,14},{12,8},{14,10},{16,20},{18,... | collective-permute-start | bytes 442376 | tf_op jit(solution)/shard_map/ppermute | solution.py:965
  152.8 18.0 %collective-permute-start.12 = (bf16[1,1,160,512]{3,2,1,0:T(8,128)(2,1)S(1)}, bf16[1,1,160,512]{3,2,1,0:T(8,128)(2,1)S(1)}, u32[]{:S(2)}, u32[]{:S(2)}) collective-permute-start(bf16[1,1,160,512]{3,2,1,0:T(8,128)(2,1)S(1)} %fusion.10), channel_id=1, source_target_pairs={{0,8},{2,10},{4,12},{6,14},{8,0},{10,2},{12,4},{14,6},{16,24},{18,... | collective-permute-start | bytes 491528 | tf_op jit(solution)/shard_map/ppermute | solution.py:965
  154.0 20.5 %collective-permute-start.11 = (bf16[2,144,512]{2,1,0:T(8,128)(2,1)S(1)}, bf16[2,144,512]{2,1,0:T(8,128)(2,1)S(1)}, u32[]{:S(2)}, u32[]{:S(2)}) collective-permute-start(bf16[2,144,512]{2,1,0:T(8,128)(2,1)S(1)} %fusion.5), channel_id=1, source_target_pairs={{1,0},{0,1},{3,2},{2,3},{5,4},{4,5},{7,6},{6,7},{9,8},{8,9},{11,10... | collective-permute-start | bytes 884744 | tf_op jit(solution)/shard_map/ppermute | solution.py:969
  170.8 3.1 %collective-permute-start.14 = (bf16[2,1,112,512]{3,2,1,0:T(8,128)(2,1)S(1)}, bf16[2,1,112,512]{3,2,1,0:T(8,128)(2,1)S(1)}, u32[]{:S(2)}, u32[]{:S(2)}) collective-permute-start(bf16[2,1,112,512]{3,2,1,0:T(8,128)(2,1)S(1)} %get-tuple-element.129), channel_id=1, source_target_pairs={{0,2},{2,0},{4,6},{6,4},{8,10},{10,8},{12,14},{14,12},{16,18},{18,... | collective-permute-start | bytes 688136 | tf_op jit(solution)/shard_map/ppermute | solution.py:965
  170.9 5.4 %copy-start.2 = (bf16[768,512]{1,0:T(8,128)(2,1)S(1)}, bf16[768,512]{1,0:T(8,128)(2,1)}, u32[]{:S(2)}) copy-start(bf16[768,512]{1,0:T(8,128)(2,1)} %own_ref.1) | copy-start | bytes 2359300
  170.9 5.4 %copy-start.4 = (bf16[400,512]{1,0:T(8,128)(2,1)S(1)}, bf16[400,512]{1,0:T(8,128)(2,1)}, u32[]{:S(2)}) copy-start(bf16[400,512]{1,0:T(8,128)(2,1)} %copy-done.3) | copy-start | bytes 1228804
  170.9 5.4 %copy-start.6 = (bf16[400,512]{1,0:T(8,128)(2,1)S(1)}, bf16[400,512]{1,0:T(8,128)(2,1)}, u32[]{:S(2)}) copy-start(bf16[400,512]{1,0:T(8,128)(2,1)} %copy-done.5) | copy-start | bytes 1228804
  170.9 14.9 %collective-permute-start.20 = (bf16[1,160,512]{2,1,0:T(8,128)(2,1)S(1)}, bf16[1,160,512]{2,1,0:T(8,128)(2,1)S(1)}, u32[]{:S(2)}, u32[]{:S(2)}) collective-permute-start(bf16[1,160,512]{2,1,0:T(8,128)(2,1)S(1)} %fusion.7), channel_id=1, source_target_pairs={{0,16},{2,18},{4,20},{6,22},{8,24},{10,26},{12,28},{14,30},{16,0},... | collective-permute-start | bytes 491528 | tf_op jit(solution)/shard_map/ppermute | solution.py:965
  173.6 14.9 %collective-permute-start.19 = (bf16[1,144,512]{2,1,0:T(8,128)(2,1)S(1)}, bf16[1,144,512]{2,1,0:T(8,128)(2,1)S(1)}, u32[]{:S(2)}, u32[]{:S(2)}) collective-permute-start(bf16[1,144,512]{2,1,0:T(8,128)(2,1)S(1)} %fusion.9), channel_id=1, source_target_pairs={{0,16},{2,18},{4,20},{6,22},{8,24},{10,26},{12,28},{14,30},{16,0},... | collective-permute-start | bytes 442376 | tf_op jit(solution)/shard_map/ppermute | solution.py:965
  174.0 10.1 %collective-permute-start.16 = (bf16[1,112,512]{2,1,0:T(8,128)(2,1)S(1)}, bf16[1,112,512]{2,1,0:T(8,128)(2,1)S(1)}, u32[]{:S(2)}, u32[]{:S(2)}) collective-permute-start(bf16[1,112,512]{2,1,0:T(8,128)(2,1)S(1)} %fusion.14), channel_id=1, source_target_pairs={{1,0},{0,1},{3,2},{2,3},{5,4},{4,5},{7,6},{6,7},{9,8},{8,9},{11,10... | collective-permute-start | bytes 344072 | tf_op jit(solution)/shard_map/ppermute | solution.py:969
  174.7 9.9 %collective-permute-start.15 = (bf16[1,1,144,512]{3,2,1,0:T(8,128)(2,1)S(1)}, bf16[1,1,144,512]{3,2,1,0:T(8,128)(2,1)S(1)}, u32[]{:S(2)}, u32[]{:S(2)}) collective-permute-start(bf16[1,1,144,512]{3,2,1,0:T(8,128)(2,1)S(1)} %fusion.13), channel_id=1, source_target_pairs={{0,4},{2,6},{4,0},{6,2},{8,12},{10,14},{12,8},{14,10},{16,20},{18,... | collective-permute-start | bytes 442376 | tf_op jit(solution)/shard_map/ppermute | solution.py:965
  184.1 6.6 %collective-permute-start.18 = (bf16[1,112,512]{2,1,0:T(8,128)(2,1)S(1)}, bf16[1,112,512]{2,1,0:T(8,128)(2,1)S(1)}, u32[]{:S(2)}, u32[]{:S(2)}) collective-permute-start(bf16[1,112,512]{2,1,0:T(8,128)(2,1)S(1)} %fusion.17), channel_id=1, source_target_pairs={{0,4},{2,6},{4,0},{6,2},{8,12},{10,14},{12,8},{14,10},{16,20},{18,... | collective-permute-start | bytes 344072 | tf_op jit(solution)/shard_map/ppermute | solution.py:965
  184.7 6.9 %collective-permute-start.17 = (bf16[1,144,512]{2,1,0:T(8,128)(2,1)S(1)}, bf16[1,144,512]{2,1,0:T(8,128)(2,1)S(1)}, u32[]{:S(2)}, u32[]{:S(2)}) collective-permute-start(bf16[1,144,512]{2,1,0:T(8,128)(2,1)S(1)} %fusion.16), channel_id=1, source_target_pairs={{0,8},{2,10},{4,12},{6,14},{8,0},{10,2},{12,4},{14,6},{16,24},{18,... | collective-permute-start | bytes 442376 | tf_op jit(solution)/shard_map/ppermute | solution.py:965
  185.8 9.6 %collective-permute-start.23 = (bf16[1,160,512]{2,1,0:T(8,128)(2,1)S(1)}, bf16[1,160,512]{2,1,0:T(8,128)(2,1)S(1)}, u32[]{:S(2)}, u32[]{:S(2)}) collective-permute-start(bf16[1,160,512]{2,1,0:T(8,128)(2,1)S(1)} %add_convert_fusion.2), channel_id=1, source_target_pairs={{0,8},{2,10},{4,12},{6,14},{8,0},{10,2},{12,4},{14,6},{16,24},{18,... | collective-permute-start | bytes 491528 | tf_op jit(solution)/shard_map/ppermute | solution.py:965
  188.5 6.0 %collective-permute-start.24 = (bf16[1,144,512]{2,1,0:T(8,128)(2,1)S(1)}, bf16[1,144,512]{2,1,0:T(8,128)(2,1)S(1)}, u32[]{:S(2)}, u32[]{:S(2)}) collective-permute-start(bf16[1,144,512]{2,1,0:T(8,128)(2,1)S(1)} %get-tuple-element.163), channel_id=1, source_target_pairs={{0,4},{2,6},{4,0},{6,2},{8,12},{10,14},{12,8},{14,10},{16,20},{18,... | collective-permute-start | bytes 442376 | tf_op jit(solution)/shard_map/ppermute | solution.py:965
  190.7 9.6 %collective-permute-start.22 = (bf16[1,112,512]{2,1,0:T(8,128)(2,1)S(1)}, bf16[1,112,512]{2,1,0:T(8,128)(2,1)S(1)}, u32[]{:S(2)}, u32[]{:S(2)}) collective-permute-start(bf16[1,112,512]{2,1,0:T(8,128)(2,1)S(1)} %fusion.11), channel_id=1, source_target_pairs={{0,8},{2,10},{4,12},{6,14},{8,0},{10,2},{12,4},{14,6},{16,24},{18,... | collective-permute-start | bytes 344072 | tf_op jit(solution)/shard_map/ppermute | solution.py:965
  191.6 9.5 %collective-permute-start.21 = (bf16[1,144,512]{2,1,0:T(8,128)(2,1)S(1)}, bf16[1,144,512]{2,1,0:T(8,128)(2,1)S(1)}, u32[]{:S(2)}, u32[]{:S(2)}) collective-permute-start(bf16[1,144,512]{2,1,0:T(8,128)(2,1)S(1)} %fusion.8), channel_id=1, source_target_pairs={{0,16},{2,18},{4,20},{6,22},{8,24},{10,26},{12,28},{14,30},{16,0},... | collective-permute-start | bytes 442376 | tf_op jit(solution)/shard_map/ppermute | solution.py:965
  194.5 14.9 %collective-permute-start.28 = (bf16[2,144,512]{2,1,0:T(8,128)(2,1)S(1)}, bf16[2,144,512]{2,1,0:T(8,128)(2,1)S(1)}, u32[]{:S(2)}, u32[]{:S(2)}) collective-permute-start(bf16[2,144,512]{2,1,0:T(8,128)(2,1)S(1)} %pad_maximum_fusion.4), channel_id=1, source_target_pairs={{0,8},{2,10},{4,12},{6,14},{8,0},{10,2},{12,4},{14,6},{16,24},{18,... | collective-permute-start | bytes 884744 | tf_op jit(solution)/shard_map/ppermute | solution.py:965
  195.5 14.1 %collective-permute-start.27 = (bf16[2,160,512]{2,1,0:T(8,128)(2,1)S(1)}, bf16[2,160,512]{2,1,0:T(8,128)(2,1)S(1)}, u32[]{:S(2)}, u32[]{:S(2)}) collective-permute-start(bf16[2,160,512]{2,1,0:T(8,128)(2,1)S(1)} %pad_maximum_fusion.3), channel_id=1, source_target_pairs={{0,4},{2,6},{4,0},{6,2},{8,12},{10,14},{12,8},{14,10},{16,20},{18,... | collective-permute-start | bytes 983048 | tf_op jit(solution)/shard_map/ppermute | solution.py:965
  200.4 9.8 %collective-permute-start.26 = (bf16[1,112,512]{2,1,0:T(8,128)(2,1)S(1)}, bf16[1,112,512]{2,1,0:T(8,128)(2,1)S(1)}, u32[]{:S(2)}, u32[]{:S(2)}) collective-permute-start(bf16[1,112,512]{2,1,0:T(8,128)(2,1)S(1)} %fusion.15), channel_id=1, source_target_pairs={{0,16},{2,18},{4,20},{6,22},{8,24},{10,26},{12,28},{14,30},{16,0},... | collective-permute-start | bytes 344072 | tf_op jit(solution)/shard_map/ppermute | solution.py:965
  201.2 9.1 %collective-permute-start.25 = (bf16[1,144,512]{2,1,0:T(8,128)(2,1)S(1)}, bf16[1,144,512]{2,1,0:T(8,128)(2,1)S(1)}, u32[]{:S(2)}, u32[]{:S(2)}) collective-permute-start(bf16[1,144,512]{2,1,0:T(8,128)(2,1)S(1)} %add_convert_fusion.3), channel_id=1, source_target_pairs={{0,4},{2,6},{4,0},{6,2},{8,12},{10,14},{12,8},{14,10},{16,20},{18,... | collective-permute-start | bytes 442376 | tf_op jit(solution)/shard_map/ppermute | solution.py:965
  209.5 4.9 %collective-permute-start.32 = (bf16[4,144,512]{2,1,0:T(8,128)(2,1)S(1)}, bf16[4,144,512]{2,1,0:T(8,128)(2,1)S(1)}, u32[]{:S(2)}, u32[]{:S(2)}) collective-permute-start(bf16[4,144,512]{2,1,0:T(8,128)(2,1)S(1)} %pad_maximum_fusion.2.up_near), channel_id=1, source_target_pairs={{0,2},{2,0},{4,6},{6,4},{8,10},{10,8},{12,14},{14,12},{16,18},{18,... | collective-permute-start | bytes 1769480 | tf_op jit(solution)/shard_map/ppermute | solution.py:965
  209.6 4.7 %collective-permute-start.31 = (bf16[4,160,512]{2,1,0:T(8,128)(2,1)S(1)}, bf16[4,160,512]{2,1,0:T(8,128)(2,1)S(1)}, u32[]{:S(2)}, u32[]{:S(2)}) collective-permute-start(bf16[4,160,512]{2,1,0:T(8,128)(2,1)S(1)} %pad_maximum_fusion.dn_near), channel_id=1, source_target_pairs={{0,2},{2,0},{4,6},{6,4},{8,10},{10,8},{12,14},{14,12},{16,18},{18,... | collective-permute-start | bytes 1966088 | tf_op jit(solution)/shard_map/ppermute | solution.py:965
  210.3 2.7 %collective-permute-start.29 = (bf16[2,144,512]{2,1,0:T(8,128)(2,1)S(1)}, bf16[2,144,512]{2,1,0:T(8,128)(2,1)S(1)}, u32[]{:S(2)}, u32[]{:S(2)}) collective-permute-start(bf16[2,144,512]{2,1,0:T(8,128)(2,1)S(1)} %pad_maximum_fusion.5.refs_0_), channel_id=1, source_target_pairs={{0,2},{2,0},{4,6},{6,4},{8,10},{10,8},{12,14},{14,12},{16,18},{18,... | collective-permute-start | bytes 884744 | tf_op jit(solution)/shard_map/ppermute | solution.py:965
  211.0 2.0 collective-permute-start.30
where the time goes:
time: 217 us
  Pallas kernels  158 us (73%)
  starting transfers between devices  30.5 us (14%)
  waiting for transfers between devices  19.4 us (9%)
  local copies, waits for them, and re-layouts  5.42 us (2%)
  other arithmetic  2.19 us (1%)
    pallas_call x4, Pallas kernels, attn_bwd(): pl.pallas_call(partial(attn_bwd_kernel, head=head, cut=cut, extra=extra,...  59.2 us
    pallas_call x1, Pallas kernels, middle(): pl.pallas_call(partial(middle_kernel, n_others=n_others, chunk=min(1024,...  43.8 us
    pallas_call x2, Pallas kernels, attn_fwd(): pl.pallas_call(partial(attn_fwd_kernel, heads=heads, q_block=q_block, fet...  39.5 us
    ppermute x27, starting transfers between devices, swap_dp(): return lax.ppermute(value, 'dp', [(i, i ^ bits) for i in range(n_dp)])  23.3 us
    ppermute x27, waiting for transfers between devices, swap_dp(): return lax.ppermute(value, 'dp', [(i, i ^ bits) for i in range(n_dp)])  19.4 us
    pallas_call x1, Pallas kernels, input_gradient(): pl.pallas_call(partial(input_grad_kernel, n_others=n_shards - 1), grid_sp...  7.73 us
    ppermute x6, starting transfers between devices, shift_tensor(): lax.ppermute(value, 'tensor', [((i + by) % n_tensor, i) for i in range(n_...  7.26 us
    unnamed x20, local copies, waits for them, and re-layouts  4.63 us
  transfers between devices with their start and end apart: 33, of which 8 were waited for; matrix products, arithmetic and copies ran while one was open for 2% of the time, Pallas kernels for 51%

commit v1 on v0

--- a/solution.py
+++ b/solution.py
@@ -377,7 +377,7 @@
 
 
 def attn_fwd_kernel(pos_ref, x_ref, *refs, heads, q_block, fetched):
-    packed_ref, probs_ref, ctx_ref, key_ref, score_a, score_b = refs[-6:]
+    packed_ref, probs_ref, ctx_ref, mixed_ref, key_ref, score_a, score_b = refs[-7:]
     seq = x_ref.shape[0]
     scale = HEAD_DIM**-0.5
     wide = heads * HEAD_DIM
@@ -418,6 +418,7 @@
         probs_ref[0, 0, h, :, c : c + q_block] = probs
         mixed = mm(packed_ref[0, 0, base + 2 * HEAD_DIM : base + 3 * HEAD_DIM, :], probs)
         ctx_ref[0, 0, h * HEAD_DIM : (h + 1) * HEAD_DIM, c : c + q_block] = mixed.astype(bf16)
+        mixed_ref[0, 0, h * HEAD_DIM : (h + 1) * HEAD_DIM, c : c + q_block] = mixed
 
     score(tiles[0], scores[0])
     for j, tile in enumerate(tiles):
@@ -442,8 +443,7 @@
     out_specs = [
         pl.BlockSpec((1, 1, part, SEQ_LEN), lambda s, k, pos: (shard, s, at(k, pos), 0)),
         pl.BlockSpec((1, 1, heads, SEQ_LEN, SEQ_LEN), lambda s, k, pos: (shard, s, at(k, pos), 0, 0)),
-        pl.BlockSpec((1, 1, heads * HEAD_DIM, SEQ_LEN), lambda s, k, pos: (shard, s, at(k, pos), 0)),
-    ]
+    ] + [pl.BlockSpec((1, 1, heads * HEAD_DIM, SEQ_LEN), lambda s, k, pos: (shard, s, at(k, pos), 0))] * 2
     q_block = 512
     share = 2 * n_seq * heads
     flops = share * (2 * SEQ_LEN * width * PART_ROWS + 4 * SEQ_LEN * SEQ_LEN * HEAD_DIM * 6)
@@ -463,7 +463,7 @@
             ],
         ),
         out_shape=shapes,
-        input_output_aliases={4: 0, 5: 1, 6: 2} if earlier else {},
+        input_output_aliases={4 + k: k for k in range(len(earlier))},
         compiler_params=kernel_params(),
         cost_estimate=cost(flops // 8 if fetched else flops, share * 3 << 20),
         name="attn_fwd",
@@ -710,60 +710,32 @@
     packed_ref,
     probs_ref,
     ctx_low_ref,
+    mixed_ref,
     sums_ref,
     *refs,
     head,
     cut,
     extra,
-    q_block,
     unroll,
 ):
-    grad_ref, keep_ref, send_ref, bias_ref, *refs = refs[-10:]
-    value_ref, key_acc, value_acc, weight_acc, grad_a, grad_b = refs
+    grad_ref, keep_ref, send_ref, bias_ref, value_ref, weight_acc = refs[-6:]
     step = pl.program_id(0)
     seq = x_ref.shape[0]
     n_shards = packed_ref.shape[0]
     scale = HEAD_DIM**-0.5
     for t in range(n_shards):
         value_ref[t] = packed_ref[t, 0, 2 * HEAD_DIM : 3 * HEAD_DIM, :].T
-    tiles = list(range(0, seq, q_block))
-    buffers = (grad_a, grad_b)
-
-    def start(t, c, ref):
-        ref[...] = mm(value_ref[t], ctx_low_ref[t, 0, :, c : c + q_block])
-
-    def finish(t, c, ref):
-        cols = slice(c, c + q_block)
-        probs_low = probs_ref[t, 0, 0, :, cols]
-        probs = probs_low.astype(f32)
-        weighted = probs * ref[...]
-        total = jnp.sum(weighted, axis=0, keepdims=True)
-        score_low = (weighted - probs * total).astype(bf16)
+    def one_shard(t, carry):
+        ctx_low = ctx_low_ref[t, 0]
+        total = jnp.sum(ctx_low.astype(f32) * mixed_ref[t, 0], axis=0, keepdims=True)
+        probs = probs_ref[t, 0, 0]
+        score_low = (probs.astype(f32) * (mm(value_ref[t], ctx_low) - total)).astype(bf16)
         grad_query = mm(packed_ref[t, 0, HEAD_DIM : 2 * HEAD_DIM, :], score_low) * scale
-        grad_ref[t, 0, :HEAD_DIM, cols] = grad_query.astype(bf16)
-        grad_key = mm_nt(packed_ref[t, 0, :HEAD_DIM, cols], score_low)
-        grad_value = mm_nt(ctx_low_ref[t, 0, :, cols], probs_low)
-        if c > 0:
-            grad_key = key_acc[...] + grad_key
-            grad_value = value_acc[...] + grad_value
-        if c + q_block < seq:
-            key_acc[...] = grad_key
-            value_acc[...] = grad_value
-        else:
-            grad_ref[t, 0, HEAD_DIM : 2 * HEAD_DIM, :] = (grad_key * scale).astype(bf16)
-            grad_ref[t, 0, 2 * HEAD_DIM :, :] = grad_value.astype(bf16)
-
-    start(0, 0, buffers[0])
-
-    def one_shard(t, carry):
-        for j, c in enumerate(tiles):
-            if j + 1 < len(tiles):
-                start(t, tiles[j + 1], buffers[(j + 1) % 2])
-            elif not unroll:
-                start(jnp.minimum(t + 1, n_shards - 1), 0, buffers[(j + 1) % 2])
-            elif t + 1 < n_shards:
-                start(t + 1, 0, buffers[(j + 1) % 2])
-            finish(t, c, buffers[j % 2])
+        grad_key = mm_nt(score_low, packed_ref[t, 0, :HEAD_DIM, :]) * scale
+        grad_value = mm_nt(probs, ctx_low)
+        grad_ref[t, 0, :HEAD_DIM, :] = grad_query.astype(bf16)
+        grad_ref[t, 0, HEAD_DIM : 2 * HEAD_DIM, :] = grad_key.T.astype(bf16)
+        grad_ref[t, 0, 2 * HEAD_DIM :, :] = grad_value.T.astype(bf16)
         return carry
 
     if unroll:
@@ -799,17 +771,16 @@
                     ref[t, slot % half, rows:] = padded.astype(bf16)
 
 
-def attn_bwd(pos, x, packed, probs, ctx_low, sums, head, first, group, cut, extra, unroll, earlier):
+def attn_bwd(pos, x, packed, probs, ctx_low, mixed, sums, head, first, group, cut, extra, unroll, earlier):
     rows, width = x.shape
     n_shards, n_seq = packed.shape[:2]
-    q_block = 256
     slots = 1 << len(cut)
     each = PART_ROWS // slots + (EXTRA if extra else 0)
     pieces = (n_shards, slots // 2, group * each, width)
     piece = pl.BlockSpec((n_shards, slots // 2, each, width), lambda s, pos: (0, 0, head - first, 0))
     sum_spec = pl.BlockSpec(sums.shape, lambda s, pos: (0, 0, 0))
     return pl.pallas_call(
-        partial(attn_bwd_kernel, head=head, cut=cut, extra=extra, q_block=q_block, unroll=unroll),
+        partial(attn_bwd_kernel, head=head, cut=cut, extra=extra, unroll=unroll),
         grid_spec=pltpu.PrefetchScalarGridSpec(
             num_scalar_prefetch=1,
             grid=(n_seq,),
@@ -817,6 +788,7 @@
                 pl.BlockSpec((SEQ_LEN, width), lambda s, pos: (s, 0)),
                 pl.BlockSpec((n_shards, 1, PART_ROWS, SEQ_LEN), lambda s, pos: (0, s, head, 0)),
                 pl.BlockSpec((n_shards, 1, 1, SEQ_LEN, SEQ_LEN), lambda s, pos: (0, s, head, 0, 0)),
+                pl.BlockSpec((n_shards, 1, HEAD_DIM, SEQ_LEN), lambda s, pos: (0, s, head, 0)),
                 pl.BlockSpec((n_shards, 1, HEAD_DIM, SEQ_LEN), lambda s, pos: (0, s, head, 0)),
                 sum_spec,
             ]
@@ -829,11 +801,7 @@
             ],
             scratch_shapes=[
                 pltpu.VMEM((n_shards, SEQ_LEN, HEAD_DIM), bf16),
-                pltpu.VMEM((HEAD_DIM, SEQ_LEN), f32),
-                pltpu.VMEM((HEAD_DIM, SEQ_LEN), f32),
                 pltpu.VMEM((n_shards, PART_ROWS, width), f32),
-                pltpu.VMEM((SEQ_LEN, q_block), f32),
-                pltpu.VMEM((SEQ_LEN, q_block), f32),
             ],
         ),
         out_shape=[
@@ -842,11 +810,11 @@
             jax.ShapeDtypeStruct(pieces, bf16),
             jax.ShapeDtypeStruct(sums.shape, f32),
         ],
-        input_output_aliases={6: 1, 7: 2} if earlier else {},
+        input_output_aliases={7: 1, 8: 2} if earlier else {},
         compiler_params=kernel_params(48_000_000),
         cost_estimate=cost(8 << 30, 10 << 20),
         name="attn_bwd",
-    )(pos, x, packed, probs, ctx_low, sums, *earlier)
+    )(pos, x, packed, probs, ctx_low, mixed, sums, *earlier)
 
 
 def input_grad_kernel(pos_ref, grad_one_ref, own_ref, *refs, n_others):
@@ -1067,6 +1035,7 @@
         jax.ShapeDtypeStruct((n_tensor, n_seq, n_heads * PART_ROWS, SEQ_LEN), bf16),
         jax.ShapeDtypeStruct((n_tensor, n_seq, n_heads, SEQ_LEN, SEQ_LEN), bf16),
         jax.ShapeDtypeStruct((n_tensor, n_seq, n_heads * HEAD_DIM, SEQ_LEN), bf16),
+        jax.ShapeDtypeStruct((n_tensor, n_seq, n_heads * HEAD_DIM, SEQ_LEN), f32),
     ]
     mlp_near = [shift_tensor(mlp_half, by, n_tensor) for by in shifts]
     x = after(layer_input, mlp_half)
@@ -1075,7 +1044,7 @@
     qkv_far = [swap_dp(near, 1, n_dp) for near in qkv_near]
     for t in shifts:
         stacks = attn_fwd(pos, layer_input, (qkv_near[t - 1], qkv_far[t - 1]), t, True, shapes, stacks)
-    packed, probs, ctx = stacks
+    packed, probs, ctx, mixed = stacks
     mlp_near = after(mlp_near, ctx)
     mlp_far = [swap_dp(near, 1, n_dp) for near in mlp_near]
     fetched = [half for pair in zip(mlp_near, mlp_far) for half in pair]
@@ -1103,6 +1072,7 @@
             packed,
             probs,
             ctx_low,
+            mixed,
             bias_sums,
             head,
             early if last else 0,

time: 217 us -> 215 us (level)
  Pallas kernels: 158 us -> 155 us
    pallas_call x4, Pallas kernels: 59.2 us -> 55.4 us  [attn_bwd(): pl.pallas_call(partial(attn_bwd_kernel, head=head, cut=cut, extra=extra,...]
  transfers between devices with their start and end apart: 33 -> 33, of which waited for: 8 -> 9; matrix products, arithmetic and copies ran while one was open for 2% -> 2% of each run, Pallas kernels for 51% -> 50%
where the time goes in v1:
time: 215 us; the launch traced here: 214 us
  Pallas kernels  155 us (72%)
  starting transfers between devices  30.7 us (14%)
  waiting for transfers between devices  20.2 us (9%)
  local copies, waits for them, and re-layouts  5.38 us (3%)
  other arithmetic  2.15 us (1%)
    pallas_call x4, Pallas kernels, attn_bwd(): pl.pallas_call(partial(attn_bwd_kernel, head=head, cut=cut, extra=extra,...  55.4 us
    pallas_call x1, Pallas kernels, middle(): pl.pallas_call(partial(middle_kernel, n_others=n_others, chunk=min(1024,...  43.8 us
    pallas_call x2, Pallas kernels, attn_fwd(): pl.pallas_call(partial(attn_fwd_kernel, heads=heads, q_block=q_block, fet...  39.9 us
    ppermute x27, starting transfers between devices, swap_dp(): return lax.ppermute(value, 'dp', [(i, i ^ bits) for i in range(n_dp)])  23.5 us
    ppermute x27, waiting for transfers between devices, swap_dp(): return lax.ppermute(value, 'dp', [(i, i ^ bits) for i in range(n_dp)])  19.6 us
    pallas_call x1, Pallas kernels, input_gradient(): pl.pallas_call(partial(input_grad_kernel, n_others=n_shards - 1), grid_sp...  7.69 us
    ppermute x6, starting transfers between devices, shift_tensor(): lax.ppermute(value, 'tensor', [((i + by) % n_tensor, i) for i in range(n_...  7.25 us
    unnamed x20, local copies, waits for them, and re-layouts  4.59 us
  transfers between devices with their start and end apart: 33, of which 9 were waited for; matrix products, arithmetic and copies ran while one was open for 2% of the time, Pallas kernels for 50%

profile of v1, /device:TPU:0, one launch (start us, length us, event | category | flops | bytes accessed | tf_op | source)
XLA Modules:
  0.0 214.3 jit_solution(10335025286635733791)
XLA Ops:
  0.7 1.8 pack_qkv.1
  2.5 2.9 %collective-permute-start = (bf16[400,512]{1,0:T(8,128)(2,1)}, bf16[400,512]{1,0:T(8,128)(2,1)S(1)}, u32[]{:S(2)}, u32[]{:S(2)}) collective-permute-start(bf16[400,512]{1,0:T(8,128)(2,1)} %get-tuple-element.90), channel_id=1, source_target_pairs={{1,0},{0,1},{3,2},{2,3},{5,4},{4,5},{7,6},{6,7},{9,8},{8,9},{11,10... | collective-permute-start | bytes 1228808 | tf_op jit(solution)/shard_map/ppermute | solution.py:937
  5.4 2.4 %pack_mlp.1 = (bf16[1168,512]{1,0:T(8,128)(2,1)}, f32[16,512]{1,0:T(8,128)}) custom-call(s32[1]{0:T(128)} %bitcast.pos_ref, bf16[256,512]{1,0:T(8,128)(2,1)} %proj_own.1, bf16[1024,512]{1,0:T(8,128)(2,1)} %down_own.1, bf16[512,1024]{1,0:T(8,128)(2,1)} %up_own.1, bf16[1024]{0:T(1024)(128)(2,1)} %up_b_ref.1, bf16[512]{0:T(512)(128)(2,1)} %refs_0_.2, ...), custom_call_target="tpu_custom_call" | custom-call | bytes 3145728 | tf_op jit(solution)/shard_map/pack_mlp/pallas_call | solution.py:361
  7.8 19.9 %attn_fwd.2 = (bf16[2,2,768,1024]{3,2,1,0:T(8,128)(2,1)}, bf16[2,2,4,1024,1024]{4,3,2,1,0:T(8,128)(2,1)}, bf16[2,2,256,1024]{3,2,1,0:T(8,128)(2,1)}, f32[2,2,256,1024]{3,2,1,0:T(8,128)}) custom-call(s32[1]{0:T(128)} %bitcast.pos_ref, bf16[2048,512]{1,0:T(8,128)(2,1)} %x_ref.8, bf16[768,512]{1,0:T(8,128)(2,1)} %own_ref.1, ...), custom_call_target="tpu_custom_call" | custom-call | flops 14495514624 | bytes 25165824 | tf_op jit(solution)/shard_map/attn_fwd/pallas_call | solution.py:450
  27.7 0.1 collective-permute-start.1
  27.8 1.7 collective-permute-done.1.refs_1_
  29.6 0.8 copy-done.5
  30.3 20.0 %attn_fwd.3 = (bf16[2,2,768,1024]{3,2,1,0:T(8,128)(2,1)}, bf16[2,2,4,1024,1024]{4,3,2,1,0:T(8,128)(2,1)}, bf16[2,2,256,1024]{3,2,1,0:T(8,128)(2,1)}, f32[2,2,256,1024]{3,2,1,0:T(8,128)}) custom-call(s32[1]{0:T(128)} %bitcast.pos_ref, bf16[2048,512]{1,0:T(8,128)(2,1)} %x_ref.8, ...), custom_call_target="tpu_custom_call", output_to_operand_aliasing={{0}: (4, {}), {1}: (5, {}), {2}: (6, {}), {3}: (7, {})} | custom-call | flops 1811939328 | bytes 25165824 | tf_op jit(solution)/shard_map/attn_fwd/pallas_call | solution.py:450
  50.3 0.2 collective-permute-start.3
  50.6 3.1 %collective-permute-done.3.refs_1_ = bf16[1168,512]{1,0:T(8,128)(2,1)} collective-permute-done((bf16[1168,512]{1,0:T(8,128)(2,1)}, bf16[1168,512]{1,0:T(8,128)(2,1)}, u32[]{:S(2)}, u32[]{:S(2)}) %collective-permute-start.3) | collective-permute-done | bytes 1196064 | tf_op jit(solution)/shard_map/ppermute | solution.py:933
  53.6 43.8 %middle.1 = (bf16[2048,512]{1,0:T(8,128)(2,1)}, f32[2048,512]{1,0:T(8,128)}, bf16[2,2,256,1024]{3,2,1,0:T(8,128)(2,1)}, bf16[2,4,160,512]{3,2,1,0:T(8,128)(2,1)}...) custom-call(s32[1]{0:T(128)} %bitcast.pos_ref, ...), custom_call_target="tpu_custom_call" | custom-call | flops 32212254720 | bytes 31457280 | tf_op jit(solution)/shard_map/middle/pallas_call | solution.py:662
  97.4 0.2 collective-permute-start.6
  97.7 0.3 collective-permute-start.4
  98.0 1.6 copy-done
  99.6 1.6 copy-done.1
  101.2 13.9 %attn_bwd.4 = (bf16[2,2,192,1024]{3,2,1,0:T(8,128)(2,1)S(1)}, bf16[2,2,144,512]{3,2,1,0:T(8,128)(2,1)S(1)}, bf16[2,2,144,512]{3,2,1,0:T(8,128)(2,1)S(1)}, f32[2,16,192]{2,1,0:T(8,128)S(1)}) custom-call(s32[1]{0:T(128)} %bitcast.pos_ref, bf16[2048,512]{1,0:T(8,128)(2,1)S(1)} %copy-done, bf16[2,2,768,1024]{3,2,1,0:T(8,128)(2,1)} %get-tuple-element.109.packed_ref, ...), custom_call_target="tpu_custom_call" | custom-call | flops 8589934592 | bytes 10485760 | tf_op jit(solution)/shard_map/attn_bwd/pallas_call | solution.py:782
  115.1 0.4 convert_add_fusion.1
  115.7 2.2 %collective-permute-start.7 = (bf16[2,2,144,512]{3,2,1,0:T(8,128)(2,1)S(1)}, bf16[2,2,144,512]{3,2,1,0:T(8,128)(2,1)S(1)}, u32[]{:S(2)}, u32[]{:S(2)}) collective-permute-start(bf16[2,2,144,512]{3,2,1,0:T(8,128)(2,1)S(1)} %pad_maximum_fusion.1), channel_id=1, source_target_pairs={{0,8},{2,10},{4,12},{6,14},{8,0},{10,2},{12,4},{14,6},{16,24},{18,... | collective-permute-start | bytes 1769480 | tf_op jit(solution)/shard_map/ppermute | solution.py:933
  117.8 0.2 fusion
  118.0 1.6 collective-permute-start.5
  119.6 13.7 %attn_bwd.5 = (bf16[2,2,192,1024]{3,2,1,0:T(8,128)(2,1)S(1)}, bf16[2,2,144,512]{3,2,1,0:T(8,128)(2,1)S(1)}, bf16[2,2,144,512]{3,2,1,0:T(8,128)(2,1)S(1)}, f32[2,16,192]{2,1,0:T(8,128)S(1)}) custom-call(s32[1]{0:T(128)} %bitcast.pos_ref, bf16[2048,512]{1,0:T(8,128)(2,1)S(1)} %copy-done, ...), custom_call_target="tpu_custom_call", output_to_operand_aliasing={{1}: (7, {}), {2}: (8, {})} | custom-call | flops 8589934592 | bytes 10485760 | tf_op jit(solution)/shard_map/attn_bwd/pallas_call | solution.py:782
  133.3 0.1 fusion.6
  133.4 0.6 collective-permute-start.9
  134.0 0.6 collective-permute-done.5
  134.6 0.3 bitcast_add_fusion
  134.9 1.6 collective-permute-start.8
  136.5 13.6 %attn_bwd.6 = (bf16[2,2,192,1024]{3,2,1,0:T(8,128)(2,1)S(1)}, bf16[2,2,144,512]{3,2,1,0:T(8,128)(2,1)S(1)}, bf16[2,2,144,512]{3,2,1,0:T(8,128)(2,1)S(1)}, f32[2,16,192]{2,1,0:T(8,128)S(1)}) custom-call(s32[1]{0:T(128)} %bitcast.pos_ref, bf16[2048,512]{1,0:T(8,128)(2,1)S(1)} %copy-done, ...), custom_call_target="tpu_custom_call", output_to_operand_aliasing={{1}: (7, {}), {2}: (8, {})} | custom-call | flops 8589934592 | bytes 10485760 | tf_op jit(solution)/shard_map/attn_bwd/pallas_call | solution.py:782
  150.2 0.1 fusion.2
  150.4 0.6 collective-permute-start.13
  151.0 0.1 slice_add_fusion
  151.1 1.4 collective-permute-start.12
  152.5 0.1 fusion.5
  152.6 1.6 collective-permute-start.11
  154.2 14.2 %attn_bwd.7 = (bf16[2,2,192,1024]{3,2,1,0:T(8,128)(2,1)S(1)}, bf16[2,1,112,512]{3,2,1,0:T(8,128)(2,1)S(1)}, bf16[2,1,112,512]{3,2,1,0:T(8,128)(2,1)S(1)}, f32[2,16,192]{2,1,0:T(8,128)}) custom-call(s32[1]{0:T(128)} %bitcast.pos_ref, bf16[2048,512]{1,0:T(8,128)(2,1)S(1)} %copy-done, bf16[2,2,768,1024]{3,2,1,0:T(8,128)(2,1)} %get-tuple-element.109.packed_ref, ...), custom_call_target="tpu_custom_call" | custom-call | flops 8589934592 | bytes 10485760 | tf_op jit(solution)/shard_map/attn_bwd/pallas_call | solution.py:782
  168.5 2.6 %collective-permute-start.20 = (bf16[1,160,512]{2,1,0:T(8,128)(2,1)S(1)}, bf16[1,160,512]{2,1,0:T(8,128)(2,1)S(1)}, u32[]{:S(2)}, u32[]{:S(2)}) collective-permute-start(bf16[1,160,512]{2,1,0:T(8,128)(2,1)S(1)} %fusion.7), channel_id=1, source_target_pairs={{0,16},{2,18},{4,20},{6,22},{8,24},{10,26},{12,28},{14,30},{16,0},... | collective-permute-start | bytes 491528 | tf_op jit(solution)/shard_map/ppermute | solution.py:933
  171.1 0.3 collective-permute-start.19
  171.5 0.6 collective-permute-start.16
  172.1 0.1 bitcast_add_fusion.1
  172.2 1.6 collective-permute-start.15
  173.8 7.7 %input_gradient.1 = bf16[2048,512]{1,0:T(8,128)(2,1)} custom-call(s32[1]{0:T(128)} %bitcast.pos_ref, f32[2048,512]{1,0:T(8,128)} %get-tuple-element.140.grad_one_ref, bf16[768,512]{1,0:T(8,128)(2,1)S(1)} %copy-done.2, bf16[400,512]{1,0:T(8,128)(2,1)S(1)} %copy-done.4, bf16[400,512]{1,0:T(8,128)(2,1)S(1)} %copy-done.6, ...), custom_call_target="tpu_custom_call" | custom-call | flops 4294967296 | bytes 12582912 | tf_op jit(solution)/shard_map/input_gradient/pallas_call | solution.py:851
  181.5 0.6 collective-permute-start.18
  182.2 1.1 collective-permute-start.17
  183.3 1.1 collective-permute-start.23
  184.4 1.6 collective-permute-done.19
  186.0 1.6 collective-permute-start.24
  187.6 0.6 fusion.20
  188.3 0.8 collective-permute-done.17
  189.2 2.5 %collective-permute-start.21 = (bf16[1,144,512]{2,1,0:T(8,128)(2,1)S(1)}, bf16[1,144,512]{2,1,0:T(8,128)(2,1)S(1)}, u32[]{:S(2)}, u32[]{:S(2)}) collective-permute-start(bf16[1,144,512]{2,1,0:T(8,128)(2,1)S(1)} %fusion.8), channel_id=1, source_target_pairs={{0,16},{2,18},{4,20},{6,22},{8,24},{10,26},{12,28},{14,30},{16,0},... | collective-permute-start | bytes 442376 | tf_op jit(solution)/shard_map/ppermute | solution.py:933
  191.7 1.2 collective-permute-start.28
  193.0 1.2 collective-permute-start.27
  194.2 3.8 %collective-permute-done.22 = bf16[1,112,512]{2,1,0:T(8,128)(2,1)S(1)} collective-permute-done((bf16[1,112,512]{2,1,0:T(8,128)(2,1)S(1)}, bf16[1,112,512]{2,1,0:T(8,128)(2,1)S(1)}, u32[]{:S(2)}, u32[]{:S(2)}) %collective-permute-start.22) | collective-permute-done | bytes 114720 | tf_op jit(solution)/shard_map/ppermute | solution.py:933
  198.0 0.1 fusion.15
  198.2 0.2 collective-permute-done.21
  198.5 1.6 collective-permute-start.25
  200.0 6.9 %collective-permute-done.28 = bf16[2,144,512]{2,1,0:T(8,128)(2,1)S(1)} collective-permute-done((bf16[2,144,512]{2,1,0:T(8,128)(2,1)S(1)}, bf16[2,144,512]{2,1,0:T(8,128)(2,1)S(1)}, u32[]{:S(2)}, u32[]{:S(2)}) %collective-permute-start.28) | collective-permute-done | bytes 294944 | tf_op jit(solution)/shard_map/ppermute | solution.py:933
  207.0 0.1 collective-permute-start.32
  207.1 0.5 collective-permute-start.31
  207.7 0.1 fusion.18
  207.8 0.1 collective-permute-start.29
  207.9 0.6 copy.38
  208.5 0.5 collective-permute-start.30
  209.0 1.6 collective-permute-done.30.refs_3_
  210.6 1.3 qkv_place.1
  211.8 2.5 %mlp_place.1 = (f32[256,512]{1,0:T(8,128)}, f32[512,1024]{1,0:T(8,128)}, f32[1024,512]{1,0:T(8,128)}) custom-call(s32[1]{0:T(128)} %bitcast.pos_ref, bf16[4,160,512]{2,1,0:T(8,128)(2,1)S(1)} %pad_maximum_fusion.dn_near, bf16[4,160,512]{2,1,0:T(8,128)(2,1)S(1)} %collective-permute-done.31.dn_far, bf16[4,144,512]{2,1,0:T(8,128)(2,1)S(1)} %pad_maximum_fusion.2.up_near, ...), custom_call_target="tpu_custom_call" | custom-call | bytes 14680064 | tf_op jit(solution)/shard_map/mlp_place/pallas_call | solution.py:886
  (69 shorter events, 1.2 us)
Async XLA Ops:
  2.5 25.3 %collective-permute-start = (bf16[400,512]{1,0:T(8,128)(2,1)}, bf16[400,512]{1,0:T(8,128)(2,1)S(1)}, u32[]{:S(2)}, u32[]{:S(2)}) collective-permute-start(bf16[400,512]{1,0:T(8,128)(2,1)} %get-tuple-element.90), channel_id=1, source_target_pairs={{1,0},{0,1},{3,2},{2,3},{5,4},{4,5},{7,6},{6,7},{9,8},{8,9},{11,10... | collective-permute-start | bytes 1228808 | tf_op jit(solution)/shard_map/ppermute | solution.py:937
  7.8 42.5 %collective-permute-start.2 = (bf16[1168,512]{1,0:T(8,128)(2,1)}, bf16[1168,512]{1,0:T(8,128)(2,1)}, u32[]{:S(2)}, u32[]{:S(2)}) collective-permute-start(bf16[1168,512]{1,0:T(8,128)(2,1)} %get-tuple-element.92), channel_id=1, source_target_pairs={{1,0},{0,1},{3,2},{2,3},{5,4},{4,5},{7,6},{6,7},{9,8},{8,9},{11,10... | collective-permute-start | bytes 3588104 | tf_op jit(solution)/shard_map/ppermute | solution.py:937
  27.7 1.8 copy-start.3
  27.7 1.8 collective-permute-start.1
  29.6 0.8 copy-start.5
  50.3 3.3 %collective-permute-start.3 = (bf16[1168,512]{1,0:T(8,128)(2,1)}, bf16[1168,512]{1,0:T(8,128)(2,1)}, u32[]{:S(2)}, u32[]{:S(2)}) collective-permute-start(bf16[1168,512]{1,0:T(8,128)(2,1)} %collective-permute-done.2.refs_0_), channel_id=1, source_target_pairs={{0,2},{2,0},{4,6},{6,4},{8,10},{10,8},{12,14},{14,12},{16,18},{18,... | collective-permute-start | bytes 3588104 | tf_op jit(solution)/shard_map/ppermute | solution.py:933
  97.4 17.7 %collective-permute-start.6 = (bf16[2,4,144,512]{3,2,1,0:T(8,128)(2,1)}, bf16[2,4,144,512]{3,2,1,0:T(8,128)(2,1)S(1)}, u32[]{:S(2)}, u32[]{:S(2)}) collective-permute-start(bf16[2,4,144,512]{3,2,1,0:T(8,128)(2,1)} %get-tuple-element.107), channel_id=1, source_target_pairs={{0,2},{2,0},{4,6},{6,4},{8,10},{10,8},{12,14},{14,12},{16,18},{18,... | collective-permute-start | bytes 3538952 | tf_op jit(solution)/shard_map/ppermute | solution.py:933
  97.7 20.2 %collective-permute-start.4 = (bf16[2,4,160,512]{3,2,1,0:T(8,128)(2,1)}, bf16[2,4,160,512]{3,2,1,0:T(8,128)(2,1)S(1)}, u32[]{:S(2)}, u32[]{:S(2)}) collective-permute-start(bf16[2,4,160,512]{3,2,1,0:T(8,128)(2,1)} %get-tuple-element.106), channel_id=1, source_target_pairs={{0,2},{2,0},{4,6},{6,4},{8,10},{10,8},{12,14},{14,12},{16,18},{18,... | collective-permute-start | bytes 3932168 | tf_op jit(solution)/shard_map/ppermute | solution.py:933
  98.0 1.6 copy-start
  99.6 1.6 copy-start.1
  101.2 13.9 %copy-start.8 = (bf16[2,4,144,512]{3,2,1,0:T(8,128)(2,1)S(1)}, bf16[2,4,144,512]{3,2,1,0:T(8,128)(2,1)}, u32[]{:S(2)}) copy-start(bf16[2,4,144,512]{3,2,1,0:T(8,128)(2,1)} %get-tuple-element.115) | copy-start | bytes 3538948
  115.5 2.3 %copy-start.7 = (bf16[2,4,160,512]{3,2,1,0:T(8,128)(2,1)S(1)}, bf16[2,4,160,512]{3,2,1,0:T(8,128)(2,1)}, u32[]{:S(2)}) copy-start(bf16[2,4,160,512]{3,2,1,0:T(8,128)(2,1)} %get-tuple-element.105) | copy-start | bytes 3932164
  115.7 17.6 %collective-permute-start.7 = (bf16[2,2,144,512]{3,2,1,0:T(8,128)(2,1)S(1)}, bf16[2,2,144,512]{3,2,1,0:T(8,128)(2,1)S(1)}, u32[]{:S(2)}, u32[]{:S(2)}) collective-permute-start(bf16[2,2,144,512]{3,2,1,0:T(8,128)(2,1)S(1)} %pad_maximum_fusion.1), channel_id=1, source_target_pairs={{0,8},{2,10},{4,12},{6,14},{8,0},{10,2},{12,4},{14,6},{16,24},{18,... | collective-permute-start | bytes 1769480 | tf_op jit(solution)/shard_map/ppermute | solution.py:933
  118.0 16.6 %collective-permute-start.5 = (bf16[4,160,512]{2,1,0:T(8,128)(2,1)S(1)}, bf16[4,160,512]{2,1,0:T(8,128)(2,1)S(1)}, u32[]{:S(2)}, u32[]{:S(2)}) collective-permute-start(bf16[4,160,512]{2,1,0:T(8,128)(2,1)S(1)} %fusion), channel_id=1, source_target_pairs={{1,0},{0,1},{3,2},{2,3},{5,4},{4,5},{7,6},{6,7},{9,8},{8,9},{11,10... | collective-permute-start | bytes 1966088 | tf_op jit(solution)/shard_map/ppermute | solution.py:937
  133.4 16.8 %collective-permute-start.9 = (bf16[2,144,512]{2,1,0:T(8,128)(2,1)S(1)}, bf16[2,144,512]{2,1,0:T(8,128)(2,1)S(1)}, u32[]{:S(2)}, u32[]{:S(2)}) collective-permute-start(bf16[2,144,512]{2,1,0:T(8,128)(2,1)S(1)} %fusion.6), channel_id=1, source_target_pairs={{1,0},{0,1},{3,2},{2,3},{5,4},{4,5},{7,6},{6,7},{9,8},{8,9},{11,10... | collective-permute-start | bytes 884744 | tf_op jit(solution)/shard_map/ppermute | solution.py:937
  134.9 16.0 %collective-permute-start.8 = (bf16[1,2,160,512]{3,2,1,0:T(8,128)(2,1)S(1)}, bf16[1,2,160,512]{3,2,1,0:T(8,128)(2,1)S(1)}, u32[]{:S(2)}, u32[]{:S(2)}) collective-permute-start(bf16[1,2,160,512]{3,2,1,0:T(8,128)(2,1)S(1)} %fusion.4), channel_id=1, source_target_pairs={{0,4},{2,6},{4,0},{6,2},{8,12},{10,14},{12,8},{14,10},{16,20},{18,... | collective-permute-start | bytes 983048 | tf_op jit(solution)/shard_map/ppermute | solution.py:933
  150.1 2.4 %collective-permute-start.10 = (bf16[2,2,144,512]{3,2,1,0:T(8,128)(2,1)S(1)}, bf16[2,2,144,512]{3,2,1,0:T(8,128)(2,1)S(1)}, u32[]{:S(2)}, u32[]{:S(2)}) collective-permute-start(bf16[2,2,144,512]{3,2,1,0:T(8,128)(2,1)S(1)} %get-tuple-element.126), channel_id=1, source_target_pairs={{0,2},{2,0},{4,6},{6,4},{8,10},{10,8},{12,14},{14,12},{16,18},{18,... | collective-permute-start | bytes 1769480 | tf_op jit(solution)/shard_map/ppermute | solution.py:933
  150.4 17.9 %collective-permute-start.13 = (bf16[1,1,144,512]{3,2,1,0:T(8,128)(2,1)S(1)}, bf16[1,1,144,512]{3,2,1,0:T(8,128)(2,1)S(1)}, u32[]{:S(2)}, u32[]{:S(2)}) collective-permute-start(bf16[1,1,144,512]{3,2,1,0:T(8,128)(2,1)S(1)} %fusion.12), channel_id=1, source_target_pairs={{0,4},{2,6},{4,0},{6,2},{8,12},{10,14},{12,8},{14,10},{16,20},{18,... | collective-permute-start | bytes 442376 | tf_op jit(solution)/shard_map/ppermute | solution.py:933
  151.1 17.2 %collective-permute-start.12 = (bf16[1,1,160,512]{3,2,1,0:T(8,128)(2,1)S(1)}, bf16[1,1,160,512]{3,2,1,0:T(8,128)(2,1)S(1)}, u32[]{:S(2)}, u32[]{:S(2)}) collective-permute-start(bf16[1,1,160,512]{3,2,1,0:T(8,128)(2,1)S(1)} %fusion.10), channel_id=1, source_target_pairs={{0,8},{2,10},{4,12},{6,14},{8,0},{10,2},{12,4},{14,6},{16,24},{18,... | collective-permute-start | bytes 491528 | tf_op jit(solution)/shard_map/ppermute | solution.py:933
  152.6 19.5 %collective-permute-start.11 = (bf16[2,144,512]{2,1,0:T(8,128)(2,1)S(1)}, bf16[2,144,512]{2,1,0:T(8,128)(2,1)S(1)}, u32[]{:S(2)}, u32[]{:S(2)}) collective-permute-start(bf16[2,144,512]{2,1,0:T(8,128)(2,1)S(1)} %fusion.5), channel_id=1, source_target_pairs={{1,0},{0,1},{3,2},{2,3},{5,4},{4,5},{7,6},{6,7},{9,8},{8,9},{11,10... | collective-permute-start | bytes 884744 | tf_op jit(solution)/shard_map/ppermute | solution.py:937
  168.3 3.1 %collective-permute-start.14 = (bf16[2,1,112,512]{3,2,1,0:T(8,128)(2,1)S(1)}, bf16[2,1,112,512]{3,2,1,0:T(8,128)(2,1)S(1)}, u32[]{:S(2)}, u32[]{:S(2)}) collective-permute-start(bf16[2,1,112,512]{3,2,1,0:T(8,128)(2,1)S(1)} %get-tuple-element.133), channel_id=1, source_target_pairs={{0,2},{2,0},{4,6},{6,4},{8,10},{10,8},{12,14},{14,12},{16,18},{18,... | collective-permute-start | bytes 688136 | tf_op jit(solution)/shard_map/ppermute | solution.py:933
  168.4 5.4 %copy-start.2 = (bf16[768,512]{1,0:T(8,128)(2,1)S(1)}, bf16[768,512]{1,0:T(8,128)(2,1)}, u32[]{:S(2)}) copy-start(bf16[768,512]{1,0:T(8,128)(2,1)} %own_ref.1) | copy-start | bytes 2359300
  168.4 5.4 %copy-start.4 = (bf16[400,512]{1,0:T(8,128)(2,1)S(1)}, bf16[400,512]{1,0:T(8,128)(2,1)}, u32[]{:S(2)}) copy-start(bf16[400,512]{1,0:T(8,128)(2,1)} %copy-done.3) | copy-start | bytes 1228804
  168.4 5.4 %copy-start.6 = (bf16[400,512]{1,0:T(8,128)(2,1)S(1)}, bf16[400,512]{1,0:T(8,128)(2,1)}, u32[]{:S(2)}) copy-start(bf16[400,512]{1,0:T(8,128)(2,1)} %copy-done.5) | copy-start | bytes 1228804
  168.5 14.8 %collective-permute-start.20 = (bf16[1,160,512]{2,1,0:T(8,128)(2,1)S(1)}, bf16[1,160,512]{2,1,0:T(8,128)(2,1)S(1)}, u32[]{:S(2)}, u32[]{:S(2)}) collective-permute-start(bf16[1,160,512]{2,1,0:T(8,128)(2,1)S(1)} %fusion.7), channel_id=1, source_target_pairs={{0,16},{2,18},{4,20},{6,22},{8,24},{10,26},{12,28},{14,30},{16,0},... | collective-permute-start | bytes 491528 | tf_op jit(solution)/shard_map/ppermute | solution.py:933
  171.1 14.8 %collective-permute-start.19 = (bf16[1,144,512]{2,1,0:T(8,128)(2,1)S(1)}, bf16[1,144,512]{2,1,0:T(8,128)(2,1)S(1)}, u32[]{:S(2)}, u32[]{:S(2)}) collective-permute-start(bf16[1,144,512]{2,1,0:T(8,128)(2,1)S(1)} %fusion.9), channel_id=1, source_target_pairs={{0,16},{2,18},{4,20},{6,22},{8,24},{10,26},{12,28},{14,30},{16,0},... | collective-permute-start | bytes 442376 | tf_op jit(solution)/shard_map/ppermute | solution.py:933
  171.5 10.0 %collective-permute-start.16 = (bf16[1,112,512]{2,1,0:T(8,128)(2,1)S(1)}, bf16[1,112,512]{2,1,0:T(8,128)(2,1)S(1)}, u32[]{:S(2)}, u32[]{:S(2)}) collective-permute-start(bf16[1,112,512]{2,1,0:T(8,128)(2,1)S(1)} %fusion.14), channel_id=1, source_target_pairs={{1,0},{0,1},{3,2},{2,3},{5,4},{4,5},{7,6},{6,7},{9,8},{8,9},{11,10... | collective-permute-start | bytes 344072 | tf_op jit(solution)/shard_map/ppermute | solution.py:937
  172.2 9.9 %collective-permute-start.15 = (bf16[1,1,144,512]{3,2,1,0:T(8,128)(2,1)S(1)}, bf16[1,1,144,512]{3,2,1,0:T(8,128)(2,1)S(1)}, u32[]{:S(2)}, u32[]{:S(2)}) collective-permute-start(bf16[1,1,144,512]{3,2,1,0:T(8,128)(2,1)S(1)} %fusion.13), channel_id=1, source_target_pairs={{0,4},{2,6},{4,0},{6,2},{8,12},{10,14},{12,8},{14,10},{16,20},{18,... | collective-permute-start | bytes 442376 | tf_op jit(solution)/shard_map/ppermute | solution.py:933
  181.5 6.7 %collective-permute-start.18 = (bf16[1,112,512]{2,1,0:T(8,128)(2,1)S(1)}, bf16[1,112,512]{2,1,0:T(8,128)(2,1)S(1)}, u32[]{:S(2)}, u32[]{:S(2)}) collective-permute-start(bf16[1,112,512]{2,1,0:T(8,128)(2,1)S(1)} %fusion.17), channel_id=1, source_target_pairs={{0,4},{2,6},{4,0},{6,2},{8,12},{10,14},{12,8},{14,10},{16,20},{18,... | collective-permute-start | bytes 344072 | tf_op jit(solution)/shard_map/ppermute | solution.py:933
  182.2 6.9 %collective-permute-start.17 = (bf16[1,144,512]{2,1,0:T(8,128)(2,1)S(1)}, bf16[1,144,512]{2,1,0:T(8,128)(2,1)S(1)}, u32[]{:S(2)}, u32[]{:S(2)}) collective-permute-start(bf16[1,144,512]{2,1,0:T(8,128)(2,1)S(1)} %fusion.16), channel_id=1, source_target_pairs={{0,8},{2,10},{4,12},{6,14},{8,0},{10,2},{12,4},{14,6},{16,24},{18,... | collective-permute-start | bytes 442376 | tf_op jit(solution)/shard_map/ppermute | solution.py:933
  183.3 9.6 %collective-permute-start.23 = (bf16[1,160,512]{2,1,0:T(8,128)(2,1)S(1)}, bf16[1,160,512]{2,1,0:T(8,128)(2,1)S(1)}, u32[]{:S(2)}, u32[]{:S(2)}) collective-permute-start(bf16[1,160,512]{2,1,0:T(8,128)(2,1)S(1)} %add_convert_fusion.2), channel_id=1, source_target_pairs={{0,8},{2,10},{4,12},{6,14},{8,0},{10,2},{12,4},{14,6},{16,24},{18,... | collective-permute-start | bytes 491528 | tf_op jit(solution)/shard_map/ppermute | solution.py:933
  186.0 5.7 %collective-permute-start.24 = (bf16[1,144,512]{2,1,0:T(8,128)(2,1)S(1)}, bf16[1,144,512]{2,1,0:T(8,128)(2,1)S(1)}, u32[]{:S(2)}, u32[]{:S(2)}) collective-permute-start(bf16[1,144,512]{2,1,0:T(8,128)(2,1)S(1)} %get-tuple-element.167), channel_id=1, source_target_pairs={{0,4},{2,6},{4,0},{6,2},{8,12},{10,14},{12,8},{14,10},{16,20},{18,... | collective-permute-start | bytes 442376 | tf_op jit(solution)/shard_map/ppermute | solution.py:933
  188.2 9.8 %collective-permute-start.22 = (bf16[1,112,512]{2,1,0:T(8,128)(2,1)S(1)}, bf16[1,112,512]{2,1,0:T(8,128)(2,1)S(1)}, u32[]{:S(2)}, u32[]{:S(2)}) collective-permute-start(bf16[1,112,512]{2,1,0:T(8,128)(2,1)S(1)} %fusion.11), channel_id=1, source_target_pairs={{0,8},{2,10},{4,12},{6,14},{8,0},{10,2},{12,4},{14,6},{16,24},{18,... | collective-permute-start | bytes 344072 | tf_op jit(solution)/shard_map/ppermute | solution.py:933
  189.2 9.2 %collective-permute-start.21 = (bf16[1,144,512]{2,1,0:T(8,128)(2,1)S(1)}, bf16[1,144,512]{2,1,0:T(8,128)(2,1)S(1)}, u32[]{:S(2)}, u32[]{:S(2)}) collective-permute-start(bf16[1,144,512]{2,1,0:T(8,128)(2,1)S(1)} %fusion.8), channel_id=1, source_target_pairs={{0,16},{2,18},{4,20},{6,22},{8,24},{10,26},{12,28},{14,30},{16,0},... | collective-permute-start | bytes 442376 | tf_op jit(solution)/shard_map/ppermute | solution.py:933
  191.7 15.2 %collective-permute-start.28 = (bf16[2,144,512]{2,1,0:T(8,128)(2,1)S(1)}, bf16[2,144,512]{2,1,0:T(8,128)(2,1)S(1)}, u32[]{:S(2)}, u32[]{:S(2)}) collective-permute-start(bf16[2,144,512]{2,1,0:T(8,128)(2,1)S(1)} %pad_maximum_fusion.4), channel_id=1, source_target_pairs={{0,8},{2,10},{4,12},{6,14},{8,0},{10,2},{12,4},{14,6},{16,24},{18,... | collective-permute-start | bytes 884744 | tf_op jit(solution)/shard_map/ppermute | solution.py:933
  193.0 14.1 %collective-permute-start.27 = (bf16[2,160,512]{2,1,0:T(8,128)(2,1)S(1)}, bf16[2,160,512]{2,1,0:T(8,128)(2,1)S(1)}, u32[]{:S(2)}, u32[]{:S(2)}) collective-permute-start(bf16[2,160,512]{2,1,0:T(8,128)(2,1)S(1)} %pad_maximum_fusion.3), channel_id=1, source_target_pairs={{0,4},{2,6},{4,0},{6,2},{8,12},{10,14},{12,8},{14,10},{16,20},{18,... | collective-permute-start | bytes 983048 | tf_op jit(solution)/shard_map/ppermute | solution.py:933
  198.1 9.6 %collective-permute-start.26 = (bf16[1,112,512]{2,1,0:T(8,128)(2,1)S(1)}, bf16[1,112,512]{2,1,0:T(8,128)(2,1)S(1)}, u32[]{:S(2)}, u32[]{:S(2)}) collective-permute-start(bf16[1,112,512]{2,1,0:T(8,128)(2,1)S(1)} %fusion.15), channel_id=1, source_target_pairs={{0,16},{2,18},{4,20},{6,22},{8,24},{10,26},{12,28},{14,30},{16,0},... | collective-permute-start | bytes 344072 | tf_op jit(solution)/shard_map/ppermute | solution.py:933
  198.5 9.3 %collective-permute-start.25 = (bf16[1,144,512]{2,1,0:T(8,128)(2,1)S(1)}, bf16[1,144,512]{2,1,0:T(8,128)(2,1)S(1)}, u32[]{:S(2)}, u32[]{:S(2)}) collective-permute-start(bf16[1,144,512]{2,1,0:T(8,128)(2,1)S(1)} %add_convert_fusion.3), channel_id=1, source_target_pairs={{0,4},{2,6},{4,0},{6,2},{8,12},{10,14},{12,8},{14,10},{16,20},{18,... | collective-permute-start | bytes 442376 | tf_op jit(solution)/shard_map/ppermute | solution.py:933
  207.0 4.9 %collective-permute-start.32 = (bf16[4,144,512]{2,1,0:T(8,128)(2,1)S(1)}, bf16[4,144,512]{2,1,0:T(8,128)(2,1)S(1)}, u32[]{:S(2)}, u32[]{:S(2)}) collective-permute-start(bf16[4,144,512]{2,1,0:T(8,128)(2,1)S(1)} %pad_maximum_fusion.2.up_near), channel_id=1, source_target_pairs={{0,2},{2,0},{4,6},{6,4},{8,10},{10,8},{12,14},{14,12},{16,18},{18,... | collective-permute-start | bytes 1769480 | tf_op jit(solution)/shard_map/ppermute | solution.py:933
  207.1 4.7 %collective-permute-start.31 = (bf16[4,160,512]{2,1,0:T(8,128)(2,1)S(1)}, bf16[4,160,512]{2,1,0:T(8,128)(2,1)S(1)}, u32[]{:S(2)}, u32[]{:S(2)}) collective-permute-start(bf16[4,160,512]{2,1,0:T(8,128)(2,1)S(1)} %pad_maximum_fusion.dn_near), channel_id=1, source_target_pairs={{0,2},{2,0},{4,6},{6,4},{8,10},{10,8},{12,14},{14,12},{16,18},{18,... | collective-permute-start | bytes 1966088 | tf_op jit(solution)/shard_map/ppermute | solution.py:933
  207.8 2.7 %collective-permute-start.29 = (bf16[2,144,512]{2,1,0:T(8,128)(2,1)S(1)}, bf16[2,144,512]{2,1,0:T(8,128)(2,1)S(1)}, u32[]{:S(2)}, u32[]{:S(2)}) collective-permute-start(bf16[2,144,512]{2,1,0:T(8,128)(2,1)S(1)} %pad_maximum_fusion.5.refs_0_), channel_id=1, source_target_pairs={{0,2},{2,0},{4,6},{6,4},{8,10},{10,8},{12,14},{14,12},{16,18},{18,... | collective-permute-start | bytes 884744 | tf_op jit(solution)/shard_map/ppermute | solution.py:933
  208.5 2.0 collective-permute-start.30

commit v2 on v1

--- a/solution.py
+++ b/solution.py
@@ -283,12 +283,13 @@
     return pl.ds(pl.multiple_of(start * size, by), size)
 
 
-def pack_qkv_kernel(pos_ref, weight_ref, query_b_ref, value_b_ref, packed_ref, own_b_ref):
-    half = weight_ref.shape[0]
+def pack_kernel(pos_ref, qkv_ref, query_b_ref, value_b_ref, proj_ref, down_ref, up_ref, up_b_ref, *refs):
+    vec_refs, (qkv_out, own_b_ref, packed_ref, vecs_ref) = refs[:-4], refs[-4:]
+    half = qkv_ref.shape[0]
     wide = query_b_ref.shape[0] // 2
     query_b, value_b = (ref[...].reshape(1, 2 * wide) for ref in (query_b_ref, value_b_ref))
-    packed_ref[:half] = weight_ref[...]
-    packed_ref[half:] = jnp.zeros_like(packed_ref[half:])
+    qkv_out[:half] = qkv_ref[...]
+    qkv_out[half:] = jnp.zeros_like(qkv_out[half:])
     own_b_ref[...] = jnp.zeros_like(own_b_ref)
     parity = lax.rem(pos_ref[0], 2)
     for k in range(2):
@@ -298,37 +299,9 @@
 
         @pl.when(parity == k)
         def _():
-            packed_ref[half : half + 1, :wide] = query_b[:, cols]
-            packed_ref[half : half + 1, wide : 2 * wide] = value_b[:, cols]
-
-
-def pack_qkv(pos, weight, query_b, value_b):
-    rows, width = weight.shape
-    half = rows // 2
-    small = pl.BlockSpec(query_b.shape, lambda i, pos: (0,))
-    return pl.pallas_call(
-        pack_qkv_kernel,
-        grid_spec=pltpu.PrefetchScalarGridSpec(
-            num_scalar_prefetch=1,
-            grid=(1,),
-            in_specs=[pl.BlockSpec((half, width), lambda i, pos: (lax.rem(pos[0], 2), 0)), small, small],
-            out_specs=[
-                pl.BlockSpec((half + EXTRA, width), lambda i, pos: (0, 0)),
-                pl.BlockSpec((2 * EXTRA, width), lambda i, pos: (0, 0)),
-            ],
-        ),
-        out_shape=[
-            jax.ShapeDtypeStruct((half + EXTRA, width), bf16),
-            jax.ShapeDtypeStruct((2 * EXTRA, width), bf16),
-        ],
-        compiler_params=kernel_params(),
-        cost_estimate=cost(0, 1 << 20),
-        name="pack_qkv",
-    )(pos, weight, query_b, value_b)
-
-
-def pack_mlp_kernel(pos_ref, proj_ref, down_ref, up_ref, up_b_ref, *refs):
-    vec_refs, packed_ref, vecs_ref = refs[:-2], refs[-2], refs[-1]
+            qkv_out[half : half + 1, :wide] = query_b[:, cols]
+            qkv_out[half : half + 1, wide : 2 * wide] = value_b[:, cols]
+
     width = proj_ref.shape[1]
     at = 0
     for value in (proj_ref[...], down_ref[...]):
@@ -348,9 +321,10 @@
         vecs_ref[k : k + 1] = ref[...].reshape(1, width).astype(f32)
 
 
-def pack_mlp(pos, proj, down, up, up_b, vectors):
+def pack(pos, qkv, query_b, value_b, proj, down, up, up_b, vectors):
     width, hidden = up.shape
-    rows = (proj.shape[0] + 2 * hidden) // 2 + EXTRA
+    qkv_rows = qkv.shape[0] // 2 + EXTRA
+    mlp_rows = (proj.shape[0] + 2 * hidden) // 2 + EXTRA
 
     def half(array):
         return pl.BlockSpec((array.shape[0] // 2, array.shape[1]), lambda i, pos: (lax.rem(pos[0], 2), 0))
@@ -358,22 +332,21 @@
     def whole(array):
         return pl.BlockSpec(array.shape, lambda i, pos: (0,))
 
+    outs = [(qkv_rows, bf16), (2 * EXTRA, bf16), (mlp_rows, bf16), (EXTRA, f32)]
     return pl.pallas_call(
-        pack_mlp_kernel,
+        pack_kernel,
         grid_spec=pltpu.PrefetchScalarGridSpec(
             num_scalar_prefetch=1,
             grid=(1,),
-            in_specs=[half(proj), half(down), half(up), whole(up_b)] + [whole(v) for v in vectors],
-            out_specs=[
-                pl.BlockSpec((rows, width), lambda i, pos: (0, 0)),
-                pl.BlockSpec((EXTRA, width), lambda i, pos: (0, 0)),
-            ],
+            in_specs=[half(qkv), whole(query_b), whole(value_b), half(proj), half(down), half(up), whole(up_b)]
+            + [whole(v) for v in vectors],
+            out_specs=[pl.BlockSpec((rows, width), lambda i, pos: (0, 0)) for rows, _ in outs],
         ),
-        out_shape=[jax.ShapeDtypeStruct((rows, width), bf16), jax.ShapeDtypeStruct((EXTRA, width), f32)],
+        out_shape=[jax.ShapeDtypeStruct((rows, width), dtype) for rows, dtype in outs],
         compiler_params=kernel_params(),
-        cost_estimate=cost(0, 3 << 20),
-        name="pack_mlp",
-    )(pos, proj, down, up, up_b, *vectors)
+        cost_estimate=cost(0, 4 << 20),
+        name="pack",
+    )(pos, qkv, query_b, value_b, proj, down, up, up_b, *vectors)
 
 
 def attn_fwd_kernel(pos_ref, x_ref, *refs, heads, q_block, fetched):
@@ -811,7 +784,7 @@
             jax.ShapeDtypeStruct(sums.shape, f32),
         ],
         input_output_aliases={7: 1, 8: 2} if earlier else {},
-        compiler_params=kernel_params(48_000_000),
+        compiler_params=kernel_params(51_000_000),
         cost_estimate=cost(8 << 30, 10 << 20),
         name="attn_bwd",
     )(pos, x, packed, probs, ctx_low, mixed, sums, *earlier)
@@ -858,7 +831,7 @@
             scratch_shapes=[pltpu.VMEM((n_shards - 1,) + own.shape, bf16)],
         ),
         out_shape=jax.ShapeDtypeStruct((rows, width), bf16),
-        compiler_params=kernel_params(48_000_000),
+        compiler_params=kernel_params(51_000_000),
         cost_estimate=cost(4 << 30, 12 << 20),
         name="input_gradient",
     )(pos, grad_one, own, *fetched, *packed_grads)
@@ -892,7 +865,7 @@
             jax.ShapeDtypeStruct((width, hidden), f32),
             jax.ShapeDtypeStruct((hidden, width), f32),
         ],
-        compiler_params=kernel_params(48_000_000),
+        compiler_params=kernel_params(51_000_000),
         cost_estimate=cost(0, 14 << 20),
         name="mlp_place",
     )(pos, *dn_parts, *up_parts)
@@ -923,7 +896,7 @@
         in_specs=[pl.BlockSpec(memory_space=pltpu.SMEM)] + [in_vmem()] * (len(flat) + 1),
         out_specs=[in_vmem()] * 3,
         out_shape=[jax.ShapeDtypeStruct((heads, PART_ROWS, flat[0].shape[2]), f32), vector, vector],
-        compiler_params=kernel_params(48_000_000),
+        compiler_params=kernel_params(51_000_000),
         cost_estimate=cost(0, 3 << 20),
         name="qkv_place",
     )(pos, *flat, bias)
@@ -1027,10 +1000,11 @@
     pos = lax.axis_index("dp").astype(jnp.int32).reshape(1)
     shifts = range(1, n_tensor)
 
-    qkv_half, own_bias = pack_qkv(pos, qkv_weight, query_bias, value_bias)
+    vectors = [proj_bias, first_gain, first_shift, down_bias, second_gain, second_shift]
+    qkv_half, own_bias, mlp_half, vecs = pack(
+        pos, qkv_weight, query_bias, value_bias, proj_weight, down_weight, up_weight, up_bias, vectors
+    )
     qkv_near = [shift_tensor(qkv_half, by, n_tensor) for by in shifts]
-    vectors = [proj_bias, first_gain, first_shift, down_bias, second_gain, second_shift]
-    mlp_half, vecs = pack_mlp(after(pos, qkv_half), proj_weight, down_weight, up_weight, up_bias, vectors)
     shapes = [
         jax.ShapeDtypeStruct((n_tensor, n_seq, n_heads * PART_ROWS, SEQ_LEN), bf16),
         jax.ShapeDtypeStruct((n_tensor, n_seq, n_heads, SEQ_LEN, SEQ_LEN), bf16),
@@ -1131,7 +1105,7 @@
     ("qb", "qa", "dn", "up", "qb"),
     ("qb", "qa", "dn", "up", "qb", "qa", "up", "dn", "qb", "qa", "up", "dn", "qb", "qa"),
 )
-UNROLLED = ()
+UNROLLED = (0,)
 
 
 def solution(mesh):

time: 215 us -> 211 us (0.981)
    unnamed x20 -> x22, local copies, waits for them, and re-layouts: 4.59 us -> 3.24 us
  transfers between devices with their start and end apart: 33 -> 33, of which waited for: 9 -> 9; matrix products, arithmetic and copies ran while one was open for 2% -> 2% of each run, Pallas kernels for 50% -> 49%
where the time goes in v2:
time: 211 us
  Pallas kernels  153 us (73%)
  starting transfers between devices  30.3 us (14%)
  waiting for transfers between devices  20.3 us (10%)
  local copies, waits for them, and re-layouts  4.03 us (2%)
  other arithmetic  2.16 us (1%)
    pallas_call x4, Pallas kernels, attn_bwd(): pl.pallas_call(partial(attn_bwd_kernel, head=head, cut=cut, extra=extra,...  54.6 us
    pallas_call x1, Pallas kernels, middle(): pl.pallas_call(partial(middle_kernel, n_others=n_others, chunk=min(1024,...  43.8 us
    pallas_call x2, Pallas kernels, attn_fwd(): pl.pallas_call(partial(attn_fwd_kernel, heads=heads, q_block=q_block, fet...  39.9 us
    ppermute x27, starting transfers between devices, swap_dp(): return lax.ppermute(value, 'dp', [(i, i ^ bits) for i in range(n_dp)])  22.9 us
    ppermute x27, waiting for transfers between devices, swap_dp(): return lax.ppermute(value, 'dp', [(i, i ^ bits) for i in range(n_dp)])  19.7 us
    pallas_call x1, Pallas kernels, input_gradient(): pl.pallas_call(partial(input_grad_kernel, n_others=n_shards - 1), grid_sp...  8.04 us
    ppermute x6, starting transfers between devices, shift_tensor(): lax.ppermute(value, 'tensor', [((i + by) % n_tensor, i) for i in range(n_...  7.32 us
  transfers between devices with their start and end apart: 33, of which 9 were waited for; matrix products, arithmetic and copies ran while one was open for 2% of the time, Pallas kernels for 49%

profile of v2, /device:TPU:0, one launch (start us, length us, event | category | flops | bytes accessed | tf_op | source)
XLA Modules:
  0.0 210.5 jit_solution(1303094161530261366)
XLA Ops:
  0.7 2.7 %pack.1 = (bf16[400,512]{1,0:T(8,128)(2,1)}, bf16[32,512]{1,0:T(8,128)(2,1)}, bf16[1168,512]{1,0:T(8,128)(2,1)}, f32[16,512]{1,0:T(8,128)}) custom-call(s32[1]{0:T(128)} %bitcast.pos_ref, bf16[768,512]{1,0:T(8,128)(2,1)} %own_ref.1, bf16[256]{0:T(256)(128)(2,1)} %query_b_ref.1, bf16[256]{0:T(256)(128)(2,1)} %value_b_ref.1, bf16[256,512]{1,0:T(8,128)(2,1)} %proj_own.1, ...), custom_call_target="tpu_custom_call" | custom-call | bytes 4194304 | tf_op jit(solution)/shard_map/pack/pallas_call | solution.py:336
  3.3 2.9 %collective-permute-start = (bf16[400,512]{1,0:T(8,128)(2,1)}, bf16[400,512]{1,0:T(8,128)(2,1)S(1)}, u32[]{:S(2)}, u32[]{:S(2)}) collective-permute-start(bf16[400,512]{1,0:T(8,128)(2,1)} %get-tuple-element.89), channel_id=1, source_target_pairs={{1,0},{0,1},{3,2},{2,3},{5,4},{4,5},{7,6},{6,7},{9,8},{8,9},{11,10... | collective-permute-start | bytes 1228808 | tf_op jit(solution)/shard_map/ppermute | solution.py:910
  6.4 19.9 %attn_fwd.2 = (bf16[2,2,768,1024]{3,2,1,0:T(8,128)(2,1)}, bf16[2,2,4,1024,1024]{4,3,2,1,0:T(8,128)(2,1)}, bf16[2,2,256,1024]{3,2,1,0:T(8,128)(2,1)}, f32[2,2,256,1024]{3,2,1,0:T(8,128)}) custom-call(s32[1]{0:T(128)} %bitcast.pos_ref, bf16[2048,512]{1,0:T(8,128)(2,1)} %x_ref.8, bf16[768,512]{1,0:T(8,128)(2,1)} %own_ref.1, ...), custom_call_target="tpu_custom_call" | custom-call | flops 14495514624 | bytes 25165824 | tf_op jit(solution)/shard_map/attn_fwd/pallas_call | solution.py:423
  26.3 0.1 collective-permute-start.1
  26.4 1.7 collective-permute-done.1.refs_1_
  28.1 0.8 copy-done.4
  28.9 20.0 %attn_fwd.3 = (bf16[2,2,768,1024]{3,2,1,0:T(8,128)(2,1)}, bf16[2,2,4,1024,1024]{4,3,2,1,0:T(8,128)(2,1)}, bf16[2,2,256,1024]{3,2,1,0:T(8,128)(2,1)}, f32[2,2,256,1024]{3,2,1,0:T(8,128)}) custom-call(s32[1]{0:T(128)} %bitcast.pos_ref, bf16[2048,512]{1,0:T(8,128)(2,1)} %x_ref.8, ...), custom_call_target="tpu_custom_call", output_to_operand_aliasing={{0}: (4, {}), {1}: (5, {}), {2}: (6, {}), {3}: (7, {})} | custom-call | flops 1811939328 | bytes 25165824 | tf_op jit(solution)/shard_map/attn_fwd/pallas_call | solution.py:423
  48.9 0.2 collective-permute-start.3
  49.1 3.1 %collective-permute-done.3.refs_1_ = bf16[1168,512]{1,0:T(8,128)(2,1)} collective-permute-done((bf16[1168,512]{1,0:T(8,128)(2,1)}, bf16[1168,512]{1,0:T(8,128)(2,1)}, u32[]{:S(2)}, u32[]{:S(2)}) %collective-permute-start.3) | collective-permute-done | bytes 1196064 | tf_op jit(solution)/shard_map/ppermute | solution.py:906
  52.2 43.8 %middle.1 = (bf16[2048,512]{1,0:T(8,128)(2,1)}, f32[2048,512]{1,0:T(8,128)}, bf16[2,2,256,1024]{3,2,1,0:T(8,128)(2,1)}, bf16[2,4,160,512]{3,2,1,0:T(8,128)(2,1)}...) custom-call(s32[1]{0:T(128)} %bitcast.pos_ref, ...), custom_call_target="tpu_custom_call" | custom-call | flops 32212254720 | bytes 31457280 | tf_op jit(solution)/shard_map/middle/pallas_call | solution.py:635
  96.0 0.2 collective-permute-start.6
  96.2 0.4 collective-permute-start.4
  96.6 1.6 copy-done
  98.2 12.9 %attn_bwd.4 = (bf16[2,2,192,1024]{3,2,1,0:T(8,128)(2,1)S(1)}, bf16[2,2,144,512]{3,2,1,0:T(8,128)(2,1)S(1)}, bf16[2,2,144,512]{3,2,1,0:T(8,128)(2,1)S(1)}, f32[2,16,192]{2,1,0:T(8,128)S(1)}) custom-call(s32[1]{0:T(128)} %bitcast.pos_ref, bf16[2048,512]{1,0:T(8,128)(2,1)S(1)} %copy-done, bf16[2,2,768,1024]{3,2,1,0:T(8,128)(2,1)} %get-tuple-element.107.packed_ref, ...), custom_call_target="tpu_custom_call" | custom-call | flops 8589934592 | bytes 10485760 | tf_op jit(solution)/shard_map/attn_bwd/pallas_call | solution.py:755
  111.1 0.4 convert_add_fusion.1
  111.6 2.1 %collective-permute-start.7 = (bf16[2,2,144,512]{3,2,1,0:T(8,128)(2,1)S(1)}, bf16[2,2,144,512]{3,2,1,0:T(8,128)(2,1)S(1)}, u32[]{:S(2)}, u32[]{:S(2)}) collective-permute-start(bf16[2,2,144,512]{3,2,1,0:T(8,128)(2,1)S(1)} %pad_maximum_fusion.1), channel_id=1, source_target_pairs={{0,8},{2,10},{4,12},{6,14},{8,0},{10,2},{12,4},{14,6},{16,24},{18,... | collective-permute-start | bytes 1769480 | tf_op jit(solution)/shard_map/ppermute | solution.py:906
  113.7 0.2 fusion
  113.9 1.5 collective-permute-start.5
  115.4 13.8 %attn_bwd.5 = (bf16[2,2,192,1024]{3,2,1,0:T(8,128)(2,1)S(1)}, bf16[2,2,144,512]{3,2,1,0:T(8,128)(2,1)S(1)}, bf16[2,2,144,512]{3,2,1,0:T(8,128)(2,1)S(1)}, f32[2,16,192]{2,1,0:T(8,128)S(1)}) custom-call(s32[1]{0:T(128)} %bitcast.pos_ref, bf16[2048,512]{1,0:T(8,128)(2,1)S(1)} %copy-done, ...), custom_call_target="tpu_custom_call", output_to_operand_aliasing={{1}: (7, {}), {2}: (8, {})} | custom-call | flops 8589934592 | bytes 10485760 | tf_op jit(solution)/shard_map/attn_bwd/pallas_call | solution.py:755
  129.2 0.1 fusion.6
  129.3 0.6 collective-permute-start.9
  129.9 0.6 collective-permute-done.5
  130.5 0.3 bitcast_add_fusion
  130.8 1.6 collective-permute-start.8
  132.4 13.7 %attn_bwd.6 = (bf16[2,2,192,1024]{3,2,1,0:T(8,128)(2,1)S(1)}, bf16[2,2,144,512]{3,2,1,0:T(8,128)(2,1)S(1)}, bf16[2,2,144,512]{3,2,1,0:T(8,128)(2,1)S(1)}, f32[2,16,192]{2,1,0:T(8,128)S(1)}) custom-call(s32[1]{0:T(128)} %bitcast.pos_ref, bf16[2048,512]{1,0:T(8,128)(2,1)S(1)} %copy-done, ...), custom_call_target="tpu_custom_call", output_to_operand_aliasing={{1}: (7, {}), {2}: (8, {})} | custom-call | flops 8589934592 | bytes 10485760 | tf_op jit(solution)/shard_map/attn_bwd/pallas_call | solution.py:755
  146.1 0.1 collective-permute-start.10
  146.2 0.1 fusion.2
  146.4 0.6 collective-permute-start.13
  146.9 0.1 slice_add_fusion
  147.0 0.2 copy-done.6
  147.3 1.4 collective-permute-start.12
  148.7 0.1 fusion.5
  148.8 1.6 collective-permute-start.11
  150.3 14.2 %attn_bwd.7 = (bf16[2,2,192,1024]{3,2,1,0:T(8,128)(2,1)S(1)}, bf16[2,1,112,512]{3,2,1,0:T(8,128)(2,1)S(1)}, bf16[2,1,112,512]{3,2,1,0:T(8,128)(2,1)S(1)}, f32[2,16,192]{2,1,0:T(8,128)}) custom-call(s32[1]{0:T(128)} %bitcast.pos_ref, bf16[2048,512]{1,0:T(8,128)(2,1)S(1)} %copy-done, bf16[2,2,768,1024]{3,2,1,0:T(8,128)(2,1)} %get-tuple-element.107.packed_ref, ...), custom_call_target="tpu_custom_call" | custom-call | flops 8589934592 | bytes 10485760 | tf_op jit(solution)/shard_map/attn_bwd/pallas_call | solution.py:755
  164.7 2.7 %collective-permute-start.20 = (bf16[1,160,512]{2,1,0:T(8,128)(2,1)S(1)}, bf16[1,160,512]{2,1,0:T(8,128)(2,1)S(1)}, u32[]{:S(2)}, u32[]{:S(2)}) collective-permute-start(bf16[1,160,512]{2,1,0:T(8,128)(2,1)S(1)} %fusion.7), channel_id=1, source_target_pairs={{0,16},{2,18},{4,20},{6,22},{8,24},{10,26},{12,28},{14,30},{16,0},... | collective-permute-start | bytes 491528 | tf_op jit(solution)/shard_map/ppermute | solution.py:906
  167.4 0.3 collective-permute-start.19
  167.7 0.6 collective-permute-start.16
  168.3 0.1 bitcast_add_fusion.1
  168.5 1.4 collective-permute-start.15
  169.9 8.0 %input_gradient.1 = bf16[2048,512]{1,0:T(8,128)(2,1)} custom-call(s32[1]{0:T(128)} %bitcast.pos_ref, f32[2048,512]{1,0:T(8,128)} %get-tuple-element.138.grad_one_ref, bf16[768,512]{1,0:T(8,128)(2,1)S(1)} %copy-done.1, bf16[400,512]{1,0:T(8,128)(2,1)S(1)} %copy-done.3, bf16[400,512]{1,0:T(8,128)(2,1)S(1)} %copy-done.5, ...), custom_call_target="tpu_custom_call" | custom-call | flops 4294967296 | bytes 12582912 | tf_op jit(solution)/shard_map/input_gradient/pallas_call | solution.py:824
  178.0 0.8 collective-permute-start.18
  178.8 0.9 collective-permute-start.17
  179.8 1.3 collective-permute-start.23
  181.0 1.2 collective-permute-done.19
  182.3 1.4 collective-permute-start.24
  183.6 0.6 fusion.20
  184.4 1.2 collective-permute-done.17
  185.6 2.7 %collective-permute-start.21 = (bf16[1,144,512]{2,1,0:T(8,128)(2,1)S(1)}, bf16[1,144,512]{2,1,0:T(8,128)(2,1)S(1)}, u32[]{:S(2)}, u32[]{:S(2)}) collective-permute-start(bf16[1,144,512]{2,1,0:T(8,128)(2,1)S(1)} %fusion.8), channel_id=1, source_target_pairs={{0,16},{2,18},{4,20},{6,22},{8,24},{10,26},{12,28},{14,30},{16,0},... | collective-permute-start | bytes 442376 | tf_op jit(solution)/shard_map/ppermute | solution.py:906
  188.4 0.8 collective-permute-start.28
  189.2 1.3 collective-permute-done.23
  190.5 1.4 collective-permute-start.27
  191.9 2.8 %collective-permute-done.22 = bf16[1,112,512]{2,1,0:T(8,128)(2,1)S(1)} collective-permute-done((bf16[1,112,512]{2,1,0:T(8,128)(2,1)S(1)}, bf16[1,112,512]{2,1,0:T(8,128)(2,1)S(1)}, u32[]{:S(2)}, u32[]{:S(2)}) %collective-permute-start.22) | collective-permute-done | bytes 114720 | tf_op jit(solution)/shard_map/ppermute | solution.py:906
  194.7 0.1 fusion.15
  194.9 0.1 add_convert_fusion.3
  195.0 1.4 collective-permute-start.25
  196.3 6.8 %collective-permute-done.28 = bf16[2,144,512]{2,1,0:T(8,128)(2,1)S(1)} collective-permute-done((bf16[2,144,512]{2,1,0:T(8,128)(2,1)S(1)}, bf16[2,144,512]{2,1,0:T(8,128)(2,1)S(1)}, u32[]{:S(2)}, u32[]{:S(2)}) %collective-permute-start.28) | collective-permute-done | bytes 294944 | tf_op jit(solution)/shard_map/ppermute | solution.py:906
  203.4 0.5 collective-permute-start.31
  203.9 0.1 fusion.18
  204.1 0.1 collective-permute-start.29
  204.2 0.6 copy.38
  204.8 0.5 collective-permute-start.30
  205.3 1.6 collective-permute-done.30.refs_3_
  206.8 1.3 qkv_place.1
  208.1 2.5 %mlp_place.1 = (f32[256,512]{1,0:T(8,128)}, f32[512,1024]{1,0:T(8,128)}, f32[1024,512]{1,0:T(8,128)}) custom-call(s32[1]{0:T(128)} %bitcast.pos_ref, bf16[4,160,512]{2,1,0:T(8,128)(2,1)S(1)} %pad_maximum_fusion.dn_near, bf16[4,160,512]{2,1,0:T(8,128)(2,1)S(1)} %collective-permute-done.31.dn_far, bf16[4,144,512]{2,1,0:T(8,128)(2,1)S(1)} %pad_maximum_fusion.2.up_near, ...), custom_call_target="tpu_custom_call" | custom-call | bytes 14680064 | tf_op jit(solution)/shard_map/mlp_place/pallas_call | solution.py:859
  (70 shorter events, 1.3 us)
Async XLA Ops:
  3.3 22.9 %collective-permute-start = (bf16[400,512]{1,0:T(8,128)(2,1)}, bf16[400,512]{1,0:T(8,128)(2,1)S(1)}, u32[]{:S(2)}, u32[]{:S(2)}) collective-permute-start(bf16[400,512]{1,0:T(8,128)(2,1)} %get-tuple-element.89), channel_id=1, source_target_pairs={{1,0},{0,1},{3,2},{2,3},{5,4},{4,5},{7,6},{6,7},{9,8},{8,9},{11,10... | collective-permute-start | bytes 1228808 | tf_op jit(solution)/shard_map/ppermute | solution.py:910
  6.3 42.6 %collective-permute-start.2 = (bf16[1168,512]{1,0:T(8,128)(2,1)}, bf16[1168,512]{1,0:T(8,128)(2,1)}, u32[]{:S(2)}, u32[]{:S(2)}) collective-permute-start(bf16[1168,512]{1,0:T(8,128)(2,1)} %get-tuple-element.90), channel_id=1, source_target_pairs={{1,0},{0,1},{3,2},{2,3},{5,4},{4,5},{7,6},{6,7},{9,8},{8,9},{11,10... | collective-permute-start | bytes 3588104 | tf_op jit(solution)/shard_map/ppermute | solution.py:910
  26.3 1.8 copy-start.2
  26.3 1.8 collective-permute-start.1
  28.1 0.8 copy-start.4
  48.9 3.3 %collective-permute-start.3 = (bf16[1168,512]{1,0:T(8,128)(2,1)}, bf16[1168,512]{1,0:T(8,128)(2,1)}, u32[]{:S(2)}, u32[]{:S(2)}) collective-permute-start(bf16[1168,512]{1,0:T(8,128)(2,1)} %collective-permute-done.2.refs_0_), channel_id=1, source_target_pairs={{0,2},{2,0},{4,6},{6,4},{8,10},{10,8},{12,14},{14,12},{16,18},{18,... | collective-permute-start | bytes 3588104 | tf_op jit(solution)/shard_map/ppermute | solution.py:906
  96.0 15.1 %collective-permute-start.6 = (bf16[2,4,144,512]{3,2,1,0:T(8,128)(2,1)}, bf16[2,4,144,512]{3,2,1,0:T(8,128)(2,1)S(1)}, u32[]{:S(2)}, u32[]{:S(2)}) collective-permute-start(bf16[2,4,144,512]{3,2,1,0:T(8,128)(2,1)} %get-tuple-element.105), channel_id=1, source_target_pairs={{0,2},{2,0},{4,6},{6,4},{8,10},{10,8},{12,14},{14,12},{16,18},{18,... | collective-permute-start | bytes 3538952 | tf_op jit(solution)/shard_map/ppermute | solution.py:906
  96.2 17.5 %collective-permute-start.4 = (bf16[2,4,160,512]{3,2,1,0:T(8,128)(2,1)}, bf16[2,4,160,512]{3,2,1,0:T(8,128)(2,1)S(1)}, u32[]{:S(2)}, u32[]{:S(2)}) collective-permute-start(bf16[2,4,160,512]{3,2,1,0:T(8,128)(2,1)} %get-tuple-element.104), channel_id=1, source_target_pairs={{0,2},{2,0},{4,6},{6,4},{8,10},{10,8},{12,14},{14,12},{16,18},{18,... | collective-permute-start | bytes 3932168 | tf_op jit(solution)/shard_map/ppermute | solution.py:906
  96.6 1.6 copy-start
  98.2 12.9 %copy-start.9 = (bf16[2,4,144,512]{3,2,1,0:T(8,128)(2,1)S(1)}, bf16[2,4,144,512]{3,2,1,0:T(8,128)(2,1)}, u32[]{:S(2)}) copy-start(bf16[2,4,144,512]{3,2,1,0:T(8,128)(2,1)} %get-tuple-element.113) | copy-start | bytes 3538948
  111.4 2.3 %copy-start.8 = (bf16[2,4,160,512]{3,2,1,0:T(8,128)(2,1)S(1)}, bf16[2,4,160,512]{3,2,1,0:T(8,128)(2,1)}, u32[]{:S(2)}) copy-start(bf16[2,4,160,512]{3,2,1,0:T(8,128)(2,1)} %get-tuple-element.103) | copy-start | bytes 3932164
  111.6 17.6 %collective-permute-start.7 = (bf16[2,2,144,512]{3,2,1,0:T(8,128)(2,1)S(1)}, bf16[2,2,144,512]{3,2,1,0:T(8,128)(2,1)S(1)}, u32[]{:S(2)}, u32[]{:S(2)}) collective-permute-start(bf16[2,2,144,512]{3,2,1,0:T(8,128)(2,1)S(1)} %pad_maximum_fusion.1), channel_id=1, source_target_pairs={{0,8},{2,10},{4,12},{6,14},{8,0},{10,2},{12,4},{14,6},{16,24},{18,... | collective-permute-start | bytes 1769480 | tf_op jit(solution)/shard_map/ppermute | solution.py:906
  113.9 16.6 %collective-permute-start.5 = (bf16[4,160,512]{2,1,0:T(8,128)(2,1)S(1)}, bf16[4,160,512]{2,1,0:T(8,128)(2,1)S(1)}, u32[]{:S(2)}, u32[]{:S(2)}) collective-permute-start(bf16[4,160,512]{2,1,0:T(8,128)(2,1)S(1)} %fusion), channel_id=1, source_target_pairs={{1,0},{0,1},{3,2},{2,3},{5,4},{4,5},{7,6},{6,7},{9,8},{8,9},{11,10... | collective-permute-start | bytes 1966088 | tf_op jit(solution)/shard_map/ppermute | solution.py:910
  129.3 16.9 %collective-permute-start.9 = (bf16[2,144,512]{2,1,0:T(8,128)(2,1)S(1)}, bf16[2,144,512]{2,1,0:T(8,128)(2,1)S(1)}, u32[]{:S(2)}, u32[]{:S(2)}) collective-permute-start(bf16[2,144,512]{2,1,0:T(8,128)(2,1)S(1)} %fusion.6), channel_id=1, source_target_pairs={{1,0},{0,1},{3,2},{2,3},{5,4},{4,5},{7,6},{6,7},{9,8},{8,9},{11,10... | collective-permute-start | bytes 884744 | tf_op jit(solution)/shard_map/ppermute | solution.py:910
  130.8 16.1 %collective-permute-start.8 = (bf16[1,2,160,512]{3,2,1,0:T(8,128)(2,1)S(1)}, bf16[1,2,160,512]{3,2,1,0:T(8,128)(2,1)S(1)}, u32[]{:S(2)}, u32[]{:S(2)}) collective-permute-start(bf16[1,2,160,512]{3,2,1,0:T(8,128)(2,1)S(1)} %fusion.4), channel_id=1, source_target_pairs={{0,4},{2,6},{4,0},{6,2},{8,12},{10,14},{12,8},{14,10},{16,20},{18,... | collective-permute-start | bytes 983048 | tf_op jit(solution)/shard_map/ppermute | solution.py:906
  146.1 1.1 copy-start.6
  146.1 2.6 %collective-permute-start.10 = (bf16[2,2,144,512]{3,2,1,0:T(8,128)(2,1)S(1)}, bf16[2,2,144,512]{3,2,1,0:T(8,128)(2,1)S(1)}, u32[]{:S(2)}, u32[]{:S(2)}) collective-permute-start(bf16[2,2,144,512]{3,2,1,0:T(8,128)(2,1)S(1)} %get-tuple-element.124), channel_id=1, source_target_pairs={{0,2},{2,0},{4,6},{6,4},{8,10},{10,8},{12,14},{14,12},{16,18},{18,... | collective-permute-start | bytes 1769480 | tf_op jit(solution)/shard_map/ppermute | solution.py:906
  146.4 18.2 %collective-permute-start.13 = (bf16[1,1,144,512]{3,2,1,0:T(8,128)(2,1)S(1)}, bf16[1,1,144,512]{3,2,1,0:T(8,128)(2,1)S(1)}, u32[]{:S(2)}, u32[]{:S(2)}) collective-permute-start(bf16[1,1,144,512]{3,2,1,0:T(8,128)(2,1)S(1)} %fusion.12), channel_id=1, source_target_pairs={{0,4},{2,6},{4,0},{6,2},{8,12},{10,14},{12,8},{14,10},{16,20},{18,... | collective-permute-start | bytes 442376 | tf_op jit(solution)/shard_map/ppermute | solution.py:906
  147.3 17.3 %collective-permute-start.12 = (bf16[1,1,160,512]{3,2,1,0:T(8,128)(2,1)S(1)}, bf16[1,1,160,512]{3,2,1,0:T(8,128)(2,1)S(1)}, u32[]{:S(2)}, u32[]{:S(2)}) collective-permute-start(bf16[1,1,160,512]{3,2,1,0:T(8,128)(2,1)S(1)} %fusion.10), channel_id=1, source_target_pairs={{0,8},{2,10},{4,12},{6,14},{8,0},{10,2},{12,4},{14,6},{16,24},{18,... | collective-permute-start | bytes 491528 | tf_op jit(solution)/shard_map/ppermute | solution.py:906
  148.8 19.6 %collective-permute-start.11 = (bf16[2,144,512]{2,1,0:T(8,128)(2,1)S(1)}, bf16[2,144,512]{2,1,0:T(8,128)(2,1)S(1)}, u32[]{:S(2)}, u32[]{:S(2)}) collective-permute-start(bf16[2,144,512]{2,1,0:T(8,128)(2,1)S(1)} %fusion.5), channel_id=1, source_target_pairs={{1,0},{0,1},{3,2},{2,3},{5,4},{4,5},{7,6},{6,7},{9,8},{8,9},{11,10... | collective-permute-start | bytes 884744 | tf_op jit(solution)/shard_map/ppermute | solution.py:910
  164.6 3.9 %copy-start.7 = (bf16[2,2,192,1024]{3,2,1,0:T(8,128)(2,1)}, bf16[2,2,192,1024]{3,2,1,0:T(8,128)(2,1)S(1)}, u32[]{:S(2)}) copy-start(bf16[2,2,192,1024]{3,2,1,0:T(8,128)(2,1)S(1)} %get-tuple-element.142.refs_5_) | copy-start | bytes 4718596
  164.6 3.1 %collective-permute-start.14 = (bf16[2,1,112,512]{3,2,1,0:T(8,128)(2,1)S(1)}, bf16[2,1,112,512]{3,2,1,0:T(8,128)(2,1)S(1)}, u32[]{:S(2)}, u32[]{:S(2)}) collective-permute-start(bf16[2,1,112,512]{3,2,1,0:T(8,128)(2,1)S(1)} %get-tuple-element.131), channel_id=1, source_target_pairs={{0,2},{2,0},{4,6},{6,4},{8,10},{10,8},{12,14},{14,12},{16,18},{18,... | collective-permute-start | bytes 688136 | tf_op jit(solution)/shard_map/ppermute | solution.py:906
  164.6 5.2 %copy-start.1 = (bf16[768,512]{1,0:T(8,128)(2,1)S(1)}, bf16[768,512]{1,0:T(8,128)(2,1)}, u32[]{:S(2)}) copy-start(bf16[768,512]{1,0:T(8,128)(2,1)} %own_ref.1) | copy-start | bytes 2359300
  164.7 5.2 %copy-start.3 = (bf16[400,512]{1,0:T(8,128)(2,1)S(1)}, bf16[400,512]{1,0:T(8,128)(2,1)}, u32[]{:S(2)}) copy-start(bf16[400,512]{1,0:T(8,128)(2,1)} %copy-done.2) | copy-start | bytes 1228804
  164.7 5.2 %copy-start.5 = (bf16[400,512]{1,0:T(8,128)(2,1)S(1)}, bf16[400,512]{1,0:T(8,128)(2,1)}, u32[]{:S(2)}) copy-start(bf16[400,512]{1,0:T(8,128)(2,1)} %copy-done.4) | copy-start | bytes 1228804
  164.7 15.0 %collective-permute-start.20 = (bf16[1,160,512]{2,1,0:T(8,128)(2,1)S(1)}, bf16[1,160,512]{2,1,0:T(8,128)(2,1)S(1)}, u32[]{:S(2)}, u32[]{:S(2)}) collective-permute-start(bf16[1,160,512]{2,1,0:T(8,128)(2,1)S(1)} %fusion.7), channel_id=1, source_target_pairs={{0,16},{2,18},{4,20},{6,22},{8,24},{10,26},{12,28},{14,30},{16,0},... | collective-permute-start | bytes 491528 | tf_op jit(solution)/shard_map/ppermute | solution.py:906
  167.4 14.8 %collective-permute-start.19 = (bf16[1,144,512]{2,1,0:T(8,128)(2,1)S(1)}, bf16[1,144,512]{2,1,0:T(8,128)(2,1)S(1)}, u32[]{:S(2)}, u32[]{:S(2)}) collective-permute-start(bf16[1,144,512]{2,1,0:T(8,128)(2,1)S(1)} %fusion.9), channel_id=1, source_target_pairs={{0,16},{2,18},{4,20},{6,22},{8,24},{10,26},{12,28},{14,30},{16,0},... | collective-permute-start | bytes 442376 | tf_op jit(solution)/shard_map/ppermute | solution.py:906
  167.7 10.2 %collective-permute-start.16 = (bf16[1,112,512]{2,1,0:T(8,128)(2,1)S(1)}, bf16[1,112,512]{2,1,0:T(8,128)(2,1)S(1)}, u32[]{:S(2)}, u32[]{:S(2)}) collective-permute-start(bf16[1,112,512]{2,1,0:T(8,128)(2,1)S(1)} %fusion.14), channel_id=1, source_target_pairs={{1,0},{0,1},{3,2},{2,3},{5,4},{4,5},{7,6},{6,7},{9,8},{8,9},{11,10... | collective-permute-start | bytes 344072 | tf_op jit(solution)/shard_map/ppermute | solution.py:910
  168.5 10.3 %collective-permute-start.15 = (bf16[1,1,144,512]{3,2,1,0:T(8,128)(2,1)S(1)}, bf16[1,1,144,512]{3,2,1,0:T(8,128)(2,1)S(1)}, u32[]{:S(2)}, u32[]{:S(2)}) collective-permute-start(bf16[1,1,144,512]{3,2,1,0:T(8,128)(2,1)S(1)} %fusion.13), channel_id=1, source_target_pairs={{0,4},{2,6},{4,0},{6,2},{8,12},{10,14},{12,8},{14,10},{16,20},{18,... | collective-permute-start | bytes 442376 | tf_op jit(solution)/shard_map/ppermute | solution.py:906
  178.0 6.3 %collective-permute-start.18 = (bf16[1,112,512]{2,1,0:T(8,128)(2,1)S(1)}, bf16[1,112,512]{2,1,0:T(8,128)(2,1)S(1)}, u32[]{:S(2)}, u32[]{:S(2)}) collective-permute-start(bf16[1,112,512]{2,1,0:T(8,128)(2,1)S(1)} %fusion.17), channel_id=1, source_target_pairs={{0,4},{2,6},{4,0},{6,2},{8,12},{10,14},{12,8},{14,10},{16,20},{18,... | collective-permute-start | bytes 344072 | tf_op jit(solution)/shard_map/ppermute | solution.py:906
  178.8 6.8 %collective-permute-start.17 = (bf16[1,144,512]{2,1,0:T(8,128)(2,1)S(1)}, bf16[1,144,512]{2,1,0:T(8,128)(2,1)S(1)}, u32[]{:S(2)}, u32[]{:S(2)}) collective-permute-start(bf16[1,144,512]{2,1,0:T(8,128)(2,1)S(1)} %fusion.16), channel_id=1, source_target_pairs={{0,8},{2,10},{4,12},{6,14},{8,0},{10,2},{12,4},{14,6},{16,24},{18,... | collective-permute-start | bytes 442376 | tf_op jit(solution)/shard_map/ppermute | solution.py:906
  179.8 10.7 %collective-permute-start.23 = (bf16[1,160,512]{2,1,0:T(8,128)(2,1)S(1)}, bf16[1,160,512]{2,1,0:T(8,128)(2,1)S(1)}, u32[]{:S(2)}, u32[]{:S(2)}) collective-permute-start(bf16[1,160,512]{2,1,0:T(8,128)(2,1)S(1)} %add_convert_fusion.2), channel_id=1, source_target_pairs={{0,8},{2,10},{4,12},{6,14},{8,0},{10,2},{12,4},{14,6},{16,24},{18,... | collective-permute-start | bytes 491528 | tf_op jit(solution)/shard_map/ppermute | solution.py:906
  182.3 6.1 %collective-permute-start.24 = (bf16[1,144,512]{2,1,0:T(8,128)(2,1)S(1)}, bf16[1,144,512]{2,1,0:T(8,128)(2,1)S(1)}, u32[]{:S(2)}, u32[]{:S(2)}) collective-permute-start(bf16[1,144,512]{2,1,0:T(8,128)(2,1)S(1)} %get-tuple-element.165), channel_id=1, source_target_pairs={{0,4},{2,6},{4,0},{6,2},{8,12},{10,14},{12,8},{14,10},{16,20},{18,... | collective-permute-start | bytes 442376 | tf_op jit(solution)/shard_map/ppermute | solution.py:906
  184.3 10.4 %collective-permute-start.22 = (bf16[1,112,512]{2,1,0:T(8,128)(2,1)S(1)}, bf16[1,112,512]{2,1,0:T(8,128)(2,1)S(1)}, u32[]{:S(2)}, u32[]{:S(2)}) collective-permute-start(bf16[1,112,512]{2,1,0:T(8,128)(2,1)S(1)} %fusion.11), channel_id=1, source_target_pairs={{0,8},{2,10},{4,12},{6,14},{8,0},{10,2},{12,4},{14,6},{16,24},{18,... | collective-permute-start | bytes 344072 | tf_op jit(solution)/shard_map/ppermute | solution.py:906
  185.6 9.2 %collective-permute-start.21 = (bf16[1,144,512]{2,1,0:T(8,128)(2,1)S(1)}, bf16[1,144,512]{2,1,0:T(8,128)(2,1)S(1)}, u32[]{:S(2)}, u32[]{:S(2)}) collective-permute-start(bf16[1,144,512]{2,1,0:T(8,128)(2,1)S(1)} %fusion.8), channel_id=1, source_target_pairs={{0,16},{2,18},{4,20},{6,22},{8,24},{10,26},{12,28},{14,30},{16,0},... | collective-permute-start | bytes 442376 | tf_op jit(solution)/shard_map/ppermute | solution.py:906
  188.4 14.8 %collective-permute-start.28 = (bf16[2,144,512]{2,1,0:T(8,128)(2,1)S(1)}, bf16[2,144,512]{2,1,0:T(8,128)(2,1)S(1)}, u32[]{:S(2)}, u32[]{:S(2)}) collective-permute-start(bf16[2,144,512]{2,1,0:T(8,128)(2,1)S(1)} %pad_maximum_fusion.4), channel_id=1, source_target_pairs={{0,8},{2,10},{4,12},{6,14},{8,0},{10,2},{12,4},{14,6},{16,24},{18,... | collective-permute-start | bytes 884744 | tf_op jit(solution)/shard_map/ppermute | solution.py:906
  190.5 12.8 %collective-permute-start.27 = (bf16[2,160,512]{2,1,0:T(8,128)(2,1)S(1)}, bf16[2,160,512]{2,1,0:T(8,128)(2,1)S(1)}, u32[]{:S(2)}, u32[]{:S(2)}) collective-permute-start(bf16[2,160,512]{2,1,0:T(8,128)(2,1)S(1)} %pad_maximum_fusion.3), channel_id=1, source_target_pairs={{0,4},{2,6},{4,0},{6,2},{8,12},{10,14},{12,8},{14,10},{16,20},{18,... | collective-permute-start | bytes 983048 | tf_op jit(solution)/shard_map/ppermute | solution.py:906
  194.8 9.2 %collective-permute-start.26 = (bf16[1,112,512]{2,1,0:T(8,128)(2,1)S(1)}, bf16[1,112,512]{2,1,0:T(8,128)(2,1)S(1)}, u32[]{:S(2)}, u32[]{:S(2)}) collective-permute-start(bf16[1,112,512]{2,1,0:T(8,128)(2,1)S(1)} %fusion.15), channel_id=1, source_target_pairs={{0,16},{2,18},{4,20},{6,22},{8,24},{10,26},{12,28},{14,30},{16,0},... | collective-permute-start | bytes 344072 | tf_op jit(solution)/shard_map/ppermute | solution.py:906
  195.0 9.1 %collective-permute-start.25 = (bf16[1,144,512]{2,1,0:T(8,128)(2,1)S(1)}, bf16[1,144,512]{2,1,0:T(8,128)(2,1)S(1)}, u32[]{:S(2)}, u32[]{:S(2)}) collective-permute-start(bf16[1,144,512]{2,1,0:T(8,128)(2,1)S(1)} %add_convert_fusion.3), channel_id=1, source_target_pairs={{0,4},{2,6},{4,0},{6,2},{8,12},{10,14},{12,8},{14,10},{16,20},{18,... | collective-permute-start | bytes 442376 | tf_op jit(solution)/shard_map/ppermute | solution.py:906
  203.2 4.9 %collective-permute-start.32 = (bf16[4,144,512]{2,1,0:T(8,128)(2,1)S(1)}, bf16[4,144,512]{2,1,0:T(8,128)(2,1)S(1)}, u32[]{:S(2)}, u32[]{:S(2)}) collective-permute-start(bf16[4,144,512]{2,1,0:T(8,128)(2,1)S(1)} %pad_maximum_fusion.2.up_near), channel_id=1, source_target_pairs={{0,2},{2,0},{4,6},{6,4},{8,10},{10,8},{12,14},{14,12},{16,18},{18,... | collective-permute-start | bytes 1769480 | tf_op jit(solution)/shard_map/ppermute | solution.py:906
  203.4 4.7 %collective-permute-start.31 = (bf16[4,160,512]{2,1,0:T(8,128)(2,1)S(1)}, bf16[4,160,512]{2,1,0:T(8,128)(2,1)S(1)}, u32[]{:S(2)}, u32[]{:S(2)}) collective-permute-start(bf16[4,160,512]{2,1,0:T(8,128)(2,1)S(1)} %pad_maximum_fusion.dn_near), channel_id=1, source_target_pairs={{0,2},{2,0},{4,6},{6,4},{8,10},{10,8},{12,14},{14,12},{16,18},{18,... | collective-permute-start | bytes 1966088 | tf_op jit(solution)/shard_map/ppermute | solution.py:906
  204.1 2.7 %collective-permute-start.29 = (bf16[2,144,512]{2,1,0:T(8,128)(2,1)S(1)}, bf16[2,144,512]{2,1,0:T(8,128)(2,1)S(1)}, u32[]{:S(2)}, u32[]{:S(2)}) collective-permute-start(bf16[2,144,512]{2,1,0:T(8,128)(2,1)S(1)} %pad_maximum_fusion.5.refs_0_), channel_id=1, source_target_pairs={{0,2},{2,0},{4,6},{6,4},{8,10},{10,8},{12,14},{14,12},{16,18},{18,... | collective-permute-start | bytes 884744 | tf_op jit(solution)/shard_map/ppermute | solution.py:906
  204.8 2.0 collective-permute-start.30

commit v3 on v2

--- a/solution.py
+++ b/solution.py
@@ -417,7 +417,7 @@
         pl.BlockSpec((1, 1, part, SEQ_LEN), lambda s, k, pos: (shard, s, at(k, pos), 0)),
         pl.BlockSpec((1, 1, heads, SEQ_LEN, SEQ_LEN), lambda s, k, pos: (shard, s, at(k, pos), 0, 0)),
     ] + [pl.BlockSpec((1, 1, heads * HEAD_DIM, SEQ_LEN), lambda s, k, pos: (shard, s, at(k, pos), 0))] * 2
-    q_block = 512
+    q_block = 1024
     share = 2 * n_seq * heads
     flops = share * (2 * SEQ_LEN * width * PART_ROWS + 4 * SEQ_LEN * SEQ_LEN * HEAD_DIM * 6)
     return pl.pallas_call(
@@ -805,8 +805,7 @@
     total = grad_one_ref[...]
     for t in range(n_others + 1):
         weight = own_ref if t == 0 else got_ref.at[t - 1]
-        for head, ref in enumerate(grads):
-            total = total + mm_tn(ref[t, 0], weight[head * PART_ROWS : (head + 1) * PART_ROWS, :])
+        total = total + mm_tn(jnp.concatenate([ref[t, 0] for ref in grads], axis=0), weight[...])
     out_ref[...] = total.astype(bf16)
 
 

time: 211 us -> 209 us (level)
  Pallas kernels: 153 us -> 150 us
  transfers between devices with their start and end apart: 33 -> 33, of which waited for: 9 -> 11; matrix products, arithmetic and copies ran while one was open for 2% -> 2% of each run, Pallas kernels for 49% -> 48%
where the time goes in v3:
time: 209 us; the launch traced here: 208 us
  Pallas kernels  150 us (72%)
  starting transfers between devices  29.3 us (14%)
  waiting for transfers between devices  22.1 us (11%)
  local copies, waits for them, and re-layouts  4.01 us (2%)
  other arithmetic  2.16 us (1%)
    pallas_call x4, Pallas kernels, attn_bwd(): pl.pallas_call(partial(attn_bwd_kernel, head=head, cut=cut, extra=extra,...  54.6 us
    pallas_call x1, Pallas kernels, middle(): pl.pallas_call(partial(middle_kernel, n_others=n_others, chunk=min(1024,...  43.8 us
    pallas_call x2, Pallas kernels, attn_fwd(): pl.pallas_call(partial(attn_fwd_kernel, heads=heads, q_block=q_block, fet...  37.8 us
    ppermute x27, starting transfers between devices, swap_dp(): return lax.ppermute(value, 'dp', [(i, i ^ bits) for i in range(n_dp)])  22 us
    ppermute x27, waiting for transfers between devices, swap_dp(): return lax.ppermute(value, 'dp', [(i, i ^ bits) for i in range(n_dp)])  21.5 us
    ppermute x6, starting transfers between devices, shift_tensor(): lax.ppermute(value, 'tensor', [((i + by) % n_tensor, i) for i in range(n_...  7.32 us
    pallas_call x1, Pallas kernels, input_gradient(): pl.pallas_call(partial(input_grad_kernel, n_others=n_shards - 1), grid_sp...  7.23 us
  transfers between devices with their start and end apart: 33, of which 11 were waited for; matrix products, arithmetic and copies ran while one was open for 2% of the time, Pallas kernels for 48%

profile of v3, /device:TPU:0, one launch (start us, length us, event | category | flops | bytes accessed | tf_op | source)
XLA Modules:
  0.0 208.5 jit_solution(6371263515372500753)
XLA Ops:
  0.7 2.7 %pack.1 = (bf16[400,512]{1,0:T(8,128)(2,1)}, bf16[32,512]{1,0:T(8,128)(2,1)}, bf16[1168,512]{1,0:T(8,128)(2,1)}, f32[16,512]{1,0:T(8,128)}) custom-call(s32[1]{0:T(128)} %bitcast.pos_ref, bf16[768,512]{1,0:T(8,128)(2,1)} %own_ref.1, bf16[256]{0:T(256)(128)(2,1)} %query_b_ref.1, bf16[256]{0:T(256)(128)(2,1)} %value_b_ref.1, bf16[256,512]{1,0:T(8,128)(2,1)} %proj_own.1, ...), custom_call_target="tpu_custom_call" | custom-call | bytes 4194304 | tf_op jit(solution)/shard_map/pack/pallas_call | solution.py:336
  3.3 2.9 %collective-permute-start = (bf16[400,512]{1,0:T(8,128)(2,1)}, bf16[400,512]{1,0:T(8,128)(2,1)S(1)}, u32[]{:S(2)}, u32[]{:S(2)}) collective-permute-start(bf16[400,512]{1,0:T(8,128)(2,1)} %get-tuple-element.89), channel_id=1, source_target_pairs={{1,0},{0,1},{3,2},{2,3},{5,4},{4,5},{7,6},{6,7},{9,8},{8,9},{11,10... | collective-permute-start | bytes 1228808 | tf_op jit(solution)/shard_map/ppermute | solution.py:909
  6.4 19.0 %attn_fwd.2 = (bf16[2,2,768,1024]{3,2,1,0:T(8,128)(2,1)}, bf16[2,2,4,1024,1024]{4,3,2,1,0:T(8,128)(2,1)}, bf16[2,2,256,1024]{3,2,1,0:T(8,128)(2,1)}, f32[2,2,256,1024]{3,2,1,0:T(8,128)}) custom-call(s32[1]{0:T(128)} %bitcast.pos_ref, bf16[2048,512]{1,0:T(8,128)(2,1)} %x_ref.8, bf16[768,512]{1,0:T(8,128)(2,1)} %own_ref.1, ...), custom_call_target="tpu_custom_call" | custom-call | flops 14495514624 | bytes 25165824 | tf_op jit(solution)/shard_map/attn_fwd/pallas_call | solution.py:423
  25.4 1.7 collective-permute-done.1.refs_1_
  27.2 0.8 copy-done.4
  27.9 18.9 %attn_fwd.3 = (bf16[2,2,768,1024]{3,2,1,0:T(8,128)(2,1)}, bf16[2,2,4,1024,1024]{4,3,2,1,0:T(8,128)(2,1)}, bf16[2,2,256,1024]{3,2,1,0:T(8,128)(2,1)}, f32[2,2,256,1024]{3,2,1,0:T(8,128)}) custom-call(s32[1]{0:T(128)} %bitcast.pos_ref, bf16[2048,512]{1,0:T(8,128)(2,1)} %x_ref.8, ...), custom_call_target="tpu_custom_call", output_to_operand_aliasing={{0}: (4, {}), {1}: (5, {}), {2}: (6, {}), {3}: (7, {})} | custom-call | flops 1811939328 | bytes 25165824 | tf_op jit(solution)/shard_map/attn_fwd/pallas_call | solution.py:423
  46.8 0.2 collective-permute-start.3
  47.0 3.1 %collective-permute-done.3.refs_1_ = bf16[1168,512]{1,0:T(8,128)(2,1)} collective-permute-done((bf16[1168,512]{1,0:T(8,128)(2,1)}, bf16[1168,512]{1,0:T(8,128)(2,1)}, u32[]{:S(2)}, u32[]{:S(2)}) %collective-permute-start.3) | collective-permute-done | bytes 1196064 | tf_op jit(solution)/shard_map/ppermute | solution.py:905
  50.1 43.8 %middle.1 = (bf16[2048,512]{1,0:T(8,128)(2,1)}, f32[2048,512]{1,0:T(8,128)}, bf16[2,2,256,1024]{3,2,1,0:T(8,128)(2,1)}, bf16[2,4,160,512]{3,2,1,0:T(8,128)(2,1)}...) custom-call(s32[1]{0:T(128)} %bitcast.pos_ref, ...), custom_call_target="tpu_custom_call" | custom-call | flops 32212254720 | bytes 31457280 | tf_op jit(solution)/shard_map/middle/pallas_call | solution.py:635
  93.9 0.2 collective-permute-start.6
  94.1 0.4 collective-permute-start.4
  94.5 1.6 copy-done
  96.1 12.9 %attn_bwd.4 = (bf16[2,2,192,1024]{3,2,1,0:T(8,128)(2,1)S(1)}, bf16[2,2,144,512]{3,2,1,0:T(8,128)(2,1)S(1)}, bf16[2,2,144,512]{3,2,1,0:T(8,128)(2,1)S(1)}, f32[2,16,192]{2,1,0:T(8,128)S(1)}) custom-call(s32[1]{0:T(128)} %bitcast.pos_ref, bf16[2048,512]{1,0:T(8,128)(2,1)S(1)} %copy-done, bf16[2,2,768,1024]{3,2,1,0:T(8,128)(2,1)} %get-tuple-element.107.packed_ref, ...), custom_call_target="tpu_custom_call" | custom-call | flops 8589934592 | bytes 10485760 | tf_op jit(solution)/shard_map/attn_bwd/pallas_call | solution.py:755
  109.0 0.4 convert_add_fusion.1
  109.5 2.1 %collective-permute-start.7 = (bf16[2,2,144,512]{3,2,1,0:T(8,128)(2,1)S(1)}, bf16[2,2,144,512]{3,2,1,0:T(8,128)(2,1)S(1)}, u32[]{:S(2)}, u32[]{:S(2)}) collective-permute-start(bf16[2,2,144,512]{3,2,1,0:T(8,128)(2,1)S(1)} %pad_maximum_fusion.1), channel_id=1, source_target_pairs={{0,8},{2,10},{4,12},{6,14},{8,0},{10,2},{12,4},{14,6},{16,24},{18,... | collective-permute-start | bytes 1769480 | tf_op jit(solution)/shard_map/ppermute | solution.py:905
  111.7 0.2 fusion
  111.8 1.5 collective-permute-start.5
  113.4 13.8 %attn_bwd.5 = (bf16[2,2,192,1024]{3,2,1,0:T(8,128)(2,1)S(1)}, bf16[2,2,144,512]{3,2,1,0:T(8,128)(2,1)S(1)}, bf16[2,2,144,512]{3,2,1,0:T(8,128)(2,1)S(1)}, f32[2,16,192]{2,1,0:T(8,128)S(1)}) custom-call(s32[1]{0:T(128)} %bitcast.pos_ref, bf16[2048,512]{1,0:T(8,128)(2,1)S(1)} %copy-done, ...), custom_call_target="tpu_custom_call", output_to_operand_aliasing={{1}: (7, {}), {2}: (8, {})} | custom-call | flops 8589934592 | bytes 10485760 | tf_op jit(solution)/shard_map/attn_bwd/pallas_call | solution.py:755
  127.1 0.1 fusion.6
  127.2 0.6 collective-permute-start.9
  127.8 0.6 collective-permute-done.5
  128.4 0.3 bitcast_add_fusion
  128.7 1.6 collective-permute-start.8
  130.3 13.7 %attn_bwd.6 = (bf16[2,2,192,1024]{3,2,1,0:T(8,128)(2,1)S(1)}, bf16[2,2,144,512]{3,2,1,0:T(8,128)(2,1)S(1)}, bf16[2,2,144,512]{3,2,1,0:T(8,128)(2,1)S(1)}, f32[2,16,192]{2,1,0:T(8,128)S(1)}) custom-call(s32[1]{0:T(128)} %bitcast.pos_ref, bf16[2048,512]{1,0:T(8,128)(2,1)S(1)} %copy-done, ...), custom_call_target="tpu_custom_call", output_to_operand_aliasing={{1}: (7, {}), {2}: (8, {})} | custom-call | flops 8589934592 | bytes 10485760 | tf_op jit(solution)/shard_map/attn_bwd/pallas_call | solution.py:755
  144.1 0.1 fusion.2
  144.3 0.6 collective-permute-start.13
  144.8 0.1 slice_add_fusion
  144.9 0.2 copy-done.6
  145.2 1.4 collective-permute-start.12
  146.6 0.1 fusion.5
  146.7 1.6 collective-permute-start.11
  148.3 14.2 %attn_bwd.7 = (bf16[2,2,192,1024]{3,2,1,0:T(8,128)(2,1)S(1)}, bf16[2,1,112,512]{3,2,1,0:T(8,128)(2,1)S(1)}, bf16[2,1,112,512]{3,2,1,0:T(8,128)(2,1)S(1)}, f32[2,16,192]{2,1,0:T(8,128)}) custom-call(s32[1]{0:T(128)} %bitcast.pos_ref, bf16[2048,512]{1,0:T(8,128)(2,1)S(1)} %copy-done, bf16[2,2,768,1024]{3,2,1,0:T(8,128)(2,1)} %get-tuple-element.107.packed_ref, ...), custom_call_target="tpu_custom_call" | custom-call | flops 8589934592 | bytes 10485760 | tf_op jit(solution)/shard_map/attn_bwd/pallas_call | solution.py:755
  162.6 2.6 %collective-permute-start.20 = (bf16[1,160,512]{2,1,0:T(8,128)(2,1)S(1)}, bf16[1,160,512]{2,1,0:T(8,128)(2,1)S(1)}, u32[]{:S(2)}, u32[]{:S(2)}) collective-permute-start(bf16[1,160,512]{2,1,0:T(8,128)(2,1)S(1)} %fusion.7), channel_id=1, source_target_pairs={{0,16},{2,18},{4,20},{6,22},{8,24},{10,26},{12,28},{14,30},{16,0},... | collective-permute-start | bytes 491528 | tf_op jit(solution)/shard_map/ppermute | solution.py:905
  165.3 0.3 collective-permute-start.19
  165.7 0.6 collective-permute-start.16
  166.2 0.1 bitcast_add_fusion.1
  166.4 1.4 collective-permute-start.15
  167.8 7.2 %input_gradient.1 = bf16[2048,512]{1,0:T(8,128)(2,1)} custom-call(s32[1]{0:T(128)} %bitcast.pos_ref, f32[2048,512]{1,0:T(8,128)} %get-tuple-element.138.grad_one_ref, bf16[768,512]{1,0:T(8,128)(2,1)S(1)} %copy-done.1, bf16[400,512]{1,0:T(8,128)(2,1)S(1)} %copy-done.3, bf16[400,512]{1,0:T(8,128)(2,1)S(1)} %copy-done.5, ...), custom_call_target="tpu_custom_call" | custom-call | flops 4294967296 | bytes 12582912 | tf_op jit(solution)/shard_map/input_gradient/pallas_call | solution.py:823
  175.1 0.8 collective-permute-start.18
  175.9 0.9 collective-permute-start.17
  176.8 0.4 collective-permute-done.20
  177.2 0.9 collective-permute-start.23
  178.1 2.0 collective-permute-done.19
  180.2 1.4 collective-permute-start.24
  181.5 0.6 fusion.20
  182.3 1.0 collective-permute-done.17
  183.3 2.3 %collective-permute-start.21 = (bf16[1,144,512]{2,1,0:T(8,128)(2,1)S(1)}, bf16[1,144,512]{2,1,0:T(8,128)(2,1)S(1)}, u32[]{:S(2)}, u32[]{:S(2)}) collective-permute-start(bf16[1,144,512]{2,1,0:T(8,128)(2,1)S(1)} %fusion.8), channel_id=1, source_target_pairs={{0,16},{2,18},{4,20},{6,22},{8,24},{10,26},{12,28},{14,30},{16,0},... | collective-permute-start | bytes 442376 | tf_op jit(solution)/shard_map/ppermute | solution.py:905
  185.7 0.1 collective-permute-done.24
  185.8 1.1 collective-permute-start.28
  186.9 1.2 collective-permute-start.27
  188.2 3.4 %collective-permute-done.22 = bf16[1,112,512]{2,1,0:T(8,128)(2,1)S(1)} collective-permute-done((bf16[1,112,512]{2,1,0:T(8,128)(2,1)S(1)}, bf16[1,112,512]{2,1,0:T(8,128)(2,1)S(1)}, u32[]{:S(2)}, u32[]{:S(2)}) %collective-permute-start.22) | collective-permute-done | bytes 114720 | tf_op jit(solution)/shard_map/ppermute | solution.py:905
  191.6 0.1 fusion.15
  191.7 1.5 collective-permute-done.21
  193.3 1.0 collective-permute-start.25
  194.3 6.8 %collective-permute-done.28 = bf16[2,144,512]{2,1,0:T(8,128)(2,1)S(1)} collective-permute-done((bf16[2,144,512]{2,1,0:T(8,128)(2,1)S(1)}, bf16[2,144,512]{2,1,0:T(8,128)(2,1)S(1)}, u32[]{:S(2)}, u32[]{:S(2)}) %collective-permute-start.28) | collective-permute-done | bytes 294944 | tf_op jit(solution)/shard_map/ppermute | solution.py:905
  201.1 0.1 collective-permute-start.32
  201.3 0.5 collective-permute-start.31
  201.9 0.1 fusion.18
  202.0 0.1 collective-permute-start.29
  202.1 0.6 copy.38
  202.7 0.5 collective-permute-start.30
  203.2 1.6 collective-permute-done.30.refs_3_
  204.7 1.3 qkv_place.1
  206.0 2.5 %mlp_place.1 = (f32[256,512]{1,0:T(8,128)}, f32[512,1024]{1,0:T(8,128)}, f32[1024,512]{1,0:T(8,128)}) custom-call(s32[1]{0:T(128)} %bitcast.pos_ref, bf16[4,160,512]{2,1,0:T(8,128)(2,1)S(1)} %pad_maximum_fusion.dn_near, bf16[4,160,512]{2,1,0:T(8,128)(2,1)S(1)} %collective-permute-done.31.dn_far, bf16[4,144,512]{2,1,0:T(8,128)(2,1)S(1)} %pad_maximum_fusion.2.up_near, ...), custom_call_target="tpu_custom_call" | custom-call | bytes 14680064 | tf_op jit(solution)/shard_map/mlp_place/pallas_call | solution.py:858
  (70 shorter events, 1.4 us)
Async XLA Ops:
  3.3 22.0 %collective-permute-start = (bf16[400,512]{1,0:T(8,128)(2,1)}, bf16[400,512]{1,0:T(8,128)(2,1)S(1)}, u32[]{:S(2)}, u32[]{:S(2)}) collective-permute-start(bf16[400,512]{1,0:T(8,128)(2,1)} %get-tuple-element.89), channel_id=1, source_target_pairs={{1,0},{0,1},{3,2},{2,3},{5,4},{4,5},{7,6},{6,7},{9,8},{8,9},{11,10... | collective-permute-start | bytes 1228808 | tf_op jit(solution)/shard_map/ppermute | solution.py:909
  6.3 40.5 %collective-permute-start.2 = (bf16[1168,512]{1,0:T(8,128)(2,1)}, bf16[1168,512]{1,0:T(8,128)(2,1)}, u32[]{:S(2)}, u32[]{:S(2)}) collective-permute-start(bf16[1168,512]{1,0:T(8,128)(2,1)} %get-tuple-element.90), channel_id=1, source_target_pairs={{1,0},{0,1},{3,2},{2,3},{5,4},{4,5},{7,6},{6,7},{9,8},{8,9},{11,10... | collective-permute-start | bytes 3588104 | tf_op jit(solution)/shard_map/ppermute | solution.py:909
  25.3 1.8 copy-start.2
  25.3 1.8 collective-permute-start.1
  27.2 0.8 copy-start.4
  46.8 3.3 %collective-permute-start.3 = (bf16[1168,512]{1,0:T(8,128)(2,1)}, bf16[1168,512]{1,0:T(8,128)(2,1)}, u32[]{:S(2)}, u32[]{:S(2)}) collective-permute-start(bf16[1168,512]{1,0:T(8,128)(2,1)} %collective-permute-done.2.refs_0_), channel_id=1, source_target_pairs={{0,2},{2,0},{4,6},{6,4},{8,10},{10,8},{12,14},{14,12},{16,18},{18,... | collective-permute-start | bytes 3588104 | tf_op jit(solution)/shard_map/ppermute | solution.py:905
  93.9 15.1 %collective-permute-start.6 = (bf16[2,4,144,512]{3,2,1,0:T(8,128)(2,1)}, bf16[2,4,144,512]{3,2,1,0:T(8,128)(2,1)S(1)}, u32[]{:S(2)}, u32[]{:S(2)}) collective-permute-start(bf16[2,4,144,512]{3,2,1,0:T(8,128)(2,1)} %get-tuple-element.105), channel_id=1, source_target_pairs={{0,2},{2,0},{4,6},{6,4},{8,10},{10,8},{12,14},{14,12},{16,18},{18,... | collective-permute-start | bytes 3538952 | tf_op jit(solution)/shard_map/ppermute | solution.py:905
  94.1 17.5 %collective-permute-start.4 = (bf16[2,4,160,512]{3,2,1,0:T(8,128)(2,1)}, bf16[2,4,160,512]{3,2,1,0:T(8,128)(2,1)S(1)}, u32[]{:S(2)}, u32[]{:S(2)}) collective-permute-start(bf16[2,4,160,512]{3,2,1,0:T(8,128)(2,1)} %get-tuple-element.104), channel_id=1, source_target_pairs={{0,2},{2,0},{4,6},{6,4},{8,10},{10,8},{12,14},{14,12},{16,18},{18,... | collective-permute-start | bytes 3932168 | tf_op jit(solution)/shard_map/ppermute | solution.py:905
  94.5 1.6 copy-start
  96.1 12.9 %copy-start.9 = (bf16[2,4,144,512]{3,2,1,0:T(8,128)(2,1)S(1)}, bf16[2,4,144,512]{3,2,1,0:T(8,128)(2,1)}, u32[]{:S(2)}) copy-start(bf16[2,4,144,512]{3,2,1,0:T(8,128)(2,1)} %get-tuple-element.113) | copy-start | bytes 3538948
  109.4 2.3 %copy-start.8 = (bf16[2,4,160,512]{3,2,1,0:T(8,128)(2,1)S(1)}, bf16[2,4,160,512]{3,2,1,0:T(8,128)(2,1)}, u32[]{:S(2)}) copy-start(bf16[2,4,160,512]{3,2,1,0:T(8,128)(2,1)} %get-tuple-element.103) | copy-start | bytes 3932164
  109.5 17.6 %collective-permute-start.7 = (bf16[2,2,144,512]{3,2,1,0:T(8,128)(2,1)S(1)}, bf16[2,2,144,512]{3,2,1,0:T(8,128)(2,1)S(1)}, u32[]{:S(2)}, u32[]{:S(2)}) collective-permute-start(bf16[2,2,144,512]{3,2,1,0:T(8,128)(2,1)S(1)} %pad_maximum_fusion.1), channel_id=1, source_target_pairs={{0,8},{2,10},{4,12},{6,14},{8,0},{10,2},{12,4},{14,6},{16,24},{18,... | collective-permute-start | bytes 1769480 | tf_op jit(solution)/shard_map/ppermute | solution.py:905
  111.8 16.6 %collective-permute-start.5 = (bf16[4,160,512]{2,1,0:T(8,128)(2,1)S(1)}, bf16[4,160,512]{2,1,0:T(8,128)(2,1)S(1)}, u32[]{:S(2)}, u32[]{:S(2)}) collective-permute-start(bf16[4,160,512]{2,1,0:T(8,128)(2,1)S(1)} %fusion), channel_id=1, source_target_pairs={{1,0},{0,1},{3,2},{2,3},{5,4},{4,5},{7,6},{6,7},{9,8},{8,9},{11,10... | collective-permute-start | bytes 1966088 | tf_op jit(solution)/shard_map/ppermute | solution.py:909
  127.2 16.9 %collective-permute-start.9 = (bf16[2,144,512]{2,1,0:T(8,128)(2,1)S(1)}, bf16[2,144,512]{2,1,0:T(8,128)(2,1)S(1)}, u32[]{:S(2)}, u32[]{:S(2)}) collective-permute-start(bf16[2,144,512]{2,1,0:T(8,128)(2,1)S(1)} %fusion.6), channel_id=1, source_target_pairs={{1,0},{0,1},{3,2},{2,3},{5,4},{4,5},{7,6},{6,7},{9,8},{8,9},{11,10... | collective-permute-start | bytes 884744 | tf_op jit(solution)/shard_map/ppermute | solution.py:909
  128.7 16.1 %collective-permute-start.8 = (bf16[1,2,160,512]{3,2,1,0:T(8,128)(2,1)S(1)}, bf16[1,2,160,512]{3,2,1,0:T(8,128)(2,1)S(1)}, u32[]{:S(2)}, u32[]{:S(2)}) collective-permute-start(bf16[1,2,160,512]{3,2,1,0:T(8,128)(2,1)S(1)} %fusion.4), channel_id=1, source_target_pairs={{0,4},{2,6},{4,0},{6,2},{8,12},{10,14},{12,8},{14,10},{16,20},{18,... | collective-permute-start | bytes 983048 | tf_op jit(solution)/shard_map/ppermute | solution.py:905
  144.0 1.1 copy-start.6
  144.0 2.6 %collective-permute-start.10 = (bf16[2,2,144,512]{3,2,1,0:T(8,128)(2,1)S(1)}, bf16[2,2,144,512]{3,2,1,0:T(8,128)(2,1)S(1)}, u32[]{:S(2)}, u32[]{:S(2)}) collective-permute-start(bf16[2,2,144,512]{3,2,1,0:T(8,128)(2,1)S(1)} %get-tuple-element.124), channel_id=1, source_target_pairs={{0,2},{2,0},{4,6},{6,4},{8,10},{10,8},{12,14},{14,12},{16,18},{18,... | collective-permute-start | bytes 1769480 | tf_op jit(solution)/shard_map/ppermute | solution.py:905
  144.3 18.2 %collective-permute-start.13 = (bf16[1,1,144,512]{3,2,1,0:T(8,128)(2,1)S(1)}, bf16[1,1,144,512]{3,2,1,0:T(8,128)(2,1)S(1)}, u32[]{:S(2)}, u32[]{:S(2)}) collective-permute-start(bf16[1,1,144,512]{3,2,1,0:T(8,128)(2,1)S(1)} %fusion.12), channel_id=1, source_target_pairs={{0,4},{2,6},{4,0},{6,2},{8,12},{10,14},{12,8},{14,10},{16,20},{18,... | collective-permute-start | bytes 442376 | tf_op jit(solution)/shard_map/ppermute | solution.py:905
  145.2 17.3 %collective-permute-start.12 = (bf16[1,1,160,512]{3,2,1,0:T(8,128)(2,1)S(1)}, bf16[1,1,160,512]{3,2,1,0:T(8,128)(2,1)S(1)}, u32[]{:S(2)}, u32[]{:S(2)}) collective-permute-start(bf16[1,1,160,512]{3,2,1,0:T(8,128)(2,1)S(1)} %fusion.10), channel_id=1, source_target_pairs={{0,8},{2,10},{4,12},{6,14},{8,0},{10,2},{12,4},{14,6},{16,24},{18,... | collective-permute-start | bytes 491528 | tf_op jit(solution)/shard_map/ppermute | solution.py:905
  146.7 19.6 %collective-permute-start.11 = (bf16[2,144,512]{2,1,0:T(8,128)(2,1)S(1)}, bf16[2,144,512]{2,1,0:T(8,128)(2,1)S(1)}, u32[]{:S(2)}, u32[]{:S(2)}) collective-permute-start(bf16[2,144,512]{2,1,0:T(8,128)(2,1)S(1)} %fusion.5), channel_id=1, source_target_pairs={{1,0},{0,1},{3,2},{2,3},{5,4},{4,5},{7,6},{6,7},{9,8},{8,9},{11,10... | collective-permute-start | bytes 884744 | tf_op jit(solution)/shard_map/ppermute | solution.py:909
  162.5 3.9 %copy-start.7 = (bf16[2,2,192,1024]{3,2,1,0:T(8,128)(2,1)}, bf16[2,2,192,1024]{3,2,1,0:T(8,128)(2,1)S(1)}, u32[]{:S(2)}) copy-start(bf16[2,2,192,1024]{3,2,1,0:T(8,128)(2,1)S(1)} %get-tuple-element.142.refs_5_) | copy-start | bytes 4718596
  162.5 3.1 %collective-permute-start.14 = (bf16[2,1,112,512]{3,2,1,0:T(8,128)(2,1)S(1)}, bf16[2,1,112,512]{3,2,1,0:T(8,128)(2,1)S(1)}, u32[]{:S(2)}, u32[]{:S(2)}) collective-permute-start(bf16[2,1,112,512]{3,2,1,0:T(8,128)(2,1)S(1)} %get-tuple-element.131), channel_id=1, source_target_pairs={{0,2},{2,0},{4,6},{6,4},{8,10},{10,8},{12,14},{14,12},{16,18},{18,... | collective-permute-start | bytes 688136 | tf_op jit(solution)/shard_map/ppermute | solution.py:905
  162.6 5.2 %copy-start.1 = (bf16[768,512]{1,0:T(8,128)(2,1)S(1)}, bf16[768,512]{1,0:T(8,128)(2,1)}, u32[]{:S(2)}) copy-start(bf16[768,512]{1,0:T(8,128)(2,1)} %own_ref.1) | copy-start | bytes 2359300
  162.6 5.2 %copy-start.3 = (bf16[400,512]{1,0:T(8,128)(2,1)S(1)}, bf16[400,512]{1,0:T(8,128)(2,1)}, u32[]{:S(2)}) copy-start(bf16[400,512]{1,0:T(8,128)(2,1)} %copy-done.2) | copy-start | bytes 1228804
  162.6 5.2 %copy-start.5 = (bf16[400,512]{1,0:T(8,128)(2,1)S(1)}, bf16[400,512]{1,0:T(8,128)(2,1)}, u32[]{:S(2)}) copy-start(bf16[400,512]{1,0:T(8,128)(2,1)} %copy-done.4) | copy-start | bytes 1228804
  162.6 14.5 %collective-permute-start.20 = (bf16[1,160,512]{2,1,0:T(8,128)(2,1)S(1)}, bf16[1,160,512]{2,1,0:T(8,128)(2,1)S(1)}, u32[]{:S(2)}, u32[]{:S(2)}) collective-permute-start(bf16[1,160,512]{2,1,0:T(8,128)(2,1)S(1)} %fusion.7), channel_id=1, source_target_pairs={{0,16},{2,18},{4,20},{6,22},{8,24},{10,26},{12,28},{14,30},{16,0},... | collective-permute-start | bytes 491528 | tf_op jit(solution)/shard_map/ppermute | solution.py:905
  165.3 14.8 %collective-permute-start.19 = (bf16[1,144,512]{2,1,0:T(8,128)(2,1)S(1)}, bf16[1,144,512]{2,1,0:T(8,128)(2,1)S(1)}, u32[]{:S(2)}, u32[]{:S(2)}) collective-permute-start(bf16[1,144,512]{2,1,0:T(8,128)(2,1)S(1)} %fusion.9), channel_id=1, source_target_pairs={{0,16},{2,18},{4,20},{6,22},{8,24},{10,26},{12,28},{14,30},{16,0},... | collective-permute-start | bytes 442376 | tf_op jit(solution)/shard_map/ppermute | solution.py:905
  165.7 9.4 %collective-permute-start.16 = (bf16[1,112,512]{2,1,0:T(8,128)(2,1)S(1)}, bf16[1,112,512]{2,1,0:T(8,128)(2,1)S(1)}, u32[]{:S(2)}, u32[]{:S(2)}) collective-permute-start(bf16[1,112,512]{2,1,0:T(8,128)(2,1)S(1)} %fusion.14), channel_id=1, source_target_pairs={{1,0},{0,1},{3,2},{2,3},{5,4},{4,5},{7,6},{6,7},{9,8},{8,9},{11,10... | collective-permute-start | bytes 344072 | tf_op jit(solution)/shard_map/ppermute | solution.py:909
  166.4 9.4 %collective-permute-start.15 = (bf16[1,1,144,512]{3,2,1,0:T(8,128)(2,1)S(1)}, bf16[1,1,144,512]{3,2,1,0:T(8,128)(2,1)S(1)}, u32[]{:S(2)}, u32[]{:S(2)}) collective-permute-start(bf16[1,1,144,512]{3,2,1,0:T(8,128)(2,1)S(1)} %fusion.13), channel_id=1, source_target_pairs={{0,4},{2,6},{4,0},{6,2},{8,12},{10,14},{12,8},{14,10},{16,20},{18,... | collective-permute-start | bytes 442376 | tf_op jit(solution)/shard_map/ppermute | solution.py:905
  175.1 7.1 %collective-permute-start.18 = (bf16[1,112,512]{2,1,0:T(8,128)(2,1)S(1)}, bf16[1,112,512]{2,1,0:T(8,128)(2,1)S(1)}, u32[]{:S(2)}, u32[]{:S(2)}) collective-permute-start(bf16[1,112,512]{2,1,0:T(8,128)(2,1)S(1)} %fusion.17), channel_id=1, source_target_pairs={{0,4},{2,6},{4,0},{6,2},{8,12},{10,14},{12,8},{14,10},{16,20},{18,... | collective-permute-start | bytes 344072 | tf_op jit(solution)/shard_map/ppermute | solution.py:905
  175.9 7.4 %collective-permute-start.17 = (bf16[1,144,512]{2,1,0:T(8,128)(2,1)S(1)}, bf16[1,144,512]{2,1,0:T(8,128)(2,1)S(1)}, u32[]{:S(2)}, u32[]{:S(2)}) collective-permute-start(bf16[1,144,512]{2,1,0:T(8,128)(2,1)S(1)} %fusion.16), channel_id=1, source_target_pairs={{0,8},{2,10},{4,12},{6,14},{8,0},{10,2},{12,4},{14,6},{16,24},{18,... | collective-permute-start | bytes 442376 | tf_op jit(solution)/shard_map/ppermute | solution.py:905
  177.2 9.7 %collective-permute-start.23 = (bf16[1,160,512]{2,1,0:T(8,128)(2,1)S(1)}, bf16[1,160,512]{2,1,0:T(8,128)(2,1)S(1)}, u32[]{:S(2)}, u32[]{:S(2)}) collective-permute-start(bf16[1,160,512]{2,1,0:T(8,128)(2,1)S(1)} %add_convert_fusion.2), channel_id=1, source_target_pairs={{0,8},{2,10},{4,12},{6,14},{8,0},{10,2},{12,4},{14,6},{16,24},{18,... | collective-permute-start | bytes 491528 | tf_op jit(solution)/shard_map/ppermute | solution.py:905
  180.2 5.6 %collective-permute-start.24 = (bf16[1,144,512]{2,1,0:T(8,128)(2,1)S(1)}, bf16[1,144,512]{2,1,0:T(8,128)(2,1)S(1)}, u32[]{:S(2)}, u32[]{:S(2)}) collective-permute-start(bf16[1,144,512]{2,1,0:T(8,128)(2,1)S(1)} %get-tuple-element.165), channel_id=1, source_target_pairs={{0,4},{2,6},{4,0},{6,2},{8,12},{10,14},{12,8},{14,10},{16,20},{18,... | collective-permute-start | bytes 442376 | tf_op jit(solution)/shard_map/ppermute | solution.py:905
  182.2 9.4 %collective-permute-start.22 = (bf16[1,112,512]{2,1,0:T(8,128)(2,1)S(1)}, bf16[1,112,512]{2,1,0:T(8,128)(2,1)S(1)}, u32[]{:S(2)}, u32[]{:S(2)}) collective-permute-start(bf16[1,112,512]{2,1,0:T(8,128)(2,1)S(1)} %fusion.11), channel_id=1, source_target_pairs={{0,8},{2,10},{4,12},{6,14},{8,0},{10,2},{12,4},{14,6},{16,24},{18,... | collective-permute-start | bytes 344072 | tf_op jit(solution)/shard_map/ppermute | solution.py:905
  183.3 9.9 %collective-permute-start.21 = (bf16[1,144,512]{2,1,0:T(8,128)(2,1)S(1)}, bf16[1,144,512]{2,1,0:T(8,128)(2,1)S(1)}, u32[]{:S(2)}, u32[]{:S(2)}) collective-permute-start(bf16[1,144,512]{2,1,0:T(8,128)(2,1)S(1)} %fusion.8), channel_id=1, source_target_pairs={{0,16},{2,18},{4,20},{6,22},{8,24},{10,26},{12,28},{14,30},{16,0},... | collective-permute-start | bytes 442376 | tf_op jit(solution)/shard_map/ppermute | solution.py:905
  185.8 15.3 %collective-permute-start.28 = (bf16[2,144,512]{2,1,0:T(8,128)(2,1)S(1)}, bf16[2,144,512]{2,1,0:T(8,128)(2,1)S(1)}, u32[]{:S(2)}, u32[]{:S(2)}) collective-permute-start(bf16[2,144,512]{2,1,0:T(8,128)(2,1)S(1)} %pad_maximum_fusion.4), channel_id=1, source_target_pairs={{0,8},{2,10},{4,12},{6,14},{8,0},{10,2},{12,4},{14,6},{16,24},{18,... | collective-permute-start | bytes 884744 | tf_op jit(solution)/shard_map/ppermute | solution.py:905
  186.9 14.3 %collective-permute-start.27 = (bf16[2,160,512]{2,1,0:T(8,128)(2,1)S(1)}, bf16[2,160,512]{2,1,0:T(8,128)(2,1)S(1)}, u32[]{:S(2)}, u32[]{:S(2)}) collective-permute-start(bf16[2,160,512]{2,1,0:T(8,128)(2,1)S(1)} %pad_maximum_fusion.3), channel_id=1, source_target_pairs={{0,4},{2,6},{4,0},{6,2},{8,12},{10,14},{12,8},{14,10},{16,20},{18,... | collective-permute-start | bytes 983048 | tf_op jit(solution)/shard_map/ppermute | solution.py:905
  191.7 10.2 %collective-permute-start.26 = (bf16[1,112,512]{2,1,0:T(8,128)(2,1)S(1)}, bf16[1,112,512]{2,1,0:T(8,128)(2,1)S(1)}, u32[]{:S(2)}, u32[]{:S(2)}) collective-permute-start(bf16[1,112,512]{2,1,0:T(8,128)(2,1)S(1)} %fusion.15), channel_id=1, source_target_pairs={{0,16},{2,18},{4,20},{6,22},{8,24},{10,26},{12,28},{14,30},{16,0},... | collective-permute-start | bytes 344072 | tf_op jit(solution)/shard_map/ppermute | solution.py:905
  193.3 8.7 %collective-permute-start.25 = (bf16[1,144,512]{2,1,0:T(8,128)(2,1)S(1)}, bf16[1,144,512]{2,1,0:T(8,128)(2,1)S(1)}, u32[]{:S(2)}, u32[]{:S(2)}) collective-permute-start(bf16[1,144,512]{2,1,0:T(8,128)(2,1)S(1)} %add_convert_fusion.3), channel_id=1, source_target_pairs={{0,4},{2,6},{4,0},{6,2},{8,12},{10,14},{12,8},{14,10},{16,20},{18,... | collective-permute-start | bytes 442376 | tf_op jit(solution)/shard_map/ppermute | solution.py:905
  201.1 4.9 %collective-permute-start.32 = (bf16[4,144,512]{2,1,0:T(8,128)(2,1)S(1)}, bf16[4,144,512]{2,1,0:T(8,128)(2,1)S(1)}, u32[]{:S(2)}, u32[]{:S(2)}) collective-permute-start(bf16[4,144,512]{2,1,0:T(8,128)(2,1)S(1)} %pad_maximum_fusion.2.up_near), channel_id=1, source_target_pairs={{0,2},{2,0},{4,6},{6,4},{8,10},{10,8},{12,14},{14,12},{16,18},{18,... | collective-permute-start | bytes 1769480 | tf_op jit(solution)/shard_map/ppermute | solution.py:905
  201.3 4.7 %collective-permute-start.31 = (bf16[4,160,512]{2,1,0:T(8,128)(2,1)S(1)}, bf16[4,160,512]{2,1,0:T(8,128)(2,1)S(1)}, u32[]{:S(2)}, u32[]{:S(2)}) collective-permute-start(bf16[4,160,512]{2,1,0:T(8,128)(2,1)S(1)} %pad_maximum_fusion.dn_near), channel_id=1, source_target_pairs={{0,2},{2,0},{4,6},{6,4},{8,10},{10,8},{12,14},{14,12},{16,18},{18,... | collective-permute-start | bytes 1966088 | tf_op jit(solution)/shard_map/ppermute | solution.py:905
  202.0 2.7 %collective-permute-start.29 = (bf16[2,144,512]{2,1,0:T(8,128)(2,1)S(1)}, bf16[2,144,512]{2,1,0:T(8,128)(2,1)S(1)}, u32[]{:S(2)}, u32[]{:S(2)}) collective-permute-start(bf16[2,144,512]{2,1,0:T(8,128)(2,1)S(1)} %pad_maximum_fusion.5.refs_0_), channel_id=1, source_target_pairs={{0,2},{2,0},{4,6},{6,4},{8,10},{10,8},{12,14},{14,12},{16,18},{18,... | collective-permute-start | bytes 884744 | tf_op jit(solution)/shard_map/ppermute | solution.py:905
  202.7 2.0 collective-permute-start.30

commit v4 on v3

--- a/solution.py
+++ b/solution.py
@@ -591,25 +591,28 @@
         low = lax.rem(pos_ref[0], MLP_SLOTS)
         dn_rows, up_rows, proj_rows = hidden // MLP_SLOTS, width // MLP_SLOTS, ctx_rows // MLP_SLOTS
         half = MLP_SLOTS // 2
-        for slot in range(MLP_SLOTS):
-            dn_ref = dn_keep_ref if slot < half else dn_send_ref
-            upk_ref = up_keep_ref if slot < half else up_send_ref
-            k = slot % half
-            dn_at = lax.bitwise_xor(low, DOWN_BITS[slot])
-            rows = aligned(lax.bitwise_xor(low, UP_BITS[slot]), up_rows, up_rows)
-            for t in range(n_shards):
-                dn_ref[t, k, :dn_rows] = dn_acc[t, aligned(dn_at, dn_rows, dn_rows), :].astype(bf16)
-                dn_ref[t, k, dn_rows:] = proj_acc[t, aligned(dn_at, proj_rows, proj_rows), :].astype(bf16)
-                for j in range(blocks):
-                    to = j * up_rows
-                    upk_ref[t, k, to : to + up_rows] = up_acc[t, rows, j * width : (j + 1) * width].astype(bf16)
-                to = blocks * up_rows
-                upk_ref[t, k, to : to + 8] = vec_acc[...].astype(bf16)
-                tail = [
-                    up_b_acc[:, t * hidden + j * width : t * hidden + (j + 1) * width] for j in range(blocks)
-                ]
-                tail.append(jnp.zeros((8 - blocks, width), f32))
-                upk_ref[t, k, to + 8 : to + EXTRA] = jnp.concatenate(tail, axis=0).astype(bf16)
+        tails = []
+        for t in range(n_shards):
+            rest = [up_b_acc[:, t * hidden + j * width : t * hidden + (j + 1) * width] for j in range(blocks)]
+            tails.append(jnp.concatenate([vec_acc[...], *rest, jnp.zeros((8 - blocks, width), f32)], axis=0).astype(bf16))
+
+        for side, (dn_ref, upk_ref) in enumerate(((dn_keep_ref, up_keep_ref), (dn_send_ref, up_send_ref))):
+
+            def emit(k, carry, side=side, dn_ref=dn_ref, upk_ref=upk_ref):
+                first, second = lax.shift_right_logical(k, 1), lax.bitwise_and(k, 1)
+                dn_at = lax.bitwise_xor(low, side + 2 * first + 4 * second)
+                up_at = lax.bitwise_xor(low, side + 4 * first + 2 * second)
+                rows = aligned(up_at, up_rows, up_rows)
+                for t in range(n_shards):
+                    dn_ref[t, k, :dn_rows] = dn_acc[t, aligned(dn_at, dn_rows, dn_rows), :].astype(bf16)
+                    dn_ref[t, k, dn_rows:] = proj_acc[t, aligned(dn_at, proj_rows, proj_rows), :].astype(bf16)
+                    for j in range(blocks):
+                        to = j * up_rows
+                        upk_ref[t, k, to : to + up_rows] = up_acc[t, rows, j * width : (j + 1) * width].astype(bf16)
+                    upk_ref[t, k, blocks * up_rows :] = tails[t]
+                return carry
+
+            lax.fori_loop(0, half, emit, 0)
 
 
 def middle(pos, x, out_grad, ctx, vecs, proj, up, down, fetched):
@@ -1104,7 +1107,7 @@
     ("qb", "qa", "dn", "up", "qb"),
     ("qb", "qa", "dn", "up", "qb", "qa", "up", "dn", "qb", "qa", "up", "dn", "qb", "qa"),
 )
-UNROLLED = (0,)
+UNROLLED = (0, 1)
 
 
 def solution(mesh):

time: 209 us -> 209 us (level)
  transfers between devices with their start and end apart: 33 -> 33, of which waited for: 11 -> 10; matrix products, arithmetic and copies ran while one was open for 2% -> 2% of each run, Pallas kernels for 48% -> 48%
where the time goes in v4:
time: 209 us
  Pallas kernels  149 us (71%)
  starting transfers between devices  30.1 us (14%)
  waiting for transfers between devices  22.7 us (11%)
  local copies, waits for them, and re-layouts  4.02 us (2%)
  other arithmetic  2.16 us (1%)
    pallas_call x4, Pallas kernels, attn_bwd(): pl.pallas_call(partial(attn_bwd_kernel, head=head, cut=cut, extra=extra,...  53.7 us
    pallas_call x1, Pallas kernels, middle(): pl.pallas_call(partial(middle_kernel, n_others=n_others, chunk=min(1024,...  43.8 us
    pallas_call x2, Pallas kernels, attn_fwd(): pl.pallas_call(partial(attn_fwd_kernel, heads=heads, q_block=q_block, fet...  37.8 us
    ppermute x27, starting transfers between devices, swap_dp(): return lax.ppermute(value, 'dp', [(i, i ^ bits) for i in range(n_dp)])  22.6 us
    ppermute x27, waiting for transfers between devices, swap_dp(): return lax.ppermute(value, 'dp', [(i, i ^ bits) for i in range(n_dp)])  21.4 us
    ppermute x6, starting transfers between devices, shift_tensor(): lax.ppermute(value, 'tensor', [((i + by) % n_tensor, i) for i in range(n_...  7.55 us
    pallas_call x1, Pallas kernels, input_gradient(): pl.pallas_call(partial(input_grad_kernel, n_others=n_shards - 1), grid_sp...  7.23 us
  transfers between devices with their start and end apart: 33, of which 10 were waited for; matrix products, arithmetic and copies ran while one was open for 2% of the time, Pallas kernels for 48%

profile of v4, /device:TPU:0, one launch (start us, length us, event | category | flops | bytes accessed | tf_op | source)
XLA Modules:
  0.0 209.1 jit_solution(1499835205785411200)
XLA Ops:
  0.7 2.7 %pack.1 = (bf16[400,512]{1,0:T(8,128)(2,1)}, bf16[32,512]{1,0:T(8,128)(2,1)}, bf16[1168,512]{1,0:T(8,128)(2,1)}, f32[16,512]{1,0:T(8,128)}) custom-call(s32[1]{0:T(128)} %bitcast.pos_ref, bf16[768,512]{1,0:T(8,128)(2,1)} %own_ref.1, bf16[256]{0:T(256)(128)(2,1)} %query_b_ref.1, bf16[256]{0:T(256)(128)(2,1)} %value_b_ref.1, bf16[256,512]{1,0:T(8,128)(2,1)} %proj_own.1, ...), custom_call_target="tpu_custom_call" | custom-call | bytes 4194304 | tf_op jit(solution)/shard_map/pack/pallas_call | solution.py:336
  3.3 2.9 %collective-permute-start = (bf16[400,512]{1,0:T(8,128)(2,1)}, bf16[400,512]{1,0:T(8,128)(2,1)S(1)}, u32[]{:S(2)}, u32[]{:S(2)}) collective-permute-start(bf16[400,512]{1,0:T(8,128)(2,1)} %get-tuple-element.89), channel_id=1, source_target_pairs={{1,0},{0,1},{3,2},{2,3},{5,4},{4,5},{7,6},{6,7},{9,8},{8,9},{11,10... | collective-permute-start | bytes 1228808 | tf_op jit(solution)/shard_map/ppermute | solution.py:912
  6.4 19.0 %attn_fwd.2 = (bf16[2,2,768,1024]{3,2,1,0:T(8,128)(2,1)}, bf16[2,2,4,1024,1024]{4,3,2,1,0:T(8,128)(2,1)}, bf16[2,2,256,1024]{3,2,1,0:T(8,128)(2,1)}, f32[2,2,256,1024]{3,2,1,0:T(8,128)}) custom-call(s32[1]{0:T(128)} %bitcast.pos_ref, bf16[2048,512]{1,0:T(8,128)(2,1)} %x_ref.8, bf16[768,512]{1,0:T(8,128)(2,1)} %own_ref.1, ...), custom_call_target="tpu_custom_call" | custom-call | flops 14495514624 | bytes 25165824 | tf_op jit(solution)/shard_map/attn_fwd/pallas_call | solution.py:423
  25.4 1.7 collective-permute-done.1.refs_1_
  27.2 0.8 copy-done.4
  27.9 18.9 %attn_fwd.3 = (bf16[2,2,768,1024]{3,2,1,0:T(8,128)(2,1)}, bf16[2,2,4,1024,1024]{4,3,2,1,0:T(8,128)(2,1)}, bf16[2,2,256,1024]{3,2,1,0:T(8,128)(2,1)}, f32[2,2,256,1024]{3,2,1,0:T(8,128)}) custom-call(s32[1]{0:T(128)} %bitcast.pos_ref, bf16[2048,512]{1,0:T(8,128)(2,1)} %x_ref.8, ...), custom_call_target="tpu_custom_call", output_to_operand_aliasing={{0}: (4, {}), {1}: (5, {}), {2}: (6, {}), {3}: (7, {})} | custom-call | flops 1811939328 | bytes 25165824 | tf_op jit(solution)/shard_map/attn_fwd/pallas_call | solution.py:423
  46.8 0.2 collective-permute-start.3
  47.0 3.1 %collective-permute-done.3.refs_1_ = bf16[1168,512]{1,0:T(8,128)(2,1)} collective-permute-done((bf16[1168,512]{1,0:T(8,128)(2,1)}, bf16[1168,512]{1,0:T(8,128)(2,1)}, u32[]{:S(2)}, u32[]{:S(2)}) %collective-permute-start.3) | collective-permute-done | bytes 1196064 | tf_op jit(solution)/shard_map/ppermute | solution.py:908
  50.1 43.8 %middle.1 = (bf16[2048,512]{1,0:T(8,128)(2,1)}, f32[2048,512]{1,0:T(8,128)}, bf16[2,2,256,1024]{3,2,1,0:T(8,128)(2,1)}, bf16[2,4,160,512]{3,2,1,0:T(8,128)(2,1)}...) custom-call(s32[1]{0:T(128)} %bitcast.pos_ref, ...), custom_call_target="tpu_custom_call" | custom-call | flops 32212254720 | bytes 31457280 | tf_op jit(solution)/shard_map/middle/pallas_call | solution.py:638
  93.9 0.2 collective-permute-start.6
  94.1 0.4 collective-permute-start.4
  94.5 1.6 copy-done
  96.1 12.9 %attn_bwd.4 = (bf16[2,2,192,1024]{3,2,1,0:T(8,128)(2,1)S(1)}, bf16[2,2,144,512]{3,2,1,0:T(8,128)(2,1)S(1)}, bf16[2,2,144,512]{3,2,1,0:T(8,128)(2,1)S(1)}, f32[2,16,192]{2,1,0:T(8,128)S(1)}) custom-call(s32[1]{0:T(128)} %bitcast.pos_ref, bf16[2048,512]{1,0:T(8,128)(2,1)S(1)} %copy-done, bf16[2,2,768,1024]{3,2,1,0:T(8,128)(2,1)} %get-tuple-element.107.packed_ref, ...), custom_call_target="tpu_custom_call" | custom-call | flops 8589934592 | bytes 10485760 | tf_op jit(solution)/shard_map/attn_bwd/pallas_call | solution.py:758
  109.0 0.4 convert_add_fusion.1
  109.6 2.1 %collective-permute-start.7 = (bf16[2,2,144,512]{3,2,1,0:T(8,128)(2,1)S(1)}, bf16[2,2,144,512]{3,2,1,0:T(8,128)(2,1)S(1)}, u32[]{:S(2)}, u32[]{:S(2)}) collective-permute-start(bf16[2,2,144,512]{3,2,1,0:T(8,128)(2,1)S(1)} %pad_maximum_fusion.1), channel_id=1, source_target_pairs={{0,8},{2,10},{4,12},{6,14},{8,0},{10,2},{12,4},{14,6},{16,24},{18,... | collective-permute-start | bytes 1769480 | tf_op jit(solution)/shard_map/ppermute | solution.py:908
  111.7 0.2 fusion
  111.8 1.5 collective-permute-start.5
  113.4 12.9 %attn_bwd.5 = (bf16[2,2,192,1024]{3,2,1,0:T(8,128)(2,1)S(1)}, bf16[2,2,144,512]{3,2,1,0:T(8,128)(2,1)S(1)}, bf16[2,2,144,512]{3,2,1,0:T(8,128)(2,1)S(1)}, f32[2,16,192]{2,1,0:T(8,128)S(1)}) custom-call(s32[1]{0:T(128)} %bitcast.pos_ref, bf16[2048,512]{1,0:T(8,128)(2,1)S(1)} %copy-done, ...), custom_call_target="tpu_custom_call", output_to_operand_aliasing={{1}: (7, {}), {2}: (8, {})} | custom-call | flops 8589934592 | bytes 10485760 | tf_op jit(solution)/shard_map/attn_bwd/pallas_call | solution.py:758
  126.3 0.1 fusion.6
  126.4 0.7 collective-permute-start.9
  127.1 1.3 collective-permute-done.5
  128.4 0.3 bitcast_add_fusion
  128.7 1.6 collective-permute-start.8
  130.3 13.7 %attn_bwd.6 = (bf16[2,2,192,1024]{3,2,1,0:T(8,128)(2,1)S(1)}, bf16[2,2,144,512]{3,2,1,0:T(8,128)(2,1)S(1)}, bf16[2,2,144,512]{3,2,1,0:T(8,128)(2,1)S(1)}, f32[2,16,192]{2,1,0:T(8,128)S(1)}) custom-call(s32[1]{0:T(128)} %bitcast.pos_ref, bf16[2048,512]{1,0:T(8,128)(2,1)S(1)} %copy-done, ...), custom_call_target="tpu_custom_call", output_to_operand_aliasing={{1}: (7, {}), {2}: (8, {})} | custom-call | flops 8589934592 | bytes 10485760 | tf_op jit(solution)/shard_map/attn_bwd/pallas_call | solution.py:758
  144.1 0.1 fusion.2
  144.3 0.6 collective-permute-start.13
  144.9 0.1 slice_add_fusion
  145.0 0.2 copy-done.6
  145.2 1.4 collective-permute-start.12
  146.6 0.1 fusion.5
  146.7 2.2 %collective-permute-start.11 = (bf16[2,144,512]{2,1,0:T(8,128)(2,1)S(1)}, bf16[2,144,512]{2,1,0:T(8,128)(2,1)S(1)}, u32[]{:S(2)}, u32[]{:S(2)}) collective-permute-start(bf16[2,144,512]{2,1,0:T(8,128)(2,1)S(1)} %fusion.5), channel_id=1, source_target_pairs={{1,0},{0,1},{3,2},{2,3},{5,4},{4,5},{7,6},{6,7},{9,8},{8,9},{11,10... | collective-permute-start | bytes 884744 | tf_op jit(solution)/shard_map/ppermute | solution.py:912
  148.9 14.2 %attn_bwd.7 = (bf16[2,2,192,1024]{3,2,1,0:T(8,128)(2,1)S(1)}, bf16[2,1,112,512]{3,2,1,0:T(8,128)(2,1)S(1)}, bf16[2,1,112,512]{3,2,1,0:T(8,128)(2,1)S(1)}, f32[2,16,192]{2,1,0:T(8,128)}) custom-call(s32[1]{0:T(128)} %bitcast.pos_ref, bf16[2048,512]{1,0:T(8,128)(2,1)S(1)} %copy-done, bf16[2,2,768,1024]{3,2,1,0:T(8,128)(2,1)} %get-tuple-element.107.packed_ref, ...), custom_call_target="tpu_custom_call" | custom-call | flops 8589934592 | bytes 10485760 | tf_op jit(solution)/shard_map/attn_bwd/pallas_call | solution.py:758
  163.2 2.6 %collective-permute-start.20 = (bf16[1,160,512]{2,1,0:T(8,128)(2,1)S(1)}, bf16[1,160,512]{2,1,0:T(8,128)(2,1)S(1)}, u32[]{:S(2)}, u32[]{:S(2)}) collective-permute-start(bf16[1,160,512]{2,1,0:T(8,128)(2,1)S(1)} %fusion.7), channel_id=1, source_target_pairs={{0,16},{2,18},{4,20},{6,22},{8,24},{10,26},{12,28},{14,30},{16,0},... | collective-permute-start | bytes 491528 | tf_op jit(solution)/shard_map/ppermute | solution.py:908
  165.9 0.3 collective-permute-start.19
  166.3 0.1 collective-permute-start.16
  166.4 0.1 bitcast_add_fusion.1
  166.5 1.4 collective-permute-start.15
  167.9 7.2 %input_gradient.1 = bf16[2048,512]{1,0:T(8,128)(2,1)} custom-call(s32[1]{0:T(128)} %bitcast.pos_ref, f32[2048,512]{1,0:T(8,128)} %get-tuple-element.138.grad_one_ref, bf16[768,512]{1,0:T(8,128)(2,1)S(1)} %copy-done.1, bf16[400,512]{1,0:T(8,128)(2,1)S(1)} %copy-done.3, bf16[400,512]{1,0:T(8,128)(2,1)S(1)} %copy-done.5, ...), custom_call_target="tpu_custom_call" | custom-call | flops 4294967296 | bytes 12582912 | tf_op jit(solution)/shard_map/input_gradient/pallas_call | solution.py:826
  175.2 0.8 collective-permute-start.18
  176.0 1.0 collective-permute-start.17
  177.0 0.7 collective-permute-done.20
  177.8 0.4 collective-permute-start.23
  178.2 2.5 %collective-permute-done.19 = bf16[1,144,512]{2,1,0:T(8,128)(2,1)S(1)} collective-permute-done((bf16[1,144,512]{2,1,0:T(8,128)(2,1)S(1)}, bf16[1,144,512]{2,1,0:T(8,128)(2,1)S(1)}, u32[]{:S(2)}, u32[]{:S(2)}) %collective-permute-start.19) | collective-permute-done | bytes 147488 | tf_op jit(solution)/shard_map/ppermute | solution.py:908
  180.8 1.4 collective-permute-start.24
  182.2 0.6 fusion.20
  182.9 1.0 collective-permute-done.17
  183.9 2.4 %collective-permute-start.21 = (bf16[1,144,512]{2,1,0:T(8,128)(2,1)S(1)}, bf16[1,144,512]{2,1,0:T(8,128)(2,1)S(1)}, u32[]{:S(2)}, u32[]{:S(2)}) collective-permute-start(bf16[1,144,512]{2,1,0:T(8,128)(2,1)S(1)} %fusion.8), channel_id=1, source_target_pairs={{0,16},{2,18},{4,20},{6,22},{8,24},{10,26},{12,28},{14,30},{16,0},... | collective-permute-start | bytes 442376 | tf_op jit(solution)/shard_map/ppermute | solution.py:908
  186.4 1.1 collective-permute-start.28
  187.6 1.3 collective-permute-start.27
  188.8 2.8 %collective-permute-done.22 = bf16[1,112,512]{2,1,0:T(8,128)(2,1)S(1)} collective-permute-done((bf16[1,112,512]{2,1,0:T(8,128)(2,1)S(1)}, bf16[1,112,512]{2,1,0:T(8,128)(2,1)S(1)}, u32[]{:S(2)}, u32[]{:S(2)}) %collective-permute-start.22) | collective-permute-done | bytes 114720 | tf_op jit(solution)/shard_map/ppermute | solution.py:908
  191.6 0.1 fusion.15
  191.7 0.6 collective-permute-start.26
  192.2 1.6 collective-permute-done.21
  193.9 1.3 collective-permute-start.25
  195.3 6.4 %collective-permute-done.28 = bf16[2,144,512]{2,1,0:T(8,128)(2,1)S(1)} collective-permute-done((bf16[2,144,512]{2,1,0:T(8,128)(2,1)S(1)}, bf16[2,144,512]{2,1,0:T(8,128)(2,1)S(1)}, u32[]{:S(2)}, u32[]{:S(2)}) %collective-permute-start.28) | collective-permute-done | bytes 294944 | tf_op jit(solution)/shard_map/ppermute | solution.py:908
  201.8 0.1 collective-permute-start.32
  201.9 0.5 collective-permute-start.31
  202.5 0.1 fusion.18
  202.6 0.1 collective-permute-start.29
  202.7 0.6 copy.38
  203.3 0.5 collective-permute-start.30
  203.8 1.6 collective-permute-done.30.refs_3_
  205.3 1.3 qkv_place.1
  206.6 2.5 %mlp_place.1 = (f32[256,512]{1,0:T(8,128)}, f32[512,1024]{1,0:T(8,128)}, f32[1024,512]{1,0:T(8,128)}) custom-call(s32[1]{0:T(128)} %bitcast.pos_ref, bf16[4,160,512]{2,1,0:T(8,128)(2,1)S(1)} %pad_maximum_fusion.dn_near, bf16[4,160,512]{2,1,0:T(8,128)(2,1)S(1)} %collective-permute-done.31.dn_far, bf16[4,144,512]{2,1,0:T(8,128)(2,1)S(1)} %pad_maximum_fusion.2.up_near, ...), custom_call_target="tpu_custom_call" | custom-call | bytes 14680064 | tf_op jit(solution)/shard_map/mlp_place/pallas_call | solution.py:861
  (70 shorter events, 1.3 us)
Async XLA Ops:
  3.3 22.0 %collective-permute-start = (bf16[400,512]{1,0:T(8,128)(2,1)}, bf16[400,512]{1,0:T(8,128)(2,1)S(1)}, u32[]{:S(2)}, u32[]{:S(2)}) collective-permute-start(bf16[400,512]{1,0:T(8,128)(2,1)} %get-tuple-element.89), channel_id=1, source_target_pairs={{1,0},{0,1},{3,2},{2,3},{5,4},{4,5},{7,6},{6,7},{9,8},{8,9},{11,10... | collective-permute-start | bytes 1228808 | tf_op jit(solution)/shard_map/ppermute | solution.py:912
  6.3 40.5 %collective-permute-start.2 = (bf16[1168,512]{1,0:T(8,128)(2,1)}, bf16[1168,512]{1,0:T(8,128)(2,1)}, u32[]{:S(2)}, u32[]{:S(2)}) collective-permute-start(bf16[1168,512]{1,0:T(8,128)(2,1)} %get-tuple-element.90), channel_id=1, source_target_pairs={{1,0},{0,1},{3,2},{2,3},{5,4},{4,5},{7,6},{6,7},{9,8},{8,9},{11,10... | collective-permute-start | bytes 3588104 | tf_op jit(solution)/shard_map/ppermute | solution.py:912
  25.3 1.8 copy-start.2
  25.3 1.8 collective-permute-start.1
  27.2 0.8 copy-start.4
  46.8 3.3 %collective-permute-start.3 = (bf16[1168,512]{1,0:T(8,128)(2,1)}, bf16[1168,512]{1,0:T(8,128)(2,1)}, u32[]{:S(2)}, u32[]{:S(2)}) collective-permute-start(bf16[1168,512]{1,0:T(8,128)(2,1)} %collective-permute-done.2.refs_0_), channel_id=1, source_target_pairs={{0,2},{2,0},{4,6},{6,4},{8,10},{10,8},{12,14},{14,12},{16,18},{18,... | collective-permute-start | bytes 3588104 | tf_op jit(solution)/shard_map/ppermute | solution.py:908
  93.9 15.1 %collective-permute-start.6 = (bf16[2,4,144,512]{3,2,1,0:T(8,128)(2,1)}, bf16[2,4,144,512]{3,2,1,0:T(8,128)(2,1)S(1)}, u32[]{:S(2)}, u32[]{:S(2)}) collective-permute-start(bf16[2,4,144,512]{3,2,1,0:T(8,128)(2,1)} %get-tuple-element.105), channel_id=1, source_target_pairs={{0,2},{2,0},{4,6},{6,4},{8,10},{10,8},{12,14},{14,12},{16,18},{18,... | collective-permute-start | bytes 3538952 | tf_op jit(solution)/shard_map/ppermute | solution.py:908
  94.1 17.5 %collective-permute-start.4 = (bf16[2,4,160,512]{3,2,1,0:T(8,128)(2,1)}, bf16[2,4,160,512]{3,2,1,0:T(8,128)(2,1)S(1)}, u32[]{:S(2)}, u32[]{:S(2)}) collective-permute-start(bf16[2,4,160,512]{3,2,1,0:T(8,128)(2,1)} %get-tuple-element.104), channel_id=1, source_target_pairs={{0,2},{2,0},{4,6},{6,4},{8,10},{10,8},{12,14},{14,12},{16,18},{18,... | collective-permute-start | bytes 3932168 | tf_op jit(solution)/shard_map/ppermute | solution.py:908
  94.5 1.6 copy-start
  96.1 12.9 %copy-start.9 = (bf16[2,4,144,512]{3,2,1,0:T(8,128)(2,1)S(1)}, bf16[2,4,144,512]{3,2,1,0:T(8,128)(2,1)}, u32[]{:S(2)}) copy-start(bf16[2,4,144,512]{3,2,1,0:T(8,128)(2,1)} %get-tuple-element.113) | copy-start | bytes 3538948
  109.4 2.3 %copy-start.8 = (bf16[2,4,160,512]{3,2,1,0:T(8,128)(2,1)S(1)}, bf16[2,4,160,512]{3,2,1,0:T(8,128)(2,1)}, u32[]{:S(2)}) copy-start(bf16[2,4,160,512]{3,2,1,0:T(8,128)(2,1)} %get-tuple-element.103) | copy-start | bytes 3932164
  109.6 16.7 %collective-permute-start.7 = (bf16[2,2,144,512]{3,2,1,0:T(8,128)(2,1)S(1)}, bf16[2,2,144,512]{3,2,1,0:T(8,128)(2,1)S(1)}, u32[]{:S(2)}, u32[]{:S(2)}) collective-permute-start(bf16[2,2,144,512]{3,2,1,0:T(8,128)(2,1)S(1)} %pad_maximum_fusion.1), channel_id=1, source_target_pairs={{0,8},{2,10},{4,12},{6,14},{8,0},{10,2},{12,4},{14,6},{16,24},{18,... | collective-permute-start | bytes 1769480 | tf_op jit(solution)/shard_map/ppermute | solution.py:908
  111.8 16.6 %collective-permute-start.5 = (bf16[4,160,512]{2,1,0:T(8,128)(2,1)S(1)}, bf16[4,160,512]{2,1,0:T(8,128)(2,1)S(1)}, u32[]{:S(2)}, u32[]{:S(2)}) collective-permute-start(bf16[4,160,512]{2,1,0:T(8,128)(2,1)S(1)} %fusion), channel_id=1, source_target_pairs={{1,0},{0,1},{3,2},{2,3},{5,4},{4,5},{7,6},{6,7},{9,8},{8,9},{11,10... | collective-permute-start | bytes 1966088 | tf_op jit(solution)/shard_map/ppermute | solution.py:912
  126.4 17.8 %collective-permute-start.9 = (bf16[2,144,512]{2,1,0:T(8,128)(2,1)S(1)}, bf16[2,144,512]{2,1,0:T(8,128)(2,1)S(1)}, u32[]{:S(2)}, u32[]{:S(2)}) collective-permute-start(bf16[2,144,512]{2,1,0:T(8,128)(2,1)S(1)} %fusion.6), channel_id=1, source_target_pairs={{1,0},{0,1},{3,2},{2,3},{5,4},{4,5},{7,6},{6,7},{9,8},{8,9},{11,10... | collective-permute-start | bytes 884744 | tf_op jit(solution)/shard_map/ppermute | solution.py:912
  128.7 16.1 %collective-permute-start.8 = (bf16[1,2,160,512]{3,2,1,0:T(8,128)(2,1)S(1)}, bf16[1,2,160,512]{3,2,1,0:T(8,128)(2,1)S(1)}, u32[]{:S(2)}, u32[]{:S(2)}) collective-permute-start(bf16[1,2,160,512]{3,2,1,0:T(8,128)(2,1)S(1)} %fusion.4), channel_id=1, source_target_pairs={{0,4},{2,6},{4,0},{6,2},{8,12},{10,14},{12,8},{14,10},{16,20},{18,... | collective-permute-start | bytes 983048 | tf_op jit(solution)/shard_map/ppermute | solution.py:908
  144.0 1.1 copy-start.6
  144.0 2.6 %collective-permute-start.10 = (bf16[2,2,144,512]{3,2,1,0:T(8,128)(2,1)S(1)}, bf16[2,2,144,512]{3,2,1,0:T(8,128)(2,1)S(1)}, u32[]{:S(2)}, u32[]{:S(2)}) collective-permute-start(bf16[2,2,144,512]{3,2,1,0:T(8,128)(2,1)S(1)} %get-tuple-element.124), channel_id=1, source_target_pairs={{0,2},{2,0},{4,6},{6,4},{8,10},{10,8},{12,14},{14,12},{16,18},{18,... | collective-permute-start | bytes 1769480 | tf_op jit(solution)/shard_map/ppermute | solution.py:908
  144.3 18.8 %collective-permute-start.13 = (bf16[1,1,144,512]{3,2,1,0:T(8,128)(2,1)S(1)}, bf16[1,1,144,512]{3,2,1,0:T(8,128)(2,1)S(1)}, u32[]{:S(2)}, u32[]{:S(2)}) collective-permute-start(bf16[1,1,144,512]{3,2,1,0:T(8,128)(2,1)S(1)} %fusion.12), channel_id=1, source_target_pairs={{0,4},{2,6},{4,0},{6,2},{8,12},{10,14},{12,8},{14,10},{16,20},{18,... | collective-permute-start | bytes 442376 | tf_op jit(solution)/shard_map/ppermute | solution.py:908
  145.2 17.9 %collective-permute-start.12 = (bf16[1,1,160,512]{3,2,1,0:T(8,128)(2,1)S(1)}, bf16[1,1,160,512]{3,2,1,0:T(8,128)(2,1)S(1)}, u32[]{:S(2)}, u32[]{:S(2)}) collective-permute-start(bf16[1,1,160,512]{3,2,1,0:T(8,128)(2,1)S(1)} %fusion.10), channel_id=1, source_target_pairs={{0,8},{2,10},{4,12},{6,14},{8,0},{10,2},{12,4},{14,6},{16,24},{18,... | collective-permute-start | bytes 491528 | tf_op jit(solution)/shard_map/ppermute | solution.py:908
  146.7 19.7 %collective-permute-start.11 = (bf16[2,144,512]{2,1,0:T(8,128)(2,1)S(1)}, bf16[2,144,512]{2,1,0:T(8,128)(2,1)S(1)}, u32[]{:S(2)}, u32[]{:S(2)}) collective-permute-start(bf16[2,144,512]{2,1,0:T(8,128)(2,1)S(1)} %fusion.5), channel_id=1, source_target_pairs={{1,0},{0,1},{3,2},{2,3},{5,4},{4,5},{7,6},{6,7},{9,8},{8,9},{11,10... | collective-permute-start | bytes 884744 | tf_op jit(solution)/shard_map/ppermute | solution.py:912
  163.1 3.4 %copy-start.7 = (bf16[2,2,192,1024]{3,2,1,0:T(8,128)(2,1)}, bf16[2,2,192,1024]{3,2,1,0:T(8,128)(2,1)S(1)}, u32[]{:S(2)}) copy-start(bf16[2,2,192,1024]{3,2,1,0:T(8,128)(2,1)S(1)} %get-tuple-element.142.refs_5_) | copy-start | bytes 4718596
  163.1 3.1 %collective-permute-start.14 = (bf16[2,1,112,512]{3,2,1,0:T(8,128)(2,1)S(1)}, bf16[2,1,112,512]{3,2,1,0:T(8,128)(2,1)S(1)}, u32[]{:S(2)}, u32[]{:S(2)}) collective-permute-start(bf16[2,1,112,512]{3,2,1,0:T(8,128)(2,1)S(1)} %get-tuple-element.131), channel_id=1, source_target_pairs={{0,2},{2,0},{4,6},{6,4},{8,10},{10,8},{12,14},{14,12},{16,18},{18,... | collective-permute-start | bytes 688136 | tf_op jit(solution)/shard_map/ppermute | solution.py:908
  163.2 4.7 %copy-start.1 = (bf16[768,512]{1,0:T(8,128)(2,1)S(1)}, bf16[768,512]{1,0:T(8,128)(2,1)}, u32[]{:S(2)}) copy-start(bf16[768,512]{1,0:T(8,128)(2,1)} %own_ref.1) | copy-start | bytes 2359300
  163.2 4.7 %copy-start.3 = (bf16[400,512]{1,0:T(8,128)(2,1)S(1)}, bf16[400,512]{1,0:T(8,128)(2,1)}, u32[]{:S(2)}) copy-start(bf16[400,512]{1,0:T(8,128)(2,1)} %copy-done.2) | copy-start | bytes 1228804
  163.2 4.7 %copy-start.5 = (bf16[400,512]{1,0:T(8,128)(2,1)S(1)}, bf16[400,512]{1,0:T(8,128)(2,1)}, u32[]{:S(2)}) copy-start(bf16[400,512]{1,0:T(8,128)(2,1)} %copy-done.4) | copy-start | bytes 1228804
  163.2 14.5 %collective-permute-start.20 = (bf16[1,160,512]{2,1,0:T(8,128)(2,1)S(1)}, bf16[1,160,512]{2,1,0:T(8,128)(2,1)S(1)}, u32[]{:S(2)}, u32[]{:S(2)}) collective-permute-start(bf16[1,160,512]{2,1,0:T(8,128)(2,1)S(1)} %fusion.7), channel_id=1, source_target_pairs={{0,16},{2,18},{4,20},{6,22},{8,24},{10,26},{12,28},{14,30},{16,0},... | collective-permute-start | bytes 491528 | tf_op jit(solution)/shard_map/ppermute | solution.py:908
  165.9 14.8 %collective-permute-start.19 = (bf16[1,144,512]{2,1,0:T(8,128)(2,1)S(1)}, bf16[1,144,512]{2,1,0:T(8,128)(2,1)S(1)}, u32[]{:S(2)}, u32[]{:S(2)}) collective-permute-start(bf16[1,144,512]{2,1,0:T(8,128)(2,1)S(1)} %fusion.9), channel_id=1, source_target_pairs={{0,16},{2,18},{4,20},{6,22},{8,24},{10,26},{12,28},{14,30},{16,0},... | collective-permute-start | bytes 442376 | tf_op jit(solution)/shard_map/ppermute | solution.py:908
  166.3 8.9 %collective-permute-start.16 = (bf16[1,112,512]{2,1,0:T(8,128)(2,1)S(1)}, bf16[1,112,512]{2,1,0:T(8,128)(2,1)S(1)}, u32[]{:S(2)}, u32[]{:S(2)}) collective-permute-start(bf16[1,112,512]{2,1,0:T(8,128)(2,1)S(1)} %fusion.14), channel_id=1, source_target_pairs={{1,0},{0,1},{3,2},{2,3},{5,4},{4,5},{7,6},{6,7},{9,8},{8,9},{11,10... | collective-permute-start | bytes 344072 | tf_op jit(solution)/shard_map/ppermute | solution.py:912
  166.5 9.4 %collective-permute-start.15 = (bf16[1,1,144,512]{3,2,1,0:T(8,128)(2,1)S(1)}, bf16[1,1,144,512]{3,2,1,0:T(8,128)(2,1)S(1)}, u32[]{:S(2)}, u32[]{:S(2)}) collective-permute-start(bf16[1,1,144,512]{3,2,1,0:T(8,128)(2,1)S(1)} %fusion.13), channel_id=1, source_target_pairs={{0,4},{2,6},{4,0},{6,2},{8,12},{10,14},{12,8},{14,10},{16,20},{18,... | collective-permute-start | bytes 442376 | tf_op jit(solution)/shard_map/ppermute | solution.py:908
  175.2 7.6 %collective-permute-start.18 = (bf16[1,112,512]{2,1,0:T(8,128)(2,1)S(1)}, bf16[1,112,512]{2,1,0:T(8,128)(2,1)S(1)}, u32[]{:S(2)}, u32[]{:S(2)}) collective-permute-start(bf16[1,112,512]{2,1,0:T(8,128)(2,1)S(1)} %fusion.17), channel_id=1, source_target_pairs={{0,4},{2,6},{4,0},{6,2},{8,12},{10,14},{12,8},{14,10},{16,20},{18,... | collective-permute-start | bytes 344072 | tf_op jit(solution)/shard_map/ppermute | solution.py:908
  176.0 7.9 %collective-permute-start.17 = (bf16[1,144,512]{2,1,0:T(8,128)(2,1)S(1)}, bf16[1,144,512]{2,1,0:T(8,128)(2,1)S(1)}, u32[]{:S(2)}, u32[]{:S(2)}) collective-permute-start(bf16[1,144,512]{2,1,0:T(8,128)(2,1)S(1)} %fusion.16), channel_id=1, source_target_pairs={{0,8},{2,10},{4,12},{6,14},{8,0},{10,2},{12,4},{14,6},{16,24},{18,... | collective-permute-start | bytes 442376 | tf_op jit(solution)/shard_map/ppermute | solution.py:908
  177.8 9.7 %collective-permute-start.23 = (bf16[1,160,512]{2,1,0:T(8,128)(2,1)S(1)}, bf16[1,160,512]{2,1,0:T(8,128)(2,1)S(1)}, u32[]{:S(2)}, u32[]{:S(2)}) collective-permute-start(bf16[1,160,512]{2,1,0:T(8,128)(2,1)S(1)} %add_convert_fusion.2), channel_id=1, source_target_pairs={{0,8},{2,10},{4,12},{6,14},{8,0},{10,2},{12,4},{14,6},{16,24},{18,... | collective-permute-start | bytes 491528 | tf_op jit(solution)/shard_map/ppermute | solution.py:908
  180.8 5.6 %collective-permute-start.24 = (bf16[1,144,512]{2,1,0:T(8,128)(2,1)S(1)}, bf16[1,144,512]{2,1,0:T(8,128)(2,1)S(1)}, u32[]{:S(2)}, u32[]{:S(2)}) collective-permute-start(bf16[1,144,512]{2,1,0:T(8,128)(2,1)S(1)} %get-tuple-element.165), channel_id=1, source_target_pairs={{0,4},{2,6},{4,0},{6,2},{8,12},{10,14},{12,8},{14,10},{16,20},{18,... | collective-permute-start | bytes 442376 | tf_op jit(solution)/shard_map/ppermute | solution.py:908
  182.8 8.8 %collective-permute-start.22 = (bf16[1,112,512]{2,1,0:T(8,128)(2,1)S(1)}, bf16[1,112,512]{2,1,0:T(8,128)(2,1)S(1)}, u32[]{:S(2)}, u32[]{:S(2)}) collective-permute-start(bf16[1,112,512]{2,1,0:T(8,128)(2,1)S(1)} %fusion.11), channel_id=1, source_target_pairs={{0,8},{2,10},{4,12},{6,14},{8,0},{10,2},{12,4},{14,6},{16,24},{18,... | collective-permute-start | bytes 344072 | tf_op jit(solution)/shard_map/ppermute | solution.py:908
  183.9 9.9 %collective-permute-start.21 = (bf16[1,144,512]{2,1,0:T(8,128)(2,1)S(1)}, bf16[1,144,512]{2,1,0:T(8,128)(2,1)S(1)}, u32[]{:S(2)}, u32[]{:S(2)}) collective-permute-start(bf16[1,144,512]{2,1,0:T(8,128)(2,1)S(1)} %fusion.8), channel_id=1, source_target_pairs={{0,16},{2,18},{4,20},{6,22},{8,24},{10,26},{12,28},{14,30},{16,0},... | collective-permute-start | bytes 442376 | tf_op jit(solution)/shard_map/ppermute | solution.py:908
  186.4 15.3 %collective-permute-start.28 = (bf16[2,144,512]{2,1,0:T(8,128)(2,1)S(1)}, bf16[2,144,512]{2,1,0:T(8,128)(2,1)S(1)}, u32[]{:S(2)}, u32[]{:S(2)}) collective-permute-start(bf16[2,144,512]{2,1,0:T(8,128)(2,1)S(1)} %pad_maximum_fusion.4), channel_id=1, source_target_pairs={{0,8},{2,10},{4,12},{6,14},{8,0},{10,2},{12,4},{14,6},{16,24},{18,... | collective-permute-start | bytes 884744 | tf_op jit(solution)/shard_map/ppermute | solution.py:908
  187.6 14.3 %collective-permute-start.27 = (bf16[2,160,512]{2,1,0:T(8,128)(2,1)S(1)}, bf16[2,160,512]{2,1,0:T(8,128)(2,1)S(1)}, u32[]{:S(2)}, u32[]{:S(2)}) collective-permute-start(bf16[2,160,512]{2,1,0:T(8,128)(2,1)S(1)} %pad_maximum_fusion.3), channel_id=1, source_target_pairs={{0,4},{2,6},{4,0},{6,2},{8,12},{10,14},{12,8},{14,10},{16,20},{18,... | collective-permute-start | bytes 983048 | tf_op jit(solution)/shard_map/ppermute | solution.py:908
  191.7 10.8 %collective-permute-start.26 = (bf16[1,112,512]{2,1,0:T(8,128)(2,1)S(1)}, bf16[1,112,512]{2,1,0:T(8,128)(2,1)S(1)}, u32[]{:S(2)}, u32[]{:S(2)}) collective-permute-start(bf16[1,112,512]{2,1,0:T(8,128)(2,1)S(1)} %fusion.15), channel_id=1, source_target_pairs={{0,16},{2,18},{4,20},{6,22},{8,24},{10,26},{12,28},{14,30},{16,0},... | collective-permute-start | bytes 344072 | tf_op jit(solution)/shard_map/ppermute | solution.py:908
  193.9 8.6 %collective-permute-start.25 = (bf16[1,144,512]{2,1,0:T(8,128)(2,1)S(1)}, bf16[1,144,512]{2,1,0:T(8,128)(2,1)S(1)}, u32[]{:S(2)}, u32[]{:S(2)}) collective-permute-start(bf16[1,144,512]{2,1,0:T(8,128)(2,1)S(1)} %add_convert_fusion.3), channel_id=1, source_target_pairs={{0,4},{2,6},{4,0},{6,2},{8,12},{10,14},{12,8},{14,10},{16,20},{18,... | collective-permute-start | bytes 442376 | tf_op jit(solution)/shard_map/ppermute | solution.py:908
  201.8 4.9 %collective-permute-start.32 = (bf16[4,144,512]{2,1,0:T(8,128)(2,1)S(1)}, bf16[4,144,512]{2,1,0:T(8,128)(2,1)S(1)}, u32[]{:S(2)}, u32[]{:S(2)}) collective-permute-start(bf16[4,144,512]{2,1,0:T(8,128)(2,1)S(1)} %pad_maximum_fusion.2.up_near), channel_id=1, source_target_pairs={{0,2},{2,0},{4,6},{6,4},{8,10},{10,8},{12,14},{14,12},{16,18},{18,... | collective-permute-start | bytes 1769480 | tf_op jit(solution)/shard_map/ppermute | solution.py:908
  201.9 4.7 %collective-permute-start.31 = (bf16[4,160,512]{2,1,0:T(8,128)(2,1)S(1)}, bf16[4,160,512]{2,1,0:T(8,128)(2,1)S(1)}, u32[]{:S(2)}, u32[]{:S(2)}) collective-permute-start(bf16[4,160,512]{2,1,0:T(8,128)(2,1)S(1)} %pad_maximum_fusion.dn_near), channel_id=1, source_target_pairs={{0,2},{2,0},{4,6},{6,4},{8,10},{10,8},{12,14},{14,12},{16,18},{18,... | collective-permute-start | bytes 1966088 | tf_op jit(solution)/shard_map/ppermute | solution.py:908
  202.6 2.7 %collective-permute-start.29 = (bf16[2,144,512]{2,1,0:T(8,128)(2,1)S(1)}, bf16[2,144,512]{2,1,0:T(8,128)(2,1)S(1)}, u32[]{:S(2)}, u32[]{:S(2)}) collective-permute-start(bf16[2,144,512]{2,1,0:T(8,128)(2,1)S(1)} %pad_maximum_fusion.5.refs_0_), channel_id=1, source_target_pairs={{0,2},{2,0},{4,6},{6,4},{8,10},{10,8},{12,14},{14,12},{16,18},{18,... | collective-permute-start | bytes 884744 | tf_op jit(solution)/shard_map/ppermute | solution.py:908
  203.3 2.0 collective-permute-start.30
